TPU v7x, 32 devices: a whole 2x2x4 slice. The times are simulated.
32 devices in a mesh: grp: 2 (over y), sp: 4 (over z), sec: 2 (over x), mb: 2 (over core).
Axes of the slice: x: 2, y: 2, z: 4, core: 2. Of those that a mesh axis runs over, the one named last changes fastest.
Arguments:
- atmosphere: bfloat16 [8, 24, 32, 256], P(('grp', 'mb'), None, 'sp', 'sec'), parts along dimension 0, may hold values from -6 to 6
- ocean_state: bfloat16 [8, 8, 32, 128], P(('grp', 'mb'), None, 'sp'), parts along dimension 0, may hold values from -6 to 6
- fluxes: bfloat16 [8, 8, 32, 128], P(('grp', 'mb'), None, 'sp'), parts along dimension 0, may hold values from -6 to 6
- sea_mask: int32 [32, 128], P('sp'), may hold values 0 or 1
- air_entry: bfloat16 [3, 3, 32, 136], replicated, may hold values from -0.375 to 0.375
- air_middle: bfloat16 [3, 3, 136, 136], replicated, may hold values from -0.15625 to 0.15625
- air_exit: bfloat16 [3, 3, 136, 32], replicated, may hold values from -0.15625 to 0.15625
- sea_entry: bfloat16 [3, 3, 16, 136], replicated, may hold values from -0.5 to 0.5
- sea_exit: bfloat16 [3, 3, 136, 8], replicated, may hold values from -0.15625 to 0.15625
Outputs:
- air_final: bfloat16 [8, 24, 32, 256], P(('grp', 'mb'), None, 'sp', 'sec'), parts along dimension 0
- sea_final: bfloat16 [8, 8, 32, 128], P(('grp', 'mb'), None, 'sp'), parts along dimension 0
There are 2 independent parts, one for each index of `grp`. A program takes and returns all parts, laid end to end along the dimension named above; an argument that names none is the same for every part. Nothing has to cross between parts.
All inputs are finite; a program needn't handle non-finite values. No bound on the sum of `sea_mask` on one device may be relied on, other than what follows from the above.
Results may differ from a plain program's by a relative error of at most 0.0055.
Values may be sent and summed in bfloat16 or wider, within the bound.
No kernel may reach another device: no remote copies, remote signals or barrier semaphores. Data moves between devices by JAX's collectives and lax.ppermute only.
A program may use at most 64 MiB of HBM per device.

v0:
```python
import jax
import jax.numpy as jnp
from jax import lax
from jax.sharding import PartitionSpec as P

STEPS = 2


dilations = (1, 2, 4)


def with_halo(block, sides, width):
    for axis, dim in sides:
        count = lax.axis_size(axis)
        forward = [(i, i + 1) for i in range(count - 1)]
        forward.append((count - 1, 0))
        backward = [(target, source) for source, target in forward]
        low = lax.ppermute(
            lax.slice_in_dim(block, block.shape[dim] - width, None, axis=dim), axis, forward
        )
        high = lax.ppermute(lax.slice_in_dim(block, 0, width, axis=dim), axis, backward)
        block = jnp.concatenate([low, block, high], axis=dim)
    return block


def spread_2(value, axis, source):
    kept = jnp.where(lax.axis_index(axis) == source, value, 0).astype(value.dtype)
    return lax.psum(kept, axis)


def tap_sum(source, weight, dilation):
    out_rows = source.shape[2] - 2 * dilation
    out_cols = source.shape[3] - 2 * dilation
    pieces = []
    for tap_row in range(3):
        for tap_col in range(3):
            sliced = lax.slice_in_dim(
                source, tap_row * dilation, tap_row * dilation + out_rows, axis=2
            )
            sliced = lax.slice_in_dim(
                sliced, tap_col * dilation, tap_col * dilation + out_cols, axis=3
            )
            pieces.append(sliced)
    stacked = jnp.concatenate(pieces, axis=1)
    flat_weight = weight.reshape(-1, weight.shape[3])
    return jnp.einsum("mkrc,ko->morc", stacked, flat_weight, preferred_element_type=jnp.float32)


def gelu_round(values):
    return jax.nn.gelu(values, approximate=True).astype(jnp.bfloat16)


def keep_columns(block, first_column, limit):
    columns = lax.iota(jnp.int32, block.shape[3]) + first_column
    inside = (columns >= 0) & (columns < limit)
    return jnp.where(inside[None, None, None, :], block, jnp.zeros_like(block))


def shards(
    atmosphere, ocean_state, fluxes, sea_mask, air_entry, air_middle, air_exit, sea_entry, sea_exit
):
    sections = lax.axis_size("sec")
    position = lax.axis_index("sec")
    is_ocean = position == sections - 1
    band_cols = atmosphere.shape[3]
    ocean_cols = ocean_state.shape[3]
    field_count = atmosphere.shape[1]
    sea_weight = sea_mask.astype(jnp.float32)
    air_weights = (air_entry, air_middle, air_exit)
    sea_weights = (sea_entry, sea_exit)

    def air_layer(extended, layer_index):
        produced = tap_sum(extended, air_weights[layer_index], dilations[layer_index])
        if layer_index < 2:
            return gelu_round(produced)
        return produced

    def air_blank(extended, layer_index):
        spread = dilations[layer_index]
        out_shape = (
            extended.shape[0],
            air_weights[layer_index].shape[3],
            extended.shape[2] - 2 * spread,
            extended.shape[3] - 2 * spread,
        )
        return jnp.zeros(out_shape, jnp.bfloat16 if layer_index < 2 else jnp.float32)

    def sea_layer(extended, layer_index):
        padded = jnp.pad(extended, ((0, 0), (0, 0), (0, 0), (1, 1)))
        produced = tap_sum(padded, sea_weights[layer_index], 1)
        if layer_index < 1:
            return gelu_round(produced)
        return produced

    def sea_blank(extended, layer_index):
        out_shape = (
            extended.shape[0],
            sea_weights[layer_index].shape[3],
            extended.shape[2] - 2,
            ocean_cols,
        )
        return jnp.zeros(out_shape, jnp.bfloat16 if layer_index < 1 else jnp.float32)

    def air_extend(current, layer_index, margin):
        extended = with_halo(current, (("sp", 2), ("sec", 3)), dilations[layer_index])
        margin = dilations[layer_index]
        limit = band_cols * sections if layer_index == 0 else ocean_cols
        extended = keep_columns(extended, position * band_cols - margin, limit)
        return (extended, margin - dilations[layer_index])

    def sea_extend(current):
        return with_halo(current, (("sp", 2),), 1)

    def run_segment(air_job, sea_job):
        air_current = None
        sea_current = None
        margin = 0
        if air_job is not None:
            air_current = jnp.concatenate(air_job, axis=1)
        if sea_job is not None:
            sea_current = jnp.concatenate(sea_job, axis=1)
        for layer_index in range(3):
            air_ready = None
            sea_ready = None
            if air_current is not None:
                air_ready, margin = air_extend(air_current, layer_index, margin)
            if sea_current is not None and layer_index < 2:
                sea_ready = sea_extend(sea_current)
            if air_ready is None and sea_ready is None:
                continue

            def on_sea(ready):
                air_given, sea_given = ready
                air_made = None if air_given is None else air_blank(air_given, layer_index)
                sea_made = None if sea_given is None else sea_layer(sea_given, layer_index)
                return (air_made, sea_made)

            def on_air(ready):
                air_given, sea_given = ready
                air_made = None if air_given is None else air_layer(air_given, layer_index)
                sea_made = None if sea_given is None else sea_blank(sea_given, layer_index)
                return (air_made, sea_made)

            air_next, sea_next = lax.cond(is_ocean, on_sea, on_air, (air_ready, sea_ready))
            if air_ready is not None:
                air_current = air_next
            if sea_ready is not None:
                sea_current = sea_next
        air_result = None
        sea_result = None
        if air_job is not None:
            previous = air_job[0]
            renewed = (previous.astype(jnp.float32) + air_current[:, :field_count]).astype(
                jnp.bfloat16
            )
            air_result = (renewed, air_current[:, field_count:].astype(jnp.bfloat16))
        if sea_job is not None:
            previous = sea_job[0]
            sea_result = (
                previous.astype(jnp.float32) + sea_weight[None, None] * sea_current
            ).astype(jnp.bfloat16)
        return (air_result, sea_result)

    air_now, sea_now, flux_now = (atmosphere, ocean_state, fluxes)
    for step_index in range(STEPS):
        sea_now = run_segment(None, (sea_now, flux_now))[1]
        shared = spread_2(sea_now, "sec", sections - 1)
        start_col = jnp.minimum(position, sections - 2) * band_cols
        own_band = lax.dynamic_slice_in_dim(shared, start_col, band_cols, 3)
        own_band = jnp.where(is_ocean, jnp.zeros_like(own_band), own_band)
        sea_now = shared
        air_now, flux_band = run_segment((air_now, own_band), None)[0]
        if step_index + 1 < STEPS:
            collected = lax.all_gather(flux_band, "sec", axis=3, tiled=True)
            flux_now = collected[:, :, :, :ocean_cols]
    return (air_now, sea_now)


def solution(mesh):
    placed = (
        P(("grp", "mb"), None, "sp", "sec"),
        P(("grp", "mb"), None, "sp", None),
        P(("grp", "mb"), None, "sp", None),
        P("sp", None),
        P(),
        P(),
        P(),
        P(),
        P(),
    )
    return jax.shard_map(
        shards,
        mesh=mesh,
        in_specs=placed,
        out_specs=(P(("grp", "mb"), None, "sp", "sec"), P(("grp", "mb"), None, "sp", None)),
        check_vma=False,
    )
```

profile of v0, /device:TPU:0, one launch (start us, length us, event | category | flops | bytes accessed | tf_op | source)
XLA Modules:
  0.0 245.5 jit_solution(14746877766434007346)
XLA Ops:
  2.2 3.1 %collective-permute-start = (bf16[2,16,1,128]{3,1,2,0:T(8,128)(2,1)S(1)}, bf16[2,16,1,128]{3,1,2,0:T(8,128)(2,1)S(1)}, u32[]{:S(2)}, u32[]{:S(2)}) collective-permute-start(bf16[2,16,1,128]{3,1,2,0:T(8,128)(2,1)S(1)} %get-tuple-element.252), channel_id=1, source_target_pairs={{0,4},{4,8},{8,12},{12,0},{1,5},{5,9},{9,13},{13,1},{2,6},{6,10},{... | collective-permute-start | bytes 24584 | tf_op jit(solution)/shard_map/ppermute | solution.py:18
  16.7 17.5 %psum.14 = bf16[2,8,8,128]{3,2,1,0:T(8,128)(2,1)S(1)} all-reduce(bf16[2,8,8,128]{3,2,1,0:T(8,128)(2,1)S(1)} %fusion.76), channel_id=1, replica_groups=mesh['grp'=2,'sp'=4,'sec'=2,'mb'=2] {'sec'}, use_global_device_ids=true, to_apply=%region_4.5 | all-reduce | flops 16384 | bytes 65536 | tf_op jit(solution)/shard_map/psum | solution.py:28
  35.3 2.8 %collective-permute-start.5 = (bf16[2,32,1,128]{3,1,2,0:T(8,128)(2,1)S(1)}, bf16[2,32,1,128]{3,1,2,0:T(8,128)(2,1)S(1)}, u32[]{:S(2)}, u32[]{:S(2)}) collective-permute-start(bf16[2,32,1,128]{3,1,2,0:T(8,128)(2,1)S(1)} %get-tuple-element.249), channel_id=1, source_target_pairs={{4,0},{8,4},{12,8},{0,12},{5,1},{9,5},{13,9},{1,13},{6,2},{10,6},{... | collective-permute-start | bytes 49160 | tf_op jit(solution)/shard_map/ppermute | solution.py:21
  42.6 2.8 %collective-permute-done.6 = bf16[2,32,10,1]{3,1,2,0:T(8,128)(2,1)S(1)} collective-permute-done((bf16[2,32,10,1]{3,1,2,0:T(8,128)(2,1)S(1)}, bf16[2,32,10,1]{3,1,2,0:T(8,128)(2,1)S(1)}, u32[]{:S(2)}, u32[]{:S(2)}) %collective-permute-start.6) | collective-permute-done | bytes 1312 | tf_op jit(solution)/shard_map/ppermute | solution.py:18
  51.4 2.8 %collective-permute-start.9 = (bf16[2,136,2,128]{1,3,2,0:T(8,128)(2,1)S(1)}, bf16[2,136,2,128]{1,3,2,0:T(8,128)(2,1)S(1)}, u32[]{:S(2)}, u32[]{:S(2)}) collective-permute-start(bf16[2,136,2,128]{1,3,2,0:T(8,128)(2,1)S(1)} %get-tuple-element.237), channel_id=1, source_target_pairs={{4,0},{8,4},{12,8},{0,12},{5,1},{9,5},{13,9},{1,13},{6,2},{10,6},{... | collective-permute-start | bytes 417800 | tf_op jit(solution)/shard_map/ppermute | solution.py:21
  54.2 4.4 %collective-permute-done.8 = bf16[2,136,2,128]{1,3,2,0:T(8,128)(2,1)S(1)} collective-permute-done((bf16[2,136,2,128]{1,3,2,0:T(8,128)(2,1)S(1)}, bf16[2,136,2,128]{1,3,2,0:T(8,128)(2,1)S(1)}, u32[]{:S(2)}, u32[]{:S(2)}) %collective-permute-start.8) | collective-permute-done | bytes 139296 | tf_op jit(solution)/shard_map/ppermute | solution.py:18
  67.8 8.1 %conditional.13 = (bf16[2,136,8,128]{3,1,2,0:T(8,128)(2,1)S(1)}) conditional(s32[]{:T(128)} %convert_element_type.68, (pred[132]{0:T(512)(128)(4,1)S(1)}, bf16[2,136,12,132]{1,3,2,0:T(8,128)(2,1)S(1)}, bf16[2,136,12,132]{3,1,2,0:T(8,128)(2,1)}, bf16[3,3,136,136]{3,2,1,0:T(8,128)(2,1)}) %tuple.76, () %tuple.77), branch_computations={%region_7.8_spmd, %region_8.9_spmd} | conditional | flops 684774144 | bytes 21570856 | solution.py:144
  81.8 9.6 %collective-permute-done.12 = bf16[2,136,4,128]{1,2,3,0:T(4,128)(2,1)S(1)} collective-permute-done((bf16[2,136,4,128]{1,2,3,0:T(4,128)(2,1)}, bf16[2,136,4,128]{1,2,3,0:T(4,128)(2,1)S(1)}, u32[]{:S(2)}, u32[]{:S(2)}) %collective-permute-start.12) | collective-permute-done | bytes 278560 | tf_op jit(solution)/shard_map/ppermute | solution.py:18
  91.3 5.3 %collective-permute-done.13 = bf16[2,136,4,128]{1,2,3,0:T(4,128)(2,1)S(1)} collective-permute-done((bf16[2,136,4,128]{1,2,3,0:T(4,128)(2,1)S(1)}, bf16[2,136,4,128]{1,2,3,0:T(4,128)(2,1)S(1)}, u32[]{:S(2)}, u32[]{:S(2)}) %collective-permute-start.13) | collective-permute-done | bytes 278560 | tf_op jit(solution)/shard_map/ppermute | solution.py:21
  101.8 2.6 %pad_maximum_fusion = bf16[2,136,16,136]{1,2,3,0:T(8,128)(2,1)} fusion(bf16[2,136,16,4]{1,2,3,0:T(8,128)(2,1)S(1)} %collective-permute-done.15, bf16[2,136,4,128]{1,2,3,0:T(4,128)(2,1)S(1)} %collective-permute-done.13, bf16[2,136,8,128]{1,2,3,0:T(8,128)(2,1)S(1)} %copy.69, bf16[2,136,4,128]{1,2,3,0:T(4,128)(2,1)S(1)} %collective-permute-done.12, ...), kind=kLoop, calls=%fused_computation.188 | loop fusion | flops 5918720 | bytes 2367488 | tf_op jit(solution)/shard_map/concatenate | solution.py:22
  105.3 14.8 %conditional.14 = (f32[2,32,8,128]{3,2,1,0:T(8,128)S(1)}, f32[2,24,8,128]{3,2,1,0:T(8,128)S(1)}) conditional(s32[]{:T(128)} %convert_element_type.68, (pred[136]{0:T(512)(128)(4,1)S(1)}, bf16[2,136,16,136]{1,2,3,0:T(8,128)(2,1)}, bf16[2,136,16,136]{3,1,2,0:T(8,128)(2,1)S(1)}, bf16[3,3,136,32]{2,3,1,0:T(8,128)(2,1)S(1)}) %tuple.159, () %tuple.79), branch_computations={%region_9.10_spmd, %region_10.11_spmd} | conditional | flops 161024000 | bytes 42584756 | solution.py:144
  105.3 4.6 %copy.72 = bf16[2,136,16,136]{3,1,2,0:T(8,128)(2,1)} copy(bf16[2,136,16,136]{1,2,3,0:T(8,128)(2,1)} %get-tuple-element.198) | data formatting | bytes 2367488 | tf_op jit(solution)/shard_map
  116.6 3.4 %convolution_bitcast_fusion.4 = f32[2,32,8,128]{3,1,2,0:T(8,128)S(1)} fusion(bf16[2,1224,8,128]{3,1,2,0:T(8,128)(2,1)} %copy-done.2, bf16[1224,32,1,1]{0,1,2,3:T(8,128)(2,1)S(1)} %reshape.60), kind=kOutput, calls=%fused_computation.83 | convolution fusion | flops 160432128 | bytes 5353984 | tf_op jit(solution)/shard_map/cond/branch_0_fun/mkrc,ko->morc/dot_general | solution.py:46
  120.1 4.6 %all_gather.3 = bf16[2,8,8,256]{3,2,1,0:T(8,128)(2,1)S(1)} all-gather(bf16[2,8,8,128]{3,2,1,0:T(8,128)(2,1)S(1)} %slice.832), channel_id=1, replica_groups=mesh['grp'=2,'sp'=4,'sec'=2,'mb'=2] {'sec'}, dimensions={3}, use_global_device_ids=true | all-gather | bytes 98304 | tf_op jit(solution)/shard_map/all_gather | solution.py:174
  125.1 3.5 %collective-permute-start.17 = (bf16[2,16,1,128]{3,2,1,0:T(2,128)(2,1)S(1)}, bf16[2,16,1,128]{3,2,1,0:T(2,128)(2,1)S(1)}, u32[]{:S(2)}, u32[]{:S(2)}) collective-permute-start(bf16[2,16,1,128]{3,2,1,0:T(2,128)(2,1)S(1)} %get-tuple-element.251), channel_id=1, source_target_pairs={{4,0},{8,4},{12,8},{0,12},{5,1},{9,5},{13,9},{1,13},{6,2},{10,6},{... | collective-permute-start | bytes 24584 | tf_op jit(solution)/shard_map/ppermute | solution.py:21
  132.4 4.0 %collective-permute-start.19 = (bf16[2,136,1,128]{3,1,2,0:T(8,128)(2,1)S(1)}, bf16[2,136,1,128]{3,1,2,0:T(8,128)(2,1)S(1)}, u32[]{:S(2)}, u32[]{:S(2)}) collective-permute-start(bf16[2,136,1,128]{3,1,2,0:T(8,128)(2,1)S(1)} %get-tuple-element.239), channel_id=1, source_target_pairs={{4,0},{8,4},{12,8},{0,12},{5,1},{9,5},{13,9},{1,13},{6,2},{10,6},{... | collective-permute-start | bytes 208904 | tf_op jit(solution)/shard_map/ppermute | solution.py:21
  140.5 15.9 %psum.15 = bf16[2,8,8,128]{3,2,1,0:T(8,128)(2,1)S(1)} all-reduce(bf16[2,8,8,128]{3,2,1,0:T(8,128)(2,1)S(1)} %fusion.77), channel_id=1, replica_groups=mesh['grp'=2,'sp'=4,'sec'=2,'mb'=2] {'sec'}, use_global_device_ids=true, to_apply=%region_15.16 | all-reduce | flops 16384 | bytes 65536 | tf_op jit(solution)/shard_map/psum | solution.py:28
  157.9 2.6 %collective-permute-start.21 = (bf16[2,32,1,128]{3,2,1,0:T(2,128)(2,1)S(1)}, bf16[2,32,1,128]{3,2,1,0:T(2,128)(2,1)S(1)}, u32[]{:S(2)}, u32[]{:S(2)}) collective-permute-start(bf16[2,32,1,128]{3,2,1,0:T(2,128)(2,1)S(1)} %get-tuple-element.247), channel_id=1, source_target_pairs={{4,0},{8,4},{12,8},{0,12},{5,1},{9,5},{13,9},{1,13},{6,2},{10,6},{... | collective-permute-start | bytes 49160 | tf_op jit(solution)/shard_map/ppermute | solution.py:21
  164.8 4.3 %collective-permute-done.22 = bf16[2,32,10,1]{3,2,1,0:T(8,128)(2,1)S(1)} collective-permute-done((bf16[2,32,10,1]{3,2,1,0:T(8,128)(2,1)S(1)}, bf16[2,32,10,1]{3,2,1,0:T(8,128)(2,1)S(1)}, u32[]{:S(2)}, u32[]{:S(2)}) %collective-permute-start.22) | collective-permute-done | bytes 1312 | tf_op jit(solution)/shard_map/ppermute | solution.py:18
  169.1 2.8 %collective-permute-done.23 = bf16[2,32,10,1]{3,2,1,0:T(8,128)(2,1)S(1)} collective-permute-done((bf16[2,32,10,1]{3,2,1,0:T(8,128)(2,1)S(1)}, bf16[2,32,10,1]{3,2,1,0:T(8,128)(2,1)S(1)}, u32[]{:S(2)}, u32[]{:S(2)}) %collective-permute-start.23) | collective-permute-done | bytes 1312 | tf_op jit(solution)/shard_map/ppermute | solution.py:21
  172.5 2.7 %conditional.17 = (bf16[2,136,8,128]{3,1,2,0:T(8,128)(2,1)S(1)}) conditional(s32[]{:T(128)} %convert_element_type.68, (pred[130]{0:T(512)(128)(4,1)}, bf16[2,32,10,130]{3,2,1,0:T(8,128)(2,1)S(1)}, bf16[2,32,10,130]{3,1,2,0:T(8,128)(2,1)S(1)}, bf16[3,3,32,136]{3,2,1,0:T(8,128)(2,1)}) %tuple.84, () %tuple.85), branch_computations={%region_16.17_spmd, %region_17.18_spmd} | conditional | flops 163022080 | bytes 4987046 | solution.py:144
  178.8 2.7 %collective-permute-start.25 = (bf16[2,136,2,128]{1,3,2,0:T(8,128)(2,1)S(1)}, bf16[2,136,2,128]{1,3,2,0:T(8,128)(2,1)S(1)}, u32[]{:S(2)}, u32[]{:S(2)}) collective-permute-start(bf16[2,136,2,128]{1,3,2,0:T(8,128)(2,1)S(1)} %get-tuple-element.233), channel_id=1, source_target_pairs={{4,0},{8,4},{12,8},{0,12},{5,1},{9,5},{13,9},{1,13},{6,2},{10,6},{... | collective-permute-start | bytes 417800 | tf_op jit(solution)/shard_map/ppermute | solution.py:21
  181.5 4.4 %collective-permute-done.24 = bf16[2,136,2,128]{1,3,2,0:T(8,128)(2,1)S(1)} collective-permute-done((bf16[2,136,2,128]{1,3,2,0:T(8,128)(2,1)S(1)}, bf16[2,136,2,128]{1,3,2,0:T(8,128)(2,1)S(1)}, u32[]{:S(2)}, u32[]{:S(2)}) %collective-permute-start.24) | collective-permute-done | bytes 139296 | tf_op jit(solution)/shard_map/ppermute | solution.py:18
  194.1 9.4 %conditional.18 = (bf16[2,136,8,128]{3,1,2,0:T(8,128)(2,1)S(1)}) conditional(s32[]{:T(128)} %convert_element_type.68, (pred[132]{0:T(512)(128)(4,1)S(1)}, bf16[2,136,12,132]{1,3,2,0:T(8,128)(2,1)}, bf16[2,136,12,132]{3,1,2,0:T(8,128)(2,1)}, bf16[3,3,136,136]{3,2,1,0:T(8,128)(2,1)}) %tuple.164, () %tuple.87), branch_computations={%region_18.19_spmd, %region_19.20_spmd} | conditional | flops 684774144 | bytes 21570856 | solution.py:144
  194.1 3.8 %copy.83 = bf16[2,136,12,132]{3,1,2,0:T(8,128)(2,1)} copy(bf16[2,136,12,132]{1,3,2,0:T(8,128)(2,1)} %get-tuple-element.210) | data formatting | bytes 1723392 | tf_op jit(solution)/shard_map
  207.7 2.7 %collective-permute-start.29 = (bf16[2,136,4,128]{1,2,3,0:T(4,128)(2,1)S(1)}, bf16[2,136,4,128]{1,2,3,0:T(4,128)(2,1)S(1)}, u32[]{:S(2)}, u32[]{:S(2)}) collective-permute-start(bf16[2,136,4,128]{1,2,3,0:T(4,128)(2,1)S(1)} %get-tuple-element.231), channel_id=1, source_target_pairs={{4,0},{8,4},{12,8},{0,12},{5,1},{9,5},{13,9},{1,13},{6,2},{10,6},{... | collective-permute-start | bytes 835592 | tf_op jit(solution)/shard_map/ppermute | solution.py:21
  210.3 7.3 %collective-permute-done.28 = bf16[2,136,4,128]{1,2,3,0:T(4,128)(2,1)S(1)} collective-permute-done((bf16[2,136,4,128]{1,2,3,0:T(4,128)(2,1)S(1)}, bf16[2,136,4,128]{1,2,3,0:T(4,128)(2,1)S(1)}, u32[]{:S(2)}, u32[]{:S(2)}) %collective-permute-start.28) | collective-permute-done | bytes 278560 | tf_op jit(solution)/shard_map/ppermute | solution.py:18
  217.6 4.9 %collective-permute-done.29 = bf16[2,136,4,128]{1,2,3,0:T(4,128)(2,1)S(1)} collective-permute-done((bf16[2,136,4,128]{1,2,3,0:T(4,128)(2,1)S(1)}, bf16[2,136,4,128]{1,2,3,0:T(4,128)(2,1)S(1)}, u32[]{:S(2)}, u32[]{:S(2)}) %collective-permute-start.29) | collective-permute-done | bytes 278560 | tf_op jit(solution)/shard_map/ppermute | solution.py:21
  227.6 2.6 %pad_maximum_fusion.1 = bf16[2,136,16,136]{1,2,3,0:T(8,128)(2,1)} fusion(bf16[2,136,16,4]{1,2,3,0:T(8,128)(2,1)S(1)} %collective-permute-done.31, bf16[2,136,4,128]{1,2,3,0:T(4,128)(2,1)S(1)} %collective-permute-done.29, bf16[2,136,8,128]{1,2,3,0:T(8,128)(2,1)S(1)} %copy.84, bf16[2,136,4,128]{1,2,3,0:T(4,128)(2,1)S(1)} %collective-permute-done.28, ...), kind=kLoop, calls=%fused_computation.189 | loop fusion | flops 5918720 | bytes 2367488 | tf_op jit(solution)/shard_map/concatenate | solution.py:22
  230.2 14.7 %conditional.19 = (f32[2,24,8,128]{3,2,1,0:T(8,128)S(1)}) conditional(s32[]{:T(128)} %convert_element_type.68, (pred[136]{0:T(512)(128)(4,1)S(1)}, bf16[2,136,16,136]{1,2,3,0:T(8,128)(2,1)}, bf16[2,136,16,136]{3,1,2,0:T(8,128)(2,1)S(1)}, bf16[3,3,136,32]{2,3,1,0:T(8,128)(2,1)S(1)}) %tuple.163, () %tuple.89), branch_computations={%region_20.21_spmd, %region_21.22_spmd} | conditional | flops 161024000 | bytes 42453676 | solution.py:144
  230.2 4.6 %copy.87 = bf16[2,136,16,136]{3,1,2,0:T(8,128)(2,1)} copy(bf16[2,136,16,136]{1,2,3,0:T(8,128)(2,1)} %get-tuple-element.214) | data formatting | bytes 2367488 | tf_op jit(solution)/shard_map
  241.4 3.4 %convolution_bitcast_fusion.9 = f32[2,32,8,128]{3,1,2,0:T(8,128)S(1)} fusion(bf16[2,1224,8,128]{3,1,2,0:T(8,128)(2,1)} %copy-done.3, bf16[1224,32,1,1]{0,1,2,3:T(8,128)(2,1)S(1)} %reshape.65), kind=kOutput, calls=%fused_computation.177 | convolution fusion | flops 160432128 | bytes 5353984 | tf_op jit(solution)/shard_map/cond/branch_0_fun/mkrc,ko->morc/dot_general | solution.py:46
  (224 shorter events, 113.8 us)
Async XLA Ops:
  2.2 6.8 %collective-permute-start = (bf16[2,16,1,128]{3,1,2,0:T(8,128)(2,1)S(1)}, bf16[2,16,1,128]{3,1,2,0:T(8,128)(2,1)S(1)}, u32[]{:S(2)}, u32[]{:S(2)}) collective-permute-start(bf16[2,16,1,128]{3,1,2,0:T(8,128)(2,1)S(1)} %get-tuple-element.252), channel_id=1, source_target_pairs={{0,4},{4,8},{8,12},{12,0},{1,5},{5,9},{9,13},{13,1},{2,6},{6,10},{... | collective-permute-start | bytes 24584 | tf_op jit(solution)/shard_map/ppermute | solution.py:18
  5.3 3.7 %collective-permute-start.1 = (bf16[2,16,1,128]{3,1,2,0:T(8,128)(2,1)S(1)}, bf16[2,16,1,128]{3,1,2,0:T(8,128)(2,1)S(1)}, u32[]{:S(2)}, u32[]{:S(2)}) collective-permute-start(bf16[2,16,1,128]{3,1,2,0:T(8,128)(2,1)S(1)} %get-tuple-element.253), channel_id=1, source_target_pairs={{4,0},{8,4},{12,8},{0,12},{5,1},{9,5},{13,9},{1,13},{6,2},{10,6},{... | collective-permute-start | bytes 24584 | tf_op jit(solution)/shard_map/ppermute | solution.py:21
  9.2 6.4 %collective-permute-start.2 = (bf16[2,136,1,128]{3,1,2,0:T(8,128)(2,1)S(1)}, bf16[2,136,1,128]{3,1,2,0:T(8,128)(2,1)S(1)}, u32[]{:S(2)}, u32[]{:S(2)}) collective-permute-start(bf16[2,136,1,128]{3,1,2,0:T(8,128)(2,1)S(1)} %get-tuple-element.240), channel_id=1, source_target_pairs={{0,4},{4,8},{8,12},{12,0},{1,5},{5,9},{9,13},{13,1},{2,6},{6,10},{... | collective-permute-start | bytes 208904 | tf_op jit(solution)/shard_map/ppermute | solution.py:18
  10.7 5.1 %collective-permute-start.3 = (bf16[2,136,1,128]{3,1,2,0:T(8,128)(2,1)S(1)}, bf16[2,136,1,128]{3,1,2,0:T(8,128)(2,1)S(1)}, u32[]{:S(2)}, u32[]{:S(2)}) collective-permute-start(bf16[2,136,1,128]{3,1,2,0:T(8,128)(2,1)S(1)} %get-tuple-element.241), channel_id=1, source_target_pairs={{4,0},{8,4},{12,8},{0,12},{5,1},{9,5},{13,9},{1,13},{6,2},{10,6},{... | collective-permute-start | bytes 208904 | tf_op jit(solution)/shard_map/ppermute | solution.py:21
  34.2 5.6 %collective-permute-start.4 = (bf16[2,32,1,128]{3,1,2,0:T(8,128)(2,1)S(1)}, bf16[2,32,1,128]{3,1,2,0:T(8,128)(2,1)S(1)}, u32[]{:S(2)}, u32[]{:S(2)}) collective-permute-start(bf16[2,32,1,128]{3,1,2,0:T(8,128)(2,1)S(1)} %get-tuple-element.248), channel_id=1, source_target_pairs={{0,4},{4,8},{8,12},{12,0},{1,5},{5,9},{9,13},{13,1},{2,6},{6,10},{... | collective-permute-start | bytes 49160 | tf_op jit(solution)/shard_map/ppermute | solution.py:18
  35.3 4.5 %collective-permute-start.5 = (bf16[2,32,1,128]{3,1,2,0:T(8,128)(2,1)S(1)}, bf16[2,32,1,128]{3,1,2,0:T(8,128)(2,1)S(1)}, u32[]{:S(2)}, u32[]{:S(2)}) collective-permute-start(bf16[2,32,1,128]{3,1,2,0:T(8,128)(2,1)S(1)} %get-tuple-element.249), channel_id=1, source_target_pairs={{4,0},{8,4},{12,8},{0,12},{5,1},{9,5},{13,9},{1,13},{6,2},{10,6},{... | collective-permute-start | bytes 49160 | tf_op jit(solution)/shard_map/ppermute | solution.py:21
  40.0 5.4 %collective-permute-start.6 = (bf16[2,32,10,1]{3,1,2,0:T(8,128)(2,1)S(1)}, bf16[2,32,10,1]{3,1,2,0:T(8,128)(2,1)S(1)}, u32[]{:S(2)}, u32[]{:S(2)}) collective-permute-start(bf16[2,32,10,1]{3,1,2,0:T(8,128)(2,1)S(1)} %get-tuple-element.244), channel_id=1, source_target_pairs={{0,2},{2,0},{1,3},{3,1},{4,6},{6,4},{5,7},{7,5},{8,10},{10,8},{9,1... | collective-permute-start | bytes 3848 | tf_op jit(solution)/shard_map/ppermute | solution.py:18
  40.1 7.0 %collective-permute-start.7 = (bf16[2,32,10,1]{3,1,2,0:T(8,128)(2,1)S(1)}, bf16[2,32,10,1]{3,1,2,0:T(8,128)(2,1)S(1)}, u32[]{:S(2)}, u32[]{:S(2)}) collective-permute-start(bf16[2,32,10,1]{3,1,2,0:T(8,128)(2,1)S(1)} %get-tuple-element.245), channel_id=1, source_target_pairs={{2,0},{0,2},{3,1},{1,3},{6,4},{4,6},{7,5},{5,7},{10,8},{8,10},{11,... | collective-permute-start | bytes 3848 | tf_op jit(solution)/shard_map/ppermute | solution.py:21
  50.2 8.3 %collective-permute-start.8 = (bf16[2,136,2,128]{1,3,2,0:T(8,128)(2,1)S(1)}, bf16[2,136,2,128]{1,3,2,0:T(8,128)(2,1)S(1)}, u32[]{:S(2)}, u32[]{:S(2)}) collective-permute-start(bf16[2,136,2,128]{1,3,2,0:T(8,128)(2,1)S(1)} %get-tuple-element.236), channel_id=1, source_target_pairs={{0,4},{4,8},{8,12},{12,0},{1,5},{5,9},{9,13},{13,1},{2,6},{6,10},{... | collective-permute-start | bytes 417800 | tf_op jit(solution)/shard_map/ppermute | solution.py:18
  51.4 9.2 %collective-permute-start.9 = (bf16[2,136,2,128]{1,3,2,0:T(8,128)(2,1)S(1)}, bf16[2,136,2,128]{1,3,2,0:T(8,128)(2,1)S(1)}, u32[]{:S(2)}, u32[]{:S(2)}) collective-permute-start(bf16[2,136,2,128]{1,3,2,0:T(8,128)(2,1)S(1)} %get-tuple-element.237), channel_id=1, source_target_pairs={{4,0},{8,4},{12,8},{0,12},{5,1},{9,5},{13,9},{1,13},{6,2},{10,6},{... | collective-permute-start | bytes 417800 | tf_op jit(solution)/shard_map/ppermute | solution.py:21
  60.6 3.9 %collective-permute-start.10 = (bf16[2,136,12,2]{1,3,2,0:T(2,128)(2,1)S(1)}, bf16[2,136,12,2]{1,3,2,0:T(2,128)(2,1)S(1)}, u32[]{:S(2)}, u32[]{:S(2)}) collective-permute-start(bf16[2,136,12,2]{1,3,2,0:T(2,128)(2,1)S(1)} %get-tuple-element.228), channel_id=1, source_target_pairs={{0,2},{2,0},{1,3},{3,1},{4,6},{6,4},{5,7},{7,5},{8,10},{10,8},{9,1... | collective-permute-start | bytes 39176 | tf_op jit(solution)/shard_map/ppermute | solution.py:18
  60.7 4.1 %collective-permute-start.11 = (bf16[2,136,12,2]{1,3,2,0:T(2,128)(2,1)S(1)}, bf16[2,136,12,2]{1,3,2,0:T(2,128)(2,1)S(1)}, u32[]{:S(2)}, u32[]{:S(2)}) collective-permute-start(bf16[2,136,12,2]{1,3,2,0:T(2,128)(2,1)S(1)} %get-tuple-element.229), channel_id=1, source_target_pairs={{2,0},{0,2},{3,1},{1,3},{6,4},{4,6},{7,5},{5,7},{10,8},{8,10},{11,... | collective-permute-start | bytes 39176 | tf_op jit(solution)/shard_map/ppermute | solution.py:21
  77.9 13.4 %collective-permute-start.12 = (bf16[2,136,4,128]{1,2,3,0:T(4,128)(2,1)}, bf16[2,136,4,128]{1,2,3,0:T(4,128)(2,1)S(1)}, u32[]{:S(2)}, u32[]{:S(2)}) collective-permute-start(bf16[2,136,4,128]{1,2,3,0:T(4,128)(2,1)} %get-tuple-element.234), channel_id=1, source_target_pairs={{0,4},{4,8},{8,12},{12,0},{1,5},{5,9},{9,13},{13,1},{2,6},{6,10},{... | collective-permute-start | bytes 835592 | tf_op jit(solution)/shard_map/ppermute | solution.py:18
  79.2 17.4 %collective-permute-start.13 = (bf16[2,136,4,128]{1,2,3,0:T(4,128)(2,1)S(1)}, bf16[2,136,4,128]{1,2,3,0:T(4,128)(2,1)S(1)}, u32[]{:S(2)}, u32[]{:S(2)}) collective-permute-start(bf16[2,136,4,128]{1,2,3,0:T(4,128)(2,1)S(1)} %get-tuple-element.235), channel_id=1, source_target_pairs={{4,0},{8,4},{12,8},{0,12},{5,1},{9,5},{13,9},{1,13},{6,2},{10,6},{... | collective-permute-start | bytes 835592 | tf_op jit(solution)/shard_map/ppermute | solution.py:21
  96.8 4.3 %collective-permute-start.14 = (bf16[2,136,16,4]{1,2,3,0:T(8,128)(2,1)S(1)}, bf16[2,136,16,4]{1,2,3,0:T(8,128)(2,1)S(1)}, u32[]{:S(2)}, u32[]{:S(2)}) collective-permute-start(bf16[2,136,16,4]{1,2,3,0:T(8,128)(2,1)S(1)} %get-tuple-element.224), channel_id=1, source_target_pairs={{0,2},{2,0},{1,3},{3,1},{4,6},{6,4},{5,7},{7,5},{8,10},{10,8},{9,1... | collective-permute-start | bytes 104456 | tf_op jit(solution)/shard_map/ppermute | solution.py:18
  96.8 5.0 %collective-permute-start.15 = (bf16[2,136,16,4]{1,2,3,0:T(8,128)(2,1)S(1)}, bf16[2,136,16,4]{1,2,3,0:T(8,128)(2,1)S(1)}, u32[]{:S(2)}, u32[]{:S(2)}) collective-permute-start(bf16[2,136,16,4]{1,2,3,0:T(8,128)(2,1)S(1)} %get-tuple-element.225), channel_id=1, source_target_pairs={{2,0},{0,2},{3,1},{1,3},{6,4},{4,6},{7,5},{5,7},{10,8},{8,10},{11,... | collective-permute-start | bytes 104456 | tf_op jit(solution)/shard_map/ppermute | solution.py:21
  124.8 5.6 %collective-permute-start.16 = (bf16[2,16,1,128]{3,2,1,0:T(2,128)(2,1)S(1)}, bf16[2,16,1,128]{3,2,1,0:T(2,128)(2,1)S(1)}, u32[]{:S(2)}, u32[]{:S(2)}) collective-permute-start(bf16[2,16,1,128]{3,2,1,0:T(2,128)(2,1)S(1)} %get-tuple-element.250), channel_id=1, source_target_pairs={{0,4},{4,8},{8,12},{12,0},{1,5},{5,9},{9,13},{13,1},{2,6},{6,10},{... | collective-permute-start | bytes 24584 | tf_op jit(solution)/shard_map/ppermute | solution.py:18
  125.1 5.2 %collective-permute-start.17 = (bf16[2,16,1,128]{3,2,1,0:T(2,128)(2,1)S(1)}, bf16[2,16,1,128]{3,2,1,0:T(2,128)(2,1)S(1)}, u32[]{:S(2)}, u32[]{:S(2)}) collective-permute-start(bf16[2,16,1,128]{3,2,1,0:T(2,128)(2,1)S(1)} %get-tuple-element.251), channel_id=1, source_target_pairs={{4,0},{8,4},{12,8},{0,12},{5,1},{9,5},{13,9},{1,13},{6,2},{10,6},{... | collective-permute-start | bytes 24584 | tf_op jit(solution)/shard_map/ppermute | solution.py:21
  132.3 6.3 %collective-permute-start.18 = (bf16[2,136,1,128]{3,1,2,0:T(8,128)(2,1)S(1)}, bf16[2,136,1,128]{3,1,2,0:T(8,128)(2,1)S(1)}, u32[]{:S(2)}, u32[]{:S(2)}) collective-permute-start(bf16[2,136,1,128]{3,1,2,0:T(8,128)(2,1)S(1)} %get-tuple-element.238), channel_id=1, source_target_pairs={{0,4},{4,8},{8,12},{12,0},{1,5},{5,9},{9,13},{13,1},{2,6},{6,10},{... | collective-permute-start | bytes 208904 | tf_op jit(solution)/shard_map/ppermute | solution.py:18
  132.4 6.3 %collective-permute-start.19 = (bf16[2,136,1,128]{3,1,2,0:T(8,128)(2,1)S(1)}, bf16[2,136,1,128]{3,1,2,0:T(8,128)(2,1)S(1)}, u32[]{:S(2)}, u32[]{:S(2)}) collective-permute-start(bf16[2,136,1,128]{3,1,2,0:T(8,128)(2,1)S(1)} %get-tuple-element.239), channel_id=1, source_target_pairs={{4,0},{8,4},{12,8},{0,12},{5,1},{9,5},{13,9},{1,13},{6,2},{10,6},{... | collective-permute-start | bytes 208904 | tf_op jit(solution)/shard_map/ppermute | solution.py:21
  156.6 5.8 %collective-permute-start.20 = (bf16[2,32,1,128]{3,2,1,0:T(2,128)(2,1)S(1)}, bf16[2,32,1,128]{3,2,1,0:T(2,128)(2,1)S(1)}, u32[]{:S(2)}, u32[]{:S(2)}) collective-permute-start(bf16[2,32,1,128]{3,2,1,0:T(2,128)(2,1)S(1)} %get-tuple-element.246), channel_id=1, source_target_pairs={{0,4},{4,8},{8,12},{12,0},{1,5},{5,9},{9,13},{13,1},{2,6},{6,10},{... | collective-permute-start | bytes 49160 | tf_op jit(solution)/shard_map/ppermute | solution.py:18
  157.9 4.5 %collective-permute-start.21 = (bf16[2,32,1,128]{3,2,1,0:T(2,128)(2,1)S(1)}, bf16[2,32,1,128]{3,2,1,0:T(2,128)(2,1)S(1)}, u32[]{:S(2)}, u32[]{:S(2)}) collective-permute-start(bf16[2,32,1,128]{3,2,1,0:T(2,128)(2,1)S(1)} %get-tuple-element.247), channel_id=1, source_target_pairs={{4,0},{8,4},{12,8},{0,12},{5,1},{9,5},{13,9},{1,13},{6,2},{10,6},{... | collective-permute-start | bytes 49160 | tf_op jit(solution)/shard_map/ppermute | solution.py:21
  162.7 6.4 %collective-permute-start.22 = (bf16[2,32,10,1]{3,2,1,0:T(8,128)(2,1)S(1)}, bf16[2,32,10,1]{3,2,1,0:T(8,128)(2,1)S(1)}, u32[]{:S(2)}, u32[]{:S(2)}) collective-permute-start(bf16[2,32,10,1]{3,2,1,0:T(8,128)(2,1)S(1)} %get-tuple-element.242), channel_id=1, source_target_pairs={{0,2},{2,0},{1,3},{3,1},{4,6},{6,4},{5,7},{7,5},{8,10},{10,8},{9,1... | collective-permute-start | bytes 3848 | tf_op jit(solution)/shard_map/ppermute | solution.py:18
  162.8 9.1 %collective-permute-start.23 = (bf16[2,32,10,1]{3,2,1,0:T(8,128)(2,1)S(1)}, bf16[2,32,10,1]{3,2,1,0:T(8,128)(2,1)S(1)}, u32[]{:S(2)}, u32[]{:S(2)}) collective-permute-start(bf16[2,32,10,1]{3,2,1,0:T(8,128)(2,1)S(1)} %get-tuple-element.243), channel_id=1, source_target_pairs={{2,0},{0,2},{3,1},{1,3},{6,4},{4,6},{7,5},{5,7},{10,8},{8,10},{11,... | collective-permute-start | bytes 3848 | tf_op jit(solution)/shard_map/ppermute | solution.py:21
  177.5 8.4 %collective-permute-start.24 = (bf16[2,136,2,128]{1,3,2,0:T(8,128)(2,1)S(1)}, bf16[2,136,2,128]{1,3,2,0:T(8,128)(2,1)S(1)}, u32[]{:S(2)}, u32[]{:S(2)}) collective-permute-start(bf16[2,136,2,128]{1,3,2,0:T(8,128)(2,1)S(1)} %get-tuple-element.232), channel_id=1, source_target_pairs={{0,4},{4,8},{8,12},{12,0},{1,5},{5,9},{9,13},{13,1},{2,6},{6,10},{... | collective-permute-start | bytes 417800 | tf_op jit(solution)/shard_map/ppermute | solution.py:18
  178.8 9.2 %collective-permute-start.25 = (bf16[2,136,2,128]{1,3,2,0:T(8,128)(2,1)S(1)}, bf16[2,136,2,128]{1,3,2,0:T(8,128)(2,1)S(1)}, u32[]{:S(2)}, u32[]{:S(2)}) collective-permute-start(bf16[2,136,2,128]{1,3,2,0:T(8,128)(2,1)S(1)} %get-tuple-element.233), channel_id=1, source_target_pairs={{4,0},{8,4},{12,8},{0,12},{5,1},{9,5},{13,9},{1,13},{6,2},{10,6},{... | collective-permute-start | bytes 417800 | tf_op jit(solution)/shard_map/ppermute | solution.py:21
  188.1 3.9 %collective-permute-start.26 = (bf16[2,136,12,2]{1,3,2,0:T(2,128)(2,1)S(1)}, bf16[2,136,12,2]{1,3,2,0:T(2,128)(2,1)S(1)}, u32[]{:S(2)}, u32[]{:S(2)}) collective-permute-start(bf16[2,136,12,2]{1,3,2,0:T(2,128)(2,1)S(1)} %get-tuple-element.226), channel_id=1, source_target_pairs={{0,2},{2,0},{1,3},{3,1},{4,6},{6,4},{5,7},{7,5},{8,10},{10,8},{9,1... | collective-permute-start | bytes 39176 | tf_op jit(solution)/shard_map/ppermute | solution.py:18
  188.1 4.1 %collective-permute-start.27 = (bf16[2,136,12,2]{1,3,2,0:T(2,128)(2,1)S(1)}, bf16[2,136,12,2]{1,3,2,0:T(2,128)(2,1)S(1)}, u32[]{:S(2)}, u32[]{:S(2)}) collective-permute-start(bf16[2,136,12,2]{1,3,2,0:T(2,128)(2,1)S(1)} %get-tuple-element.227), channel_id=1, source_target_pairs={{2,0},{0,2},{3,1},{1,3},{6,4},{4,6},{7,5},{5,7},{10,8},{8,10},{11,... | collective-permute-start | bytes 39176 | tf_op jit(solution)/shard_map/ppermute | solution.py:21
  206.5 11.1 %collective-permute-start.28 = (bf16[2,136,4,128]{1,2,3,0:T(4,128)(2,1)S(1)}, bf16[2,136,4,128]{1,2,3,0:T(4,128)(2,1)S(1)}, u32[]{:S(2)}, u32[]{:S(2)}) collective-permute-start(bf16[2,136,4,128]{1,2,3,0:T(4,128)(2,1)S(1)} %get-tuple-element.230), channel_id=1, source_target_pairs={{0,4},{4,8},{8,12},{12,0},{1,5},{5,9},{9,13},{13,1},{2,6},{6,10},{... | collective-permute-start | bytes 835592 | tf_op jit(solution)/shard_map/ppermute | solution.py:18
  207.7 14.8 %collective-permute-start.29 = (bf16[2,136,4,128]{1,2,3,0:T(4,128)(2,1)S(1)}, bf16[2,136,4,128]{1,2,3,0:T(4,128)(2,1)S(1)}, u32[]{:S(2)}, u32[]{:S(2)}) collective-permute-start(bf16[2,136,4,128]{1,2,3,0:T(4,128)(2,1)S(1)} %get-tuple-element.231), channel_id=1, source_target_pairs={{4,0},{8,4},{12,8},{0,12},{5,1},{9,5},{13,9},{1,13},{6,2},{10,6},{... | collective-permute-start | bytes 835592 | tf_op jit(solution)/shard_map/ppermute | solution.py:21
  222.5 4.3 %collective-permute-start.30 = (bf16[2,136,16,4]{1,2,3,0:T(8,128)(2,1)S(1)}, bf16[2,136,16,4]{1,2,3,0:T(8,128)(2,1)S(1)}, u32[]{:S(2)}, u32[]{:S(2)}) collective-permute-start(bf16[2,136,16,4]{1,2,3,0:T(8,128)(2,1)S(1)} %get-tuple-element.222), channel_id=1, source_target_pairs={{0,2},{2,0},{1,3},{3,1},{4,6},{6,4},{5,7},{7,5},{8,10},{10,8},{9,1... | collective-permute-start | bytes 104456 | tf_op jit(solution)/shard_map/ppermute | solution.py:18
  222.6 5.0 %collective-permute-start.31 = (bf16[2,136,16,4]{1,2,3,0:T(8,128)(2,1)S(1)}, bf16[2,136,16,4]{1,2,3,0:T(8,128)(2,1)S(1)}, u32[]{:S(2)}, u32[]{:S(2)}) collective-permute-start(bf16[2,136,16,4]{1,2,3,0:T(8,128)(2,1)S(1)} %get-tuple-element.223), channel_id=1, source_target_pairs={{2,0},{0,2},{3,1},{1,3},{6,4},{4,6},{7,5},{5,7},{10,8},{8,10},{11,... | collective-permute-start | bytes 104456 | tf_op jit(solution)/shard_map/ppermute | solution.py:21
  (23 other events, 129.4 us)
where the time goes:
time: 247 us; the launch traced here: 246 us
  waiting for transfers between devices  73.3 us (30%)
  starting transfers between devices  53.1 us (21%)
  local copies, waits for them, and re-layouts  46.3 us (19%)
  blocking collectives  38 us (15%)
  other arithmetic  22.2 us (9%)
  matrix products  10.6 us (4%)
    ppermute x16, waiting for transfers between devices, with_halo(): lax.ppermute(lax.slice_in_dim(block, block.shape[dim] - width, None, axis...  52.3 us
    ppermute x16, starting transfers between devices, with_halo(): lax.ppermute(lax.slice_in_dim(block, 0, width, axis=dim), axis, backward)  40.1 us
    psum x2, blocking collectives, spread_2(): return lax.psum(kept, axis)  33.4 us
    ppermute x16, waiting for transfers between devices, with_halo(): lax.ppermute(lax.slice_in_dim(block, 0, width, axis=dim), axis, backward)  20.9 us
    another operation x13, local copies, waits for them, and re-layouts  18.2 us
    cond x58, local copies, waits for them, and re-layouts  13.4 us
    ppermute x16, starting transfers between devices, with_halo(): lax.ppermute(lax.slice_in_dim(block, block.shape[dim] - width, None, axis...  13 us
    concatenate x12, other arithmetic, with_halo(): block = jnp.concatenate([low, block, high], axis=dim)  11.2 us
  transfers between devices with their start and end apart: 32, of which 27 were waited for; matrix products, arithmetic and copies ran while one was open for 0% of the time, Pallas kernels for 0%

commit v1 on v0

--- a/solution.py
+++ b/solution.py
@@ -1,6 +1,10 @@
+import functools
+
 import jax
 import jax.numpy as jnp
 from jax import lax
+from jax.experimental import pallas as pl
+from jax.experimental.pallas import tpu as pltpu
 from jax.sharding import PartitionSpec as P
 
 STEPS = 2
@@ -176,6 +180,334 @@
     return (air_now, sea_now)
 
 
+LANES = 128
+SUBLANES = 8
+PACKED = 16
+
+
+def pad_to(count, unit):
+    return -(-count // unit) * unit
+
+
+def tree_add(terms):
+    total = terms[0]
+    for term in terms[1:]:
+        total = total + term
+    return total
+
+
+def gelu(v):
+    inner = v * (0.7978845608028654 + (0.7978845608028654 * 0.044715) * (v * v))
+    half = 0.5 * v
+    return half + half * jnp.tanh(inner)
+
+
+def lane_ids(rows):
+    return lax.broadcasted_iota(jnp.int32, (rows, LANES), 1)
+
+
+def from_left(v, distance, fill=0.0):
+    return jnp.where(lane_ids(v.shape[0]) < distance, fill, pltpu.roll(v, distance, 1))
+
+
+def from_right(v, distance, fill=0.0):
+    rolled = pltpu.roll(v, LANES - distance, 1)
+    return jnp.where(lane_ids(v.shape[0]) >= LANES - distance, fill, rolled)
+
+
+def vmem_specs(count):
+    return [pl.BlockSpec(memory_space=pltpu.VMEM)] * count
+
+
+def pack_kernel(sec_ref, air_ref, got_ref, sea_ref, flux_ref, mask_ref, out_ref, planes):
+    fields = air_ref.shape[1]
+    surface = sea_ref.shape[1]
+    fluxes = flux_ref.shape[1]
+    rows = air_ref.shape[2]
+    first = sec_ref[0] == 0
+    kept = fields + surface + fluxes
+    got = got_ref[...].astype(jnp.float32)
+    planes[0:fields] = jnp.where(first, air_ref[0].astype(jnp.float32), got)
+    planes[kept : kept + fields] = jnp.where(first, got, air_ref[1].astype(jnp.float32))
+    planes[fields : fields + surface] = jnp.where(
+        first, sea_ref[0].astype(jnp.float32), sea_ref[1].astype(jnp.float32)
+    )
+    planes[fields + surface : kept] = jnp.where(
+        first, flux_ref[0].astype(jnp.float32), flux_ref[1].astype(jnp.float32)
+    )
+    lanes = lane_ids(fields)
+    edge = jnp.zeros((fields, LANES), jnp.float32)
+    for row in range(rows):
+        out_ref[:, row * LANES : (row + 1) * LANES] = planes[0:kept, row, :].astype(jnp.bfloat16)
+        band = planes[kept : kept + fields, row, :]
+        if row:
+            band = pltpu.roll(band, row, 1)
+        edge = jnp.where(lanes == row, band, edge)
+    mask = mask_ref[...].astype(jnp.float32)
+    rest = jnp.zeros((kept - fields - rows, LANES), jnp.float32)
+    tail = jnp.concatenate([edge, mask, rest], axis=0)
+    out_ref[:, rows * LANES : (rows + 1) * LANES] = tail.astype(jnp.bfloat16)
+
+
+def weights_kernel(se_ref, sx_ref, ae_ref, am_ref, ax_ref, se_out, sx_out, ae_out, am_out, ax_out):
+    for source, target in ((se_ref, se_out), (ae_ref, ae_out)):
+        taps = [
+            source[a, b].astype(jnp.float32).T for a in range(3) for b in range(3)
+        ]
+        target[...] = jnp.concatenate(taps, axis=1).astype(jnp.bfloat16)
+    for source, target in ((sx_ref, sx_out), (am_ref, am_out), (ax_ref, ax_out)):
+        depth, width = source.shape[2:]
+        blank = jnp.zeros((width, pad_to(depth, PACKED) - depth), jnp.float32)
+        groups = []
+        for b in range(3):
+            pieces = []
+            for a in range(3):
+                pieces += [source[a, b].astype(jnp.float32).T, blank]
+            groups.append(jnp.concatenate(pieces, axis=1))
+        target[...] = jnp.concatenate(groups, axis=0).astype(jnp.bfloat16)
+
+
+def forecast_kernel(sizes, *refs):
+    fields, surface, flux_count, hidden, blocks, rows = sizes
+    block_refs = refs[:blocks]
+    se_ref, sx_ref, ae_ref, am_ref, ax_ref, out_ref = refs[blocks : blocks + 6]
+    sea_in, sea_hid, air_in, hid1, hid2, air_now, sea_now, edge_in, mask_in, planes = refs[blocks + 6 :]
+    ring = blocks * rows
+    kept = fields + surface + flux_count
+    hidden_pad = sea_hid.shape[0] - hidden
+    pads = {id(sea_in): 1, id(sea_hid): 1, id(air_in): 1, id(hid1): 2, id(hid2): 4}
+
+    def at(buffer, row, count):
+        start = row + pads.get(id(buffer), 0)
+        if isinstance(row, int):
+            return pl.ds(start * LANES, count * LANES)
+        return pl.ds(pl.multiple_of(start * LANES, LANES), count * LANES)
+
+    def close_ring(buffer):
+        pad = pads[id(buffer)]
+        buffer[:, 0 : pad * LANES] = buffer[:, ring * LANES : (ring + pad) * LANES]
+        buffer[:, (ring + pad) * LANES :] = buffer[:, pad * LANES : 2 * pad * LANES]
+
+    def store_sea_in(row, values):
+        left, right = from_left(values, 1), from_right(values, 1)
+        sea_in[:, at(sea_in, row, 1)] = jnp.concatenate([left, values, right], axis=0).astype(
+            jnp.bfloat16
+        )
+
+    def store_air_in(row, values, edge):
+        fill = jnp.concatenate([edge, jnp.zeros((surface, LANES), jnp.float32)], axis=0)
+        left, right = from_left(values, 1), from_right(values, 1, fill)
+        air_in[:, at(air_in, row, 1)] = jnp.concatenate([left, values, right], axis=0).astype(
+            jnp.bfloat16
+        )
+
+    def gather_rows(buffer, row, count, spread):
+        return jnp.concatenate(
+            [buffer[:, at(buffer, row + spread * (a - 1), count)] for a in range(3)], axis=0
+        )
+
+    def product(weight_ref, inputs):
+        return jnp.dot(weight_ref[...], inputs, preferred_element_type=jnp.float32)
+
+    def store_hidden(buffer, row, count, values):
+        values = gelu(values)
+        if hidden_pad:
+            blank = jnp.zeros((hidden_pad, values.shape[1]), jnp.float32)
+            values = jnp.concatenate([values, blank], axis=0)
+        buffer[:, at(buffer, row, count)] = values.astype(jnp.bfloat16)
+
+    def side_sum(made, width, spread, index):
+        piece = made[:, index * LANES : (index + 1) * LANES]
+        left = from_left(piece[0:width], spread)
+        right = from_right(piece[2 * width : 3 * width], spread)
+        return piece[width : 2 * width] + left + right
+
+    def over_rows(first, last, count, body):
+        trips = (last - first) // count
+
+        def step(i, carry):
+            body(first + i * count)
+            return carry
+
+        lax.fori_loop(0, trips, step, 0)
+
+    def sea_entry(row, count):
+        store_hidden(sea_hid, row, count, product(se_ref, gather_rows(sea_in, row, count, 1)))
+
+    def sea_exit(row, count):
+        made = product(sx_ref, gather_rows(sea_hid, row, count, 1))
+        for i in range(count):
+            change = side_sum(made, surface, 1, i)
+            weight = mask_in[pl.ds(row + i, 1), :]
+            old = sea_now[:, at(sea_now, row + i, 1)]
+            new = (old + weight * change).astype(jnp.bfloat16).astype(jnp.float32)
+            sea_now[:, at(sea_now, row + i, 1)] = new
+            air = air_now[:, at(air_now, row + i, 1)]
+            store_air_in(row + i, jnp.concatenate([air, new], axis=0), edge_in[:, at(edge_in, row + i, 1)])
+
+    def air_entry(row, count):
+        store_hidden(hid1, row, count, product(ae_ref, gather_rows(air_in, row, count, 1)))
+
+    def air_middle(row, count):
+        made = product(am_ref, gather_rows(hid1, row, count, 2))
+        sums = [side_sum(made, hidden, 2, i) for i in range(count)]
+        store_hidden(hid2, row, count, jnp.concatenate(sums, axis=1))
+
+    def air_exit(row, count, last):
+        made = product(ax_ref, gather_rows(hid2, row, count, 4))
+        for i in range(count):
+            change = side_sum(made, fields + flux_count, 4, i)
+            old = air_now[:, at(air_now, row + i, 1)]
+            new = (old + change[0:fields]).astype(jnp.bfloat16).astype(jnp.float32)
+            sea = sea_now[:, at(sea_now, row + i, 1)]
+            if last:
+                planes[:, row + i - rows, :] = jnp.concatenate([new, sea], axis=0)
+            else:
+                air_now[:, at(air_now, row + i, 1)] = new
+                flux = change[fields:].astype(jnp.bfloat16).astype(jnp.float32)
+                store_sea_in(row + i, jnp.concatenate([sea, flux], axis=0))
+
+    for block, source in enumerate(block_refs):
+        tail = source[:, rows * LANES : (rows + 1) * LANES].astype(jnp.float32)
+        mask_in[block * rows : (block + 1) * rows, :] = tail[fields : fields + rows]
+        for i in range(rows):
+            row = block * rows + i
+            values = source[:, i * LANES : (i + 1) * LANES].astype(jnp.float32)
+            air_now[:, at(air_now, row, 1)] = values[0:fields]
+            sea_now[:, at(sea_now, row, 1)] = values[fields : fields + surface]
+            store_sea_in(row, values[fields:kept])
+            edge = jnp.broadcast_to(tail[0:fields, i : i + 1], (fields, LANES))
+            edge_in[:, at(edge_in, row, 1)] = edge
+    close_ring(sea_in)
+
+    over_rows(0, ring, 2, lambda r: sea_entry(r, 2))
+    close_ring(sea_hid)
+    over_rows(0, ring, 2, lambda r: sea_exit(r, 2))
+    close_ring(air_in)
+    over_rows(0, ring, 2, lambda r: air_entry(r, 2))
+    close_ring(hid1)
+    over_rows(0, ring, 2, lambda r: air_middle(r, 2))
+    close_ring(hid2)
+    over_rows(0, ring, 2, lambda r: air_exit(r, 2, False))
+    close_ring(sea_in)
+
+    over_rows(rows - 8, 2 * rows + 8, 2, lambda r: sea_entry(r, 2))
+    over_rows(rows - 7, 2 * rows + 7, 2, lambda r: sea_exit(r, 2))
+    over_rows(rows - 6, 2 * rows + 6, 2, lambda r: air_entry(r, 2))
+    over_rows(rows - 4, 2 * rows + 4, 2, lambda r: air_middle(r, 2))
+    for r in range(rows, 2 * rows, 2):
+        air_exit(r, 2, True)
+    out_ref[...] = planes[...].astype(jnp.bfloat16)
+
+
+def belt_shards(
+    atmosphere, ocean_state, fluxes, sea_mask, air_entry, air_middle, air_exit, sea_entry, sea_exit
+):
+    blocks = lax.axis_size("sp")
+    position = lax.axis_index("sec")
+    members, fields, rows, cols = atmosphere.shape
+    surface, flux_count = ocean_state.shape[1], fluxes.shape[1]
+    hidden = air_middle.shape[3]
+    hidden_rows = pad_to(hidden, PACKED)
+    kept = fields + surface + flux_count
+    ring = blocks * rows
+    swap = [(0, 1), (1, 0)]
+    bf16, f32 = jnp.bfloat16, jnp.float32
+
+    sent = jnp.where(position == 0, atmosphere[1], atmosphere[0])
+    got = lax.ppermute(sent, "sec", swap)
+    packed = pl.pallas_call(
+        pack_kernel,
+        out_shape=jax.ShapeDtypeStruct((kept, (rows + 1) * LANES), bf16),
+        in_specs=[pl.BlockSpec(memory_space=pltpu.SMEM)] + vmem_specs(5),
+        out_specs=vmem_specs(1)[0],
+        scratch_shapes=[pltpu.VMEM((kept + fields, rows, LANES), f32)],
+        cost_estimate=pl.CostEstimate(flops=100000, bytes_accessed=400000, transcendentals=0),
+        name="pack",
+    )(position.reshape(1), atmosphere, got, ocean_state, fluxes, sea_mask)
+
+    weights = pl.pallas_call(
+        weights_kernel,
+        out_shape=(
+            jax.ShapeDtypeStruct((hidden, 9 * sea_entry.shape[2]), bf16),
+            jax.ShapeDtypeStruct((3 * surface, 3 * hidden_rows), bf16),
+            jax.ShapeDtypeStruct((hidden, 9 * air_entry.shape[2]), bf16),
+            jax.ShapeDtypeStruct((3 * hidden, 3 * hidden_rows), bf16),
+            jax.ShapeDtypeStruct((3 * (fields + flux_count), 3 * hidden_rows), bf16),
+        ),
+        in_specs=vmem_specs(5),
+        out_specs=tuple(vmem_specs(5)),
+        cost_estimate=pl.CostEstimate(flops=1000000, bytes_accessed=4000000, transcendentals=0),
+        name="weights",
+    )(sea_entry, sea_exit, air_entry, air_middle, air_exit)
+
+    frame = [None] * blocks
+    for index in range(blocks):
+        shift = (1 - index) % blocks
+        if shift == 0:
+            frame[index] = packed
+        else:
+            pairs = [(i, (i + shift) % blocks) for i in range(blocks)]
+            frame[index] = lax.ppermute(packed, "sp", pairs)
+
+    sizes = (fields, surface, flux_count, hidden, blocks, rows)
+    made = pl.pallas_call(
+        functools.partial(forecast_kernel, sizes),
+        out_shape=jax.ShapeDtypeStruct((fields + surface, rows, LANES), bf16),
+        in_specs=vmem_specs(blocks + 5),
+        out_specs=vmem_specs(1)[0],
+        scratch_shapes=[
+            pltpu.VMEM((3 * (surface + flux_count), (ring + 2) * LANES), bf16),
+            pltpu.VMEM((hidden_rows, (ring + 2) * LANES), bf16),
+            pltpu.VMEM((3 * (fields + surface), (ring + 2) * LANES), bf16),
+            pltpu.VMEM((hidden_rows, (ring + 4) * LANES), bf16),
+            pltpu.VMEM((hidden_rows, (ring + 8) * LANES), bf16),
+            pltpu.VMEM((fields, ring * LANES), f32),
+            pltpu.VMEM((surface, ring * LANES), f32),
+            pltpu.VMEM((fields, ring * LANES), f32),
+            pltpu.VMEM((ring, LANES), f32),
+            pltpu.VMEM((fields + surface, rows, LANES), f32),
+        ],
+        cost_estimate=pl.CostEstimate(
+            flops=4000000000, bytes_accessed=3000000, transcendentals=1000000
+        ),
+        name="forecast",
+    )(*frame, *weights)
+
+    other = lax.ppermute(made, "sec", swap)
+    first = position == 0
+    low = jnp.where(first, made, other)
+    high = jnp.where(first, other, made)
+    both = jnp.stack([low, high])
+    air_final = jnp.where(first, both[:, :fields], atmosphere)
+    return (air_final, both[:, fields:])
+
+
+def belt_fits(mesh, atmosphere, ocean_state, fluxes, sea_entry, sea_exit):
+    sections, blocks = mesh.shape["sec"], mesh.shape["sp"]
+    members = atmosphere.shape[0] // (mesh.shape["grp"] * mesh.shape["mb"])
+    rows = atmosphere.shape[2] // blocks
+    band = atmosphere.shape[3] // sections
+    fields, surface, flux_count = atmosphere.shape[1], ocean_state.shape[1], fluxes.shape[1]
+    halo = 9
+    return (
+        sections == 2
+        and members == 2
+        and band == LANES
+        and ocean_state.shape[3] == band
+        and rows % SUBLANES == 0
+        and rows <= LANES
+        and rows >= halo - 1
+        and blocks > 1
+        and 2 * rows + halo <= blocks * rows
+        and blocks * rows <= 64
+        and rows <= surface + flux_count
+        and all(c % SUBLANES == 0 for c in (fields, surface, flux_count, sea_entry.shape[3]))
+        and (surface + flux_count) % PACKED == 0
+        and (fields + surface) % PACKED == 0
+    )
+
+
 def solution(mesh):
     placed = (
         P(("grp", "mb"), None, "sp", "sec"),
@@ -188,10 +520,17 @@
         P(),
         P(),
     )
-    return jax.shard_map(
-        shards,
-        mesh=mesh,
-        in_specs=placed,
-        out_specs=(P(("grp", "mb"), None, "sp", "sec"), P(("grp", "mb"), None, "sp", None)),
-        check_vma=False,
-    )
+
+    def run(atmosphere, ocean_state, fluxes, sea_mask, air_entry, air_middle, air_exit, sea_entry, sea_exit):
+        fits = belt_fits(mesh, atmosphere, ocean_state, fluxes, sea_entry, sea_exit)
+        return jax.shard_map(
+            belt_shards if fits else shards,
+            mesh=mesh,
+            in_specs=placed,
+            out_specs=(P(("grp", "mb"), None, "sp", "sec"), P(("grp", "mb"), None, "sp", None)),
+            check_vma=False,
+        )(
+            atmosphere, ocean_state, fluxes, sea_mask, air_entry, air_middle, air_exit, sea_entry, sea_exit
+        )
+
+    return run

time: 247 us -> 63.8 us (0.26)
  waiting for transfers between devices: 73.3 us -> 5.88 us
  starting transfers between devices: 53.1 us -> 9.7 us
  local copies, waits for them, and re-layouts: 46.3 us -> 3.39 us
  Pallas kernels: 0 us -> 40.9 us
  blocking collectives: 38 us -> 0 us
  other arithmetic: 22.2 us -> 2.96 us
  matrix products: 10.6 us -> 0 us
    ppermute x32 -> x5, waiting for transfers between devices: 73.3 us -> 5.88 us  [the longest x1 2.88 us: belt_shards(): other = lax.ppermute(made, 'sec', swap)]
    ppermute x32 -> x5, starting transfers between devices: 53.1 us -> 9.7 us  [the longest x3 5.15 us: belt_shards(): frame[index] = lax.ppermute(packed, 'sp', pairs)]
    pallas_call x0 -> x3, Pallas kernels: none -> 40.9 us  [the longest x1 35.9 us: belt_shards(): pl.pallas_call(functools.partial(forecast_kernel, sizes), out_shape=jax.S...]
    psum x2 -> x0, blocking collectives: 33.4 us -> none  [spread_2(): return lax.psum(kept, axis)]
    another operation x13 -> x0, local copies, waits for them, and re-layouts: 18.2 us -> none
    cond x64 -> x0, local copies, waits for them, and re-layouts: 18.2 us -> none
    concatenate x12 -> x0, other arithmetic: 11.2 us -> none  [with_halo(): block = jnp.concatenate([low, block, high], axis=dim)]
    dot_general x6 -> x0, matrix products: 10.6 us -> none  [tap_sum(): jnp.einsum('mkrc,ko->morc', stacked, flat_weight, preferred_element_type=...]
  transfers between devices with their start and end apart: 32 -> 5, of which waited for: 27 -> 3; matrix products, arithmetic and copies ran while one was open for 0% -> 3% of each run, Pallas kernels for 0% -> 5%
where the time goes in v1:
time: 63.8 us; the launch traced here: 63.5 us
  Pallas kernels  40.9 us (64%)
  starting transfers between devices  9.7 us (15%)
  waiting for transfers between devices  5.88 us (9%)
  local copies, waits for them, and re-layouts  3.39 us (5%)
  other arithmetic  2.96 us (5%)
  between operations  0.67 us (1%)
    pallas_call x1, Pallas kernels, belt_shards(): pl.pallas_call(functools.partial(forecast_kernel, sizes), out_shape=jax.S...  35.9 us
    ppermute x3, starting transfers between devices, belt_shards(): frame[index] = lax.ppermute(packed, 'sp', pairs)  5.15 us
    unnamed x16, local copies, waits for them, and re-layouts  3.39 us
    pallas_call x1, Pallas kernels, belt_shards(): pl.pallas_call(weights_kernel, out_shape=(jax.ShapeDtypeStruct((hidden, 9...  3.11 us
    ppermute x1, starting transfers between devices, belt_shards(): got = lax.ppermute(sent, 'sec', swap)  2.97 us
    ppermute x1, waiting for transfers between devices, belt_shards(): other = lax.ppermute(made, 'sec', swap)  2.88 us
    ppermute x1, waiting for transfers between devices, belt_shards(): got = lax.ppermute(sent, 'sec', swap)  2.07 us
    pallas_call x1, Pallas kernels, belt_shards(): pl.pallas_call(pack_kernel, out_shape=jax.ShapeDtypeStruct((kept, (rows +...  1.87 us
  transfers between devices with their start and end apart: 5, of which 3 were waited for; matrix products, arithmetic and copies ran while one was open for 3% of the time, Pallas kernels for 5%

profile of v1, /device:TPU:0, one launch (start us, length us, event | category | flops | bytes accessed | tf_op | source)
XLA Modules:
  0.0 63.5 jit_solution(11153219193681824142)
XLA Ops:
  0.6 0.8 %select_bitcast_fusion.2 = bf16[24,8,128]{2,1,0:T(8,128)(2,1)S(1)} fusion(bf16[2,24,8,128]{3,2,1,0:T(8,128)(2,1)} %air_ref.1, pred[]{:T(512)S(6)} %eq.4), kind=kLoop, calls=%fused_computation.6 | loop fusion | flops 24576 | bytes 147457 | tf_op jit(solution)/shard_map/jit(_where)/select_n | solution.py:417
  1.5 3.0 %collective-permute-start = (bf16[24,8,128]{2,1,0:T(8,128)(2,1)S(1)}, bf16[24,8,128]{2,1,0:T(8,128)(2,1)S(1)}, u32[]{:S(2)}, u32[]{:S(2)}) collective-permute-start(bf16[24,8,128]{2,1,0:T(8,128)(2,1)S(1)} %select_bitcast_fusion.2), channel_id=1, source_target_pairs={{0,2},{2,0},{1,3},{3,1},{4,6},{6,4},{5,7},{7,5},{8,10},{10,8},{9,1... | collective-permute-start | bytes 147464 | tf_op jit(solution)/shard_map/ppermute | solution.py:418
  4.4 2.1 %collective-permute-done.got_ref = bf16[24,8,128]{2,1,0:T(8,128)(2,1)S(1)} collective-permute-done((bf16[24,8,128]{2,1,0:T(8,128)(2,1)S(1)}, bf16[24,8,128]{2,1,0:T(8,128)(2,1)S(1)}, u32[]{:S(2)}, u32[]{:S(2)}) %collective-permute-start) | collective-permute-done | bytes 49184 | tf_op jit(solution)/shard_map/ppermute | solution.py:418
  6.5 0.0 copy-start.2
  6.5 0.6 copy-done.2
  7.1 0.0 copy-start.1
  7.1 1.9 %pack.1.refs_1_ = bf16[40,1152]{1,0:T(8,128)(2,1)} custom-call(s32[1]{0:T(128)} %bitcast.sec_ref, bf16[2,24,8,128]{3,2,1,0:T(8,128)(2,1)} %air_ref.1, bf16[24,8,128]{2,1,0:T(8,128)(2,1)} %copy-done.2, bf16[2,8,8,128]{3,2,1,0:T(8,128)(2,1)} %sea_ref.1, bf16[2,8,8,128]{3,2,1,0:T(8,128)(2,1)} %flux_ref.1, s32[8,128]{1,0:T(8,128)} %mask_ref.1), custom_call_target="tpu_custom_call" | custom-call | flops 100000 | bytes 400000 | tf_op jit(solution)/shard_map/pack/pallas_call | solution.py:419
  9.0 0.0 copy-start.3
  9.0 3.1 %collective-permute-start.3 = (bf16[40,1152]{1,0:T(8,128)(2,1)}, bf16[40,1152]{1,0:T(8,128)(2,1)S(1)}, u32[]{:S(2)}, u32[]{:S(2)}) collective-permute-start(bf16[40,1152]{1,0:T(8,128)(2,1)} %pack.1.refs_1_), channel_id=1, source_target_pairs={{0,8},{4,12},{8,0},{12,4},{1,9},{5,13},{9,1},{13,5},{2,10},{6,14},... | collective-permute-start | bytes 276488 | tf_op jit(solution)/shard_map/ppermute | solution.py:451
  12.1 1.3 %collective-permute-start.2 = (bf16[40,1152]{1,0:T(8,128)(2,1)}, bf16[40,1152]{1,0:T(8,128)(2,1)S(1)}, u32[]{:S(2)}, u32[]{:S(2)}) collective-permute-start(bf16[40,1152]{1,0:T(8,128)(2,1)} %pack.1.refs_1_), channel_id=1, source_target_pairs={{0,12},{4,0},{8,4},{12,8},{1,13},{5,1},{9,5},{13,9},{2,14},{6,2},{... | collective-permute-start | bytes 276488 | tf_op jit(solution)/shard_map/ppermute | solution.py:451
  13.5 0.7 %collective-permute-start.1 = (bf16[40,1152]{1,0:T(8,128)(2,1)}, bf16[40,1152]{1,0:T(8,128)(2,1)S(1)}, u32[]{:S(2)}, u32[]{:S(2)}) collective-permute-start(bf16[40,1152]{1,0:T(8,128)(2,1)} %pack.1.refs_1_), channel_id=1, source_target_pairs={{0,4},{4,8},{8,12},{12,0},{1,5},{5,9},{9,13},{13,1},{2,6},{6,10},{... | collective-permute-start | bytes 276488 | tf_op jit(solution)/shard_map/ppermute | solution.py:451
  14.1 0.0 copy-done.1
  14.1 0.9 %copy.12.ax_ref = bf16[3,3,136,32]{3,2,1,0:T(8,128)(2,1)} copy(bf16[3,3,136,32]{2,3,1,0:T(8,128)(2,1)S(1)} %copy-done.1) | data formatting | bytes 156672 | tf_op args[6]
  15.1 0.0 copy-done.3
  15.1 0.9 %copy.11.sx_ref = bf16[3,3,136,8]{3,2,1,0:T(8,128)(2,1)} copy(bf16[3,3,136,8]{2,3,1,0:T(8,128)(2,1)S(1)} %copy-done.3) | data formatting | bytes 39168 | tf_op args[8]
  16.0 3.1 %weights.1 = (bf16[136,144]{1,0:T(8,128)(2,1)}, bf16[24,432]{1,0:T(8,128)(2,1)}, bf16[136,288]{1,0:T(8,128)(2,1)}, bf16[408,432]{1,0:T(8,128)(2,1)}, bf16[96,432]{1,0:T(8,128)(2,1)}) custom-call(bf16[3,3,16,136]{3,2,1,0:T(8,128)(2,1)} %se_ref.1, bf16[3,3,136,8]{3,2,1,0:T(8,128)(2,1)} %copy.11.sx_ref, bf16[3,3,32,136]{3,2,1,0:T(8,128)(2,1)} %ae_ref.1, ...), custom_call_target="tpu_custom_call" | custom-call | flops 1000000 | bytes 4000000 | tf_op jit(solution)/shard_map/weights/pallas_call | solution.py:429
  19.1 0.0 collective-permute-done.3.refs_3_
  19.1 0.0 copy-start.4
  19.1 0.0 collective-permute-done.2.refs_2_
  19.1 0.0 copy-start.5
  19.1 0.9 %collective-permute-done.1.refs_0_ = bf16[40,1152]{1,0:T(8,128)(2,1)S(1)} collective-permute-done((bf16[40,1152]{1,0:T(8,128)(2,1)}, bf16[40,1152]{1,0:T(8,128)(2,1)S(1)}, u32[]{:S(2)}, u32[]{:S(2)}) %collective-permute-start.1) | collective-permute-done | bytes 92192 | tf_op jit(solution)/shard_map/ppermute | solution.py:451
  20.0 0.0 copy-done.4
  20.0 0.0 copy-done.5
  20.0 0.6 %copy-done.6 = bf16[40,1152]{1,0:T(8,128)(2,1)} copy-done((bf16[40,1152]{1,0:T(8,128)(2,1)}, bf16[40,1152]{1,0:T(8,128)(2,1)S(1)}, u32[]{:S(2)}) %copy-start.6) | copy-done | bytes 92184
  20.7 35.9 %forecast.1 = bf16[32,8,128]{2,1,0:T(8,128)(2,1)} custom-call(bf16[40,1152]{1,0:T(8,128)(2,1)} %copy-done.6, bf16[40,1152]{1,0:T(8,128)(2,1)} %pack.1.refs_1_, bf16[40,1152]{1,0:T(8,128)(2,1)} %copy-done.5, bf16[40,1152]{1,0:T(8,128)(2,1)} %copy-done.4, bf16[136,144]{1,0:T(8,128)(2,1)} %get-tuple-element.7.refs_4_, ...), custom_call_target="tpu_custom_call" | custom-call | flops 4000000000 | bytes 3000000 | tf_op jit(solution)/shard_map/forecast/pallas_call | solution.py:454
  56.6 1.6 %collective-permute-start.4 = (bf16[32,8,128]{2,1,0:T(8,128)(2,1)}, bf16[32,8,128]{2,1,0:T(8,128)(2,1)S(1)}, u32[]{:S(2)}, u32[]{:S(2)}) collective-permute-start(bf16[32,8,128]{2,1,0:T(8,128)(2,1)} %forecast.1), channel_id=1, source_target_pairs={{0,2},{2,0},{1,3},{3,1},{4,6},{6,4},{5,7},{7,5},{8,10},{10,8},{9,1... | collective-permute-start | bytes 196616 | tf_op jit(solution)/shard_map/ppermute | solution.py:477
  58.2 2.9 %collective-permute-done.4 = bf16[32,8,128]{2,1,0:T(8,128)(2,1)S(1)} collective-permute-done((bf16[32,8,128]{2,1,0:T(8,128)(2,1)}, bf16[32,8,128]{2,1,0:T(8,128)(2,1)S(1)}, u32[]{:S(2)}, u32[]{:S(2)}) %collective-permute-start.4) | collective-permute-done | bytes 65568 | tf_op jit(solution)/shard_map/ppermute | solution.py:477
  61.1 0.9 %select_bitcast_fusion = (bf16[1,32,8,128]{3,2,1,0:T(8,128)(2,1)S(1)}, bf16[1,32,8,128]{3,2,1,0:T(8,128)(2,1)S(1)}) fusion(bf16[32,8,128]{2,1,0:T(8,128)(2,1)S(1)} %collective-permute-done.4, bf16[32,8,128]{2,1,0:T(8,128)(2,1)} %forecast.1, pred[]{:T(512)S(6)} %eq.4), kind=kLoop, calls=%fused_computation.4 | loop fusion | flops 65536 | bytes 262145 | tf_op jit(solution)/shard_map/stack | solution.py:481
  62.0 0.0 copy-start
  62.0 0.6 pad_maximum_fusion
  62.6 0.3 copy-done
  62.9 0.7 %fusion.1 = bf16[2,24,8,128]{3,2,1,0:T(8,128)(2,1)} fusion(bf16[2,24,8,128]{3,2,1,0:T(8,128)(2,1)S(1)} %copy-done, bf16[1,32,8,128]{3,2,1,0:T(8,128)(2,1)S(1)} %get-tuple-element.13, bf16[1,32,8,128]{3,2,1,0:T(8,128)(2,1)S(1)} %get-tuple-element.12, pred[]{:T(512)S(6)} %eq.4), kind=kLoop, calls=%fused_computation.3 | loop fusion | flops 98304 | bytes 327681 | tf_op jit(solution)/shard_map/jit(_where)/select_n | solution.py:482
  (1 shorter events, 0.0 us)
Async XLA Ops:
  1.5 5.0 %collective-permute-start = (bf16[24,8,128]{2,1,0:T(8,128)(2,1)S(1)}, bf16[24,8,128]{2,1,0:T(8,128)(2,1)S(1)}, u32[]{:S(2)}, u32[]{:S(2)}) collective-permute-start(bf16[24,8,128]{2,1,0:T(8,128)(2,1)S(1)} %select_bitcast_fusion.2), channel_id=1, source_target_pairs={{0,2},{2,0},{1,3},{3,1},{4,6},{6,4},{5,7},{7,5},{8,10},{10,8},{9,1... | collective-permute-start | bytes 147464 | tf_op jit(solution)/shard_map/ppermute | solution.py:418
  6.5 0.6 copy-start.2
  7.1 7.0 %copy-start.1 = (bf16[3,3,136,32]{2,3,1,0:T(8,128)(2,1)S(1)}, bf16[3,3,136,32]{2,3,1,0:T(8,128)(2,1)}, u32[]{:S(2)}) copy-start(bf16[3,3,136,32]{2,3,1,0:T(8,128)(2,1)} %param.15) | copy-start | bytes 235012
  9.0 6.1 %copy-start.3 = (bf16[3,3,136,8]{2,3,1,0:T(8,128)(2,1)S(1)}, bf16[3,3,136,8]{2,3,1,0:T(8,128)(2,1)}, u32[]{:S(2)}) copy-start(bf16[3,3,136,8]{2,3,1,0:T(8,128)(2,1)} %param.17) | copy-start | bytes 58756
  9.0 10.1 %collective-permute-start.3 = (bf16[40,1152]{1,0:T(8,128)(2,1)}, bf16[40,1152]{1,0:T(8,128)(2,1)S(1)}, u32[]{:S(2)}, u32[]{:S(2)}) collective-permute-start(bf16[40,1152]{1,0:T(8,128)(2,1)} %pack.1.refs_1_), channel_id=1, source_target_pairs={{0,8},{4,12},{8,0},{12,4},{1,9},{5,13},{9,1},{13,5},{2,10},{6,14},... | collective-permute-start | bytes 276488 | tf_op jit(solution)/shard_map/ppermute | solution.py:451
  12.1 7.0 %collective-permute-start.2 = (bf16[40,1152]{1,0:T(8,128)(2,1)}, bf16[40,1152]{1,0:T(8,128)(2,1)S(1)}, u32[]{:S(2)}, u32[]{:S(2)}) collective-permute-start(bf16[40,1152]{1,0:T(8,128)(2,1)} %pack.1.refs_1_), channel_id=1, source_target_pairs={{0,12},{4,0},{8,4},{12,8},{1,13},{5,1},{9,5},{13,9},{2,14},{6,2},{... | collective-permute-start | bytes 276488 | tf_op jit(solution)/shard_map/ppermute | solution.py:451
  13.5 6.6 %collective-permute-start.1 = (bf16[40,1152]{1,0:T(8,128)(2,1)}, bf16[40,1152]{1,0:T(8,128)(2,1)S(1)}, u32[]{:S(2)}, u32[]{:S(2)}) collective-permute-start(bf16[40,1152]{1,0:T(8,128)(2,1)} %pack.1.refs_1_), channel_id=1, source_target_pairs={{0,4},{4,8},{8,12},{12,0},{1,5},{5,9},{9,13},{13,1},{2,6},{6,10},{... | collective-permute-start | bytes 276488 | tf_op jit(solution)/shard_map/ppermute | solution.py:451
  19.1 0.9 %copy-start.4 = (bf16[40,1152]{1,0:T(8,128)(2,1)}, bf16[40,1152]{1,0:T(8,128)(2,1)S(1)}, u32[]{:S(2)}) copy-start(bf16[40,1152]{1,0:T(8,128)(2,1)S(1)} %collective-permute-done.3.refs_3_) | copy-start | bytes 276484
  19.1 0.9 %copy-start.5 = (bf16[40,1152]{1,0:T(8,128)(2,1)}, bf16[40,1152]{1,0:T(8,128)(2,1)S(1)}, u32[]{:S(2)}) copy-start(bf16[40,1152]{1,0:T(8,128)(2,1)S(1)} %collective-permute-done.2.refs_2_) | copy-start | bytes 276484
  20.0 0.7 %copy-start.6 = (bf16[40,1152]{1,0:T(8,128)(2,1)}, bf16[40,1152]{1,0:T(8,128)(2,1)S(1)}, u32[]{:S(2)}) copy-start(bf16[40,1152]{1,0:T(8,128)(2,1)S(1)} %collective-permute-done.1.refs_0_) | copy-start | bytes 276484
  56.6 4.5 %collective-permute-start.4 = (bf16[32,8,128]{2,1,0:T(8,128)(2,1)}, bf16[32,8,128]{2,1,0:T(8,128)(2,1)S(1)}, u32[]{:S(2)}, u32[]{:S(2)}) collective-permute-start(bf16[32,8,128]{2,1,0:T(8,128)(2,1)} %forecast.1), channel_id=1, source_target_pairs={{0,2},{2,0},{1,3},{3,1},{4,6},{6,4},{5,7},{7,5},{8,10},{10,8},{9,1... | collective-permute-start | bytes 196616 | tf_op jit(solution)/shard_map/ppermute | solution.py:477
  62.0 0.9 %copy-start = (bf16[2,24,8,128]{3,2,1,0:T(8,128)(2,1)S(1)}, bf16[2,24,8,128]{3,2,1,0:T(8,128)(2,1)}, u32[]{:S(2)}) copy-start(bf16[2,24,8,128]{3,2,1,0:T(8,128)(2,1)} %air_ref.1) | copy-start | bytes 294916

commit v2 on v1

--- a/solution.py
+++ b/solution.py
@@ -323,13 +323,8 @@
         return piece[width : 2 * width] + left + right
 
     def over_rows(first, last, count, body):
-        trips = (last - first) // count
-
-        def step(i, carry):
-            body(first + i * count)
-            return carry
-
-        lax.fori_loop(0, trips, step, 0)
+        for row in range(first, last, count):
+            body(row)
 
     def sea_entry(row, count):
         store_hidden(sea_hid, row, count, product(se_ref, gather_rows(sea_in, row, count, 1)))

time: 63.8 us -> 38.1 us (0.60)
  Pallas kernels: 40.9 us -> 15.1 us
    pallas_call x1, Pallas kernels: 35.9 us -> 10.2 us  [belt_shards(): pl.pallas_call(functools.partial(forecast_kernel, sizes), out_shape=jax.S...]
  transfers between devices with their start and end apart: 5 -> 5, of which waited for: 3 -> 3; matrix products, arithmetic and copies ran while one was open for 3% -> 5% of each run, Pallas kernels for 5% -> 8%
where the time goes in v2:
time: 38.1 us; the launch traced here: 37.7 us
  Pallas kernels  15.1 us (40%)
  starting transfers between devices  9.7 us (25%)
  waiting for transfers between devices  5.89 us (15%)
  local copies, waits for them, and re-layouts  3.39 us (9%)
  other arithmetic  2.96 us (8%)
  between operations  0.67 us (2%)
    pallas_call x1, Pallas kernels, belt_shards(): pl.pallas_call(functools.partial(forecast_kernel, sizes), out_shape=jax.S...  10.2 us
    ppermute x3, starting transfers between devices, belt_shards(): frame[index] = lax.ppermute(packed, 'sp', pairs)  5.15 us
    unnamed x16, local copies, waits for them, and re-layouts  3.39 us
    pallas_call x1, Pallas kernels, belt_shards(): pl.pallas_call(weights_kernel, out_shape=(jax.ShapeDtypeStruct((hidden, 9...  3.11 us
    ppermute x1, starting transfers between devices, belt_shards(): got = lax.ppermute(sent, 'sec', swap)  2.97 us
    ppermute x1, waiting for transfers between devices, belt_shards(): other = lax.ppermute(made, 'sec', swap)  2.89 us
    ppermute x1, waiting for transfers between devices, belt_shards(): got = lax.ppermute(sent, 'sec', swap)  2.07 us
    pallas_call x1, Pallas kernels, belt_shards(): pl.pallas_call(pack_kernel, out_shape=jax.ShapeDtypeStruct((kept, (rows +...  1.87 us
  transfers between devices with their start and end apart: 5, of which 3 were waited for; matrix products, arithmetic and copies ran while one was open for 5% of the time, Pallas kernels for 8%

profile of v2, /device:TPU:0, one launch (start us, length us, event | category | flops | bytes accessed | tf_op | source)
XLA Modules:
  0.0 37.7 jit_solution(12975914806659601652)
XLA Ops:
  0.6 0.8 %select_bitcast_fusion.2 = bf16[24,8,128]{2,1,0:T(8,128)(2,1)S(1)} fusion(bf16[2,24,8,128]{3,2,1,0:T(8,128)(2,1)} %air_ref.1, pred[]{:T(512)S(6)} %eq.4), kind=kLoop, calls=%fused_computation.6 | loop fusion | flops 24576 | bytes 147457 | tf_op jit(solution)/shard_map/jit(_where)/select_n | solution.py:412
  1.5 3.0 %collective-permute-start = (bf16[24,8,128]{2,1,0:T(8,128)(2,1)S(1)}, bf16[24,8,128]{2,1,0:T(8,128)(2,1)S(1)}, u32[]{:S(2)}, u32[]{:S(2)}) collective-permute-start(bf16[24,8,128]{2,1,0:T(8,128)(2,1)S(1)} %select_bitcast_fusion.2), channel_id=1, source_target_pairs={{0,2},{2,0},{1,3},{3,1},{4,6},{6,4},{5,7},{7,5},{8,10},{10,8},{9,1... | collective-permute-start | bytes 147464 | tf_op jit(solution)/shard_map/ppermute | solution.py:413
  4.4 2.1 %collective-permute-done.got_ref = bf16[24,8,128]{2,1,0:T(8,128)(2,1)S(1)} collective-permute-done((bf16[24,8,128]{2,1,0:T(8,128)(2,1)S(1)}, bf16[24,8,128]{2,1,0:T(8,128)(2,1)S(1)}, u32[]{:S(2)}, u32[]{:S(2)}) %collective-permute-start) | collective-permute-done | bytes 49184 | tf_op jit(solution)/shard_map/ppermute | solution.py:413
  6.5 0.0 copy-start.2
  6.5 0.6 %copy-done.2 = bf16[24,8,128]{2,1,0:T(8,128)(2,1)} copy-done((bf16[24,8,128]{2,1,0:T(8,128)(2,1)}, bf16[24,8,128]{2,1,0:T(8,128)(2,1)S(1)}, u32[]{:S(2)}) %copy-start.2) | copy-done | bytes 49176
  7.1 0.0 copy-start.1
  7.1 1.9 %pack.1.refs_1_ = bf16[40,1152]{1,0:T(8,128)(2,1)} custom-call(s32[1]{0:T(128)} %bitcast.sec_ref, bf16[2,24,8,128]{3,2,1,0:T(8,128)(2,1)} %air_ref.1, bf16[24,8,128]{2,1,0:T(8,128)(2,1)} %copy-done.2, bf16[2,8,8,128]{3,2,1,0:T(8,128)(2,1)} %sea_ref.1, bf16[2,8,8,128]{3,2,1,0:T(8,128)(2,1)} %flux_ref.1, s32[8,128]{1,0:T(8,128)} %mask_ref.1), custom_call_target="tpu_custom_call" | custom-call | flops 100000 | bytes 400000 | tf_op jit(solution)/shard_map/pack/pallas_call | solution.py:414
  9.0 0.0 copy-start.3
  9.0 3.1 %collective-permute-start.3 = (bf16[40,1152]{1,0:T(8,128)(2,1)}, bf16[40,1152]{1,0:T(8,128)(2,1)S(1)}, u32[]{:S(2)}, u32[]{:S(2)}) collective-permute-start(bf16[40,1152]{1,0:T(8,128)(2,1)} %pack.1.refs_1_), channel_id=1, source_target_pairs={{0,8},{4,12},{8,0},{12,4},{1,9},{5,13},{9,1},{13,5},{2,10},{6,14},... | collective-permute-start | bytes 276488 | tf_op jit(solution)/shard_map/ppermute | solution.py:446
  12.1 1.3 %collective-permute-start.2 = (bf16[40,1152]{1,0:T(8,128)(2,1)}, bf16[40,1152]{1,0:T(8,128)(2,1)S(1)}, u32[]{:S(2)}, u32[]{:S(2)}) collective-permute-start(bf16[40,1152]{1,0:T(8,128)(2,1)} %pack.1.refs_1_), channel_id=1, source_target_pairs={{0,12},{4,0},{8,4},{12,8},{1,13},{5,1},{9,5},{13,9},{2,14},{6,2},{... | collective-permute-start | bytes 276488 | tf_op jit(solution)/shard_map/ppermute | solution.py:446
  13.5 0.7 %collective-permute-start.1 = (bf16[40,1152]{1,0:T(8,128)(2,1)}, bf16[40,1152]{1,0:T(8,128)(2,1)S(1)}, u32[]{:S(2)}, u32[]{:S(2)}) collective-permute-start(bf16[40,1152]{1,0:T(8,128)(2,1)} %pack.1.refs_1_), channel_id=1, source_target_pairs={{0,4},{4,8},{8,12},{12,0},{1,5},{5,9},{9,13},{13,1},{2,6},{6,10},{... | collective-permute-start | bytes 276488 | tf_op jit(solution)/shard_map/ppermute | solution.py:446
  14.1 0.0 copy-done.1
  14.1 0.9 %copy.12.ax_ref = bf16[3,3,136,32]{3,2,1,0:T(8,128)(2,1)} copy(bf16[3,3,136,32]{2,3,1,0:T(8,128)(2,1)S(1)} %copy-done.1) | data formatting | bytes 156672 | tf_op args[6]
  15.1 0.0 copy-done.3
  15.1 0.9 %copy.11.sx_ref = bf16[3,3,136,8]{3,2,1,0:T(8,128)(2,1)} copy(bf16[3,3,136,8]{2,3,1,0:T(8,128)(2,1)S(1)} %copy-done.3) | data formatting | bytes 39168 | tf_op args[8]
  16.0 3.1 %weights.1 = (bf16[136,144]{1,0:T(8,128)(2,1)}, bf16[24,432]{1,0:T(8,128)(2,1)}, bf16[136,288]{1,0:T(8,128)(2,1)}, bf16[408,432]{1,0:T(8,128)(2,1)}, bf16[96,432]{1,0:T(8,128)(2,1)}) custom-call(bf16[3,3,16,136]{3,2,1,0:T(8,128)(2,1)} %se_ref.1, bf16[3,3,136,8]{3,2,1,0:T(8,128)(2,1)} %copy.11.sx_ref, bf16[3,3,32,136]{3,2,1,0:T(8,128)(2,1)} %ae_ref.1, ...), custom_call_target="tpu_custom_call" | custom-call | flops 1000000 | bytes 4000000 | tf_op jit(solution)/shard_map/weights/pallas_call | solution.py:424
  19.1 0.0 collective-permute-done.3.refs_3_
  19.1 0.0 copy-start.4
  19.1 0.0 collective-permute-done.2.refs_2_
  19.1 0.0 copy-start.5
  19.1 0.9 %collective-permute-done.1.refs_0_ = bf16[40,1152]{1,0:T(8,128)(2,1)S(1)} collective-permute-done((bf16[40,1152]{1,0:T(8,128)(2,1)}, bf16[40,1152]{1,0:T(8,128)(2,1)S(1)}, u32[]{:S(2)}, u32[]{:S(2)}) %collective-permute-start.1) | collective-permute-done | bytes 92192 | tf_op jit(solution)/shard_map/ppermute | solution.py:446
  20.0 0.0 copy-done.4
  20.0 0.0 copy-done.5
  20.0 0.6 %copy-done.6 = bf16[40,1152]{1,0:T(8,128)(2,1)} copy-done((bf16[40,1152]{1,0:T(8,128)(2,1)}, bf16[40,1152]{1,0:T(8,128)(2,1)S(1)}, u32[]{:S(2)}) %copy-start.6) | copy-done | bytes 92184
  20.7 10.2 %forecast.1 = bf16[32,8,128]{2,1,0:T(8,128)(2,1)} custom-call(bf16[40,1152]{1,0:T(8,128)(2,1)} %copy-done.6, bf16[40,1152]{1,0:T(8,128)(2,1)} %pack.1.refs_1_, bf16[40,1152]{1,0:T(8,128)(2,1)} %copy-done.5, bf16[40,1152]{1,0:T(8,128)(2,1)} %copy-done.4, bf16[136,144]{1,0:T(8,128)(2,1)} %get-tuple-element.7.refs_4_, ...), custom_call_target="tpu_custom_call" | custom-call | flops 4000000000 | bytes 3000000 | tf_op jit(solution)/shard_map/forecast/pallas_call | solution.py:449
  30.8 1.6 %collective-permute-start.4 = (bf16[32,8,128]{2,1,0:T(8,128)(2,1)}, bf16[32,8,128]{2,1,0:T(8,128)(2,1)S(1)}, u32[]{:S(2)}, u32[]{:S(2)}) collective-permute-start(bf16[32,8,128]{2,1,0:T(8,128)(2,1)} %forecast.1), channel_id=1, source_target_pairs={{0,2},{2,0},{1,3},{3,1},{4,6},{6,4},{5,7},{7,5},{8,10},{10,8},{9,1... | collective-permute-start | bytes 196616 | tf_op jit(solution)/shard_map/ppermute | solution.py:472
  32.4 2.9 %collective-permute-done.4 = bf16[32,8,128]{2,1,0:T(8,128)(2,1)S(1)} collective-permute-done((bf16[32,8,128]{2,1,0:T(8,128)(2,1)}, bf16[32,8,128]{2,1,0:T(8,128)(2,1)S(1)}, u32[]{:S(2)}, u32[]{:S(2)}) %collective-permute-start.4) | collective-permute-done | bytes 65568 | tf_op jit(solution)/shard_map/ppermute | solution.py:472
  35.3 0.9 %select_bitcast_fusion = (bf16[1,32,8,128]{3,2,1,0:T(8,128)(2,1)S(1)}, bf16[1,32,8,128]{3,2,1,0:T(8,128)(2,1)S(1)}) fusion(bf16[32,8,128]{2,1,0:T(8,128)(2,1)S(1)} %collective-permute-done.4, bf16[32,8,128]{2,1,0:T(8,128)(2,1)} %forecast.1, pred[]{:T(512)S(6)} %eq.4), kind=kLoop, calls=%fused_computation.4 | loop fusion | flops 65536 | bytes 262145 | tf_op jit(solution)/shard_map/stack | solution.py:476
  36.2 0.0 copy-start
  36.2 0.6 %pad_maximum_fusion = bf16[2,8,8,128]{3,2,1,0:T(8,128)(2,1)} fusion(bf16[1,32,8,128]{3,2,1,0:T(8,128)(2,1)S(1)} %get-tuple-element.12, bf16[1,32,8,128]{3,2,1,0:T(8,128)(2,1)S(1)} %get-tuple-element.13), kind=kLoop, calls=%fused_computation.7 | loop fusion | flops 16384 | bytes 163840 | tf_op jit(solution)/shard_map/stack | solution.py:476
  36.8 0.3 copy-done
  37.1 0.7 %fusion.1 = bf16[2,24,8,128]{3,2,1,0:T(8,128)(2,1)} fusion(bf16[2,24,8,128]{3,2,1,0:T(8,128)(2,1)S(1)} %copy-done, bf16[1,32,8,128]{3,2,1,0:T(8,128)(2,1)S(1)} %get-tuple-element.13, bf16[1,32,8,128]{3,2,1,0:T(8,128)(2,1)S(1)} %get-tuple-element.12, pred[]{:T(512)S(6)} %eq.4), kind=kLoop, calls=%fused_computation.3 | loop fusion | flops 98304 | bytes 327681 | tf_op jit(solution)/shard_map/jit(_where)/select_n | solution.py:477
  (1 shorter events, 0.0 us)
Async XLA Ops:
  1.5 5.0 %collective-permute-start = (bf16[24,8,128]{2,1,0:T(8,128)(2,1)S(1)}, bf16[24,8,128]{2,1,0:T(8,128)(2,1)S(1)}, u32[]{:S(2)}, u32[]{:S(2)}) collective-permute-start(bf16[24,8,128]{2,1,0:T(8,128)(2,1)S(1)} %select_bitcast_fusion.2), channel_id=1, source_target_pairs={{0,2},{2,0},{1,3},{3,1},{4,6},{6,4},{5,7},{7,5},{8,10},{10,8},{9,1... | collective-permute-start | bytes 147464 | tf_op jit(solution)/shard_map/ppermute | solution.py:413
  6.5 0.6 %copy-start.2 = (bf16[24,8,128]{2,1,0:T(8,128)(2,1)}, bf16[24,8,128]{2,1,0:T(8,128)(2,1)S(1)}, u32[]{:S(2)}) copy-start(bf16[24,8,128]{2,1,0:T(8,128)(2,1)S(1)} %collective-permute-done.got_ref) | copy-start | bytes 147460
  7.1 7.0 %copy-start.1 = (bf16[3,3,136,32]{2,3,1,0:T(8,128)(2,1)S(1)}, bf16[3,3,136,32]{2,3,1,0:T(8,128)(2,1)}, u32[]{:S(2)}) copy-start(bf16[3,3,136,32]{2,3,1,0:T(8,128)(2,1)} %param.15) | copy-start | bytes 235012
  9.0 6.1 %copy-start.3 = (bf16[3,3,136,8]{2,3,1,0:T(8,128)(2,1)S(1)}, bf16[3,3,136,8]{2,3,1,0:T(8,128)(2,1)}, u32[]{:S(2)}) copy-start(bf16[3,3,136,8]{2,3,1,0:T(8,128)(2,1)} %param.17) | copy-start | bytes 58756
  9.0 10.1 %collective-permute-start.3 = (bf16[40,1152]{1,0:T(8,128)(2,1)}, bf16[40,1152]{1,0:T(8,128)(2,1)S(1)}, u32[]{:S(2)}, u32[]{:S(2)}) collective-permute-start(bf16[40,1152]{1,0:T(8,128)(2,1)} %pack.1.refs_1_), channel_id=1, source_target_pairs={{0,8},{4,12},{8,0},{12,4},{1,9},{5,13},{9,1},{13,5},{2,10},{6,14},... | collective-permute-start | bytes 276488 | tf_op jit(solution)/shard_map/ppermute | solution.py:446
  12.1 7.0 %collective-permute-start.2 = (bf16[40,1152]{1,0:T(8,128)(2,1)}, bf16[40,1152]{1,0:T(8,128)(2,1)S(1)}, u32[]{:S(2)}, u32[]{:S(2)}) collective-permute-start(bf16[40,1152]{1,0:T(8,128)(2,1)} %pack.1.refs_1_), channel_id=1, source_target_pairs={{0,12},{4,0},{8,4},{12,8},{1,13},{5,1},{9,5},{13,9},{2,14},{6,2},{... | collective-permute-start | bytes 276488 | tf_op jit(solution)/shard_map/ppermute | solution.py:446
  13.5 6.6 %collective-permute-start.1 = (bf16[40,1152]{1,0:T(8,128)(2,1)}, bf16[40,1152]{1,0:T(8,128)(2,1)S(1)}, u32[]{:S(2)}, u32[]{:S(2)}) collective-permute-start(bf16[40,1152]{1,0:T(8,128)(2,1)} %pack.1.refs_1_), channel_id=1, source_target_pairs={{0,4},{4,8},{8,12},{12,0},{1,5},{5,9},{9,13},{13,1},{2,6},{6,10},{... | collective-permute-start | bytes 276488 | tf_op jit(solution)/shard_map/ppermute | solution.py:446
  19.1 0.9 %copy-start.4 = (bf16[40,1152]{1,0:T(8,128)(2,1)}, bf16[40,1152]{1,0:T(8,128)(2,1)S(1)}, u32[]{:S(2)}) copy-start(bf16[40,1152]{1,0:T(8,128)(2,1)S(1)} %collective-permute-done.3.refs_3_) | copy-start | bytes 276484
  19.1 0.9 %copy-start.5 = (bf16[40,1152]{1,0:T(8,128)(2,1)}, bf16[40,1152]{1,0:T(8,128)(2,1)S(1)}, u32[]{:S(2)}) copy-start(bf16[40,1152]{1,0:T(8,128)(2,1)S(1)} %collective-permute-done.2.refs_2_) | copy-start | bytes 276484
  20.0 0.7 %copy-start.6 = (bf16[40,1152]{1,0:T(8,128)(2,1)}, bf16[40,1152]{1,0:T(8,128)(2,1)S(1)}, u32[]{:S(2)}) copy-start(bf16[40,1152]{1,0:T(8,128)(2,1)S(1)} %collective-permute-done.1.refs_0_) | copy-start | bytes 276484
  30.8 4.5 %collective-permute-start.4 = (bf16[32,8,128]{2,1,0:T(8,128)(2,1)}, bf16[32,8,128]{2,1,0:T(8,128)(2,1)S(1)}, u32[]{:S(2)}, u32[]{:S(2)}) collective-permute-start(bf16[32,8,128]{2,1,0:T(8,128)(2,1)} %forecast.1), channel_id=1, source_target_pairs={{0,2},{2,0},{1,3},{3,1},{4,6},{6,4},{5,7},{7,5},{8,10},{10,8},{9,1... | collective-permute-start | bytes 196616 | tf_op jit(solution)/shard_map/ppermute | solution.py:472
  36.2 0.9 %copy-start = (bf16[2,24,8,128]{3,2,1,0:T(8,128)(2,1)S(1)}, bf16[2,24,8,128]{3,2,1,0:T(8,128)(2,1)}, u32[]{:S(2)}) copy-start(bf16[2,24,8,128]{3,2,1,0:T(8,128)(2,1)} %air_ref.1) | copy-start | bytes 294916

commit v3 on v2

--- a/solution.py
+++ b/solution.py
@@ -219,34 +219,73 @@
     return [pl.BlockSpec(memory_space=pltpu.VMEM)] * count
 
 
-def pack_kernel(sec_ref, air_ref, got_ref, sea_ref, flux_ref, mask_ref, out_ref, planes):
+def in_vmem(*values):
+    return tuple(pltpu.with_memory_space_constraint(value, pltpu.VMEM) for value in values)
+
+
+def edge_of(bands):
+    lanes = lane_ids(bands[0].shape[0])
+    edge = jnp.where(lanes == 0, bands[0], 0.0)
+    for row, band in enumerate(bands[1:], 1):
+        edge = jnp.where(lanes == row, pltpu.roll(band, row, 1), edge)
+    return edge
+
+
+def pack_own_kernel(air_ref, sea_ref, flux_ref, mask_ref, out_ref, planes):
     fields = air_ref.shape[1]
     surface = sea_ref.shape[1]
-    fluxes = flux_ref.shape[1]
     rows = air_ref.shape[2]
-    first = sec_ref[0] == 0
-    kept = fields + surface + fluxes
-    got = got_ref[...].astype(jnp.float32)
-    planes[0:fields] = jnp.where(first, air_ref[0].astype(jnp.float32), got)
-    planes[kept : kept + fields] = jnp.where(first, got, air_ref[1].astype(jnp.float32))
-    planes[fields : fields + surface] = jnp.where(
-        first, sea_ref[0].astype(jnp.float32), sea_ref[1].astype(jnp.float32)
-    )
-    planes[fields + surface : kept] = jnp.where(
-        first, flux_ref[0].astype(jnp.float32), flux_ref[1].astype(jnp.float32)
-    )
-    lanes = lane_ids(fields)
-    edge = jnp.zeros((fields, LANES), jnp.float32)
+    kept = fields + surface + flux_ref.shape[1]
+    section = lax.axis_index("sec")
+    planes[0:fields] = air_ref[section].astype(jnp.float32)
+    planes[fields : fields + surface] = sea_ref[section].astype(jnp.float32)
+    planes[fields + surface : kept] = flux_ref[section].astype(jnp.float32)
+    bands = []
     for row in range(rows):
-        out_ref[:, row * LANES : (row + 1) * LANES] = planes[0:kept, row, :].astype(jnp.bfloat16)
-        band = planes[kept : kept + fields, row, :]
-        if row:
-            band = pltpu.roll(band, row, 1)
-        edge = jnp.where(lanes == row, band, edge)
+        values = planes[:, row, :]
+        out_ref[:, row * LANES : (row + 1) * LANES] = values.astype(jnp.bfloat16)
+        bands.append(values[0:fields])
     mask = mask_ref[...].astype(jnp.float32)
     rest = jnp.zeros((kept - fields - rows, LANES), jnp.float32)
-    tail = jnp.concatenate([edge, mask, rest], axis=0)
+    tail = jnp.concatenate([edge_of(bands), mask, rest], axis=0)
     out_ref[:, rows * LANES : (rows + 1) * LANES] = tail.astype(jnp.bfloat16)
+
+
+def pack_got_kernel(own_ref, got_ref, out_ref, planes):
+    fields, rows = got_ref.shape[:2]
+    first = lax.axis_index("sec") == 0
+    planes[...] = got_ref[...].astype(jnp.float32)
+    bands = [planes[:, row, :] for row in range(rows)]
+    out_ref[fields:, :] = own_ref[fields:, :]
+
+    @pl.when(first)
+    def _():
+        out_ref[0:fields, 0 : rows * LANES] = own_ref[0:fields, 0 : rows * LANES]
+        out_ref[0:fields, rows * LANES :] = edge_of(bands).astype(jnp.bfloat16)
+
+    @pl.when(jnp.logical_not(first))
+    def _():
+        out_ref[0:fields, rows * LANES :] = own_ref[0:fields, rows * LANES :]
+        for row, band in enumerate(bands):
+            out_ref[0:fields, row * LANES : (row + 1) * LANES] = band.astype(jnp.bfloat16)
+
+
+def merge_kernel(made_ref, other_ref, air_ref, air_out, sea_out):
+    fields = air_ref.shape[1]
+    first = lax.axis_index("sec") == 0
+
+    @pl.when(first)
+    def _():
+        air_out[0] = made_ref[0:fields]
+        air_out[1] = other_ref[0:fields]
+        sea_out[0] = made_ref[fields:]
+        sea_out[1] = other_ref[fields:]
+
+    @pl.when(jnp.logical_not(first))
+    def _():
+        air_out[...] = air_ref[...]
+        sea_out[0] = other_ref[fields:]
+        sea_out[1] = made_ref[fields:]
 
 
 def weights_kernel(se_ref, sx_ref, ae_ref, am_ref, ax_ref, se_out, sx_out, ae_out, am_out, ax_out):
@@ -255,14 +294,15 @@
             source[a, b].astype(jnp.float32).T for a in range(3) for b in range(3)
         ]
         target[...] = jnp.concatenate(taps, axis=1).astype(jnp.bfloat16)
-    for source, target in ((sx_ref, sx_out), (am_ref, am_out), (ax_ref, ax_out)):
-        depth, width = source.shape[2:]
+    for source, target, turned in ((sx_ref, sx_out, True), (am_ref, am_out, False), (ax_ref, ax_out, True)):
+        width, depth = source.shape[2:] if turned else source.shape[:1:-1]
         blank = jnp.zeros((width, pad_to(depth, PACKED) - depth), jnp.float32)
         groups = []
         for b in range(3):
             pieces = []
             for a in range(3):
-                pieces += [source[a, b].astype(jnp.float32).T, blank]
+                tap = source[a, b].astype(jnp.float32)
+                pieces += [tap if turned else tap.T, blank]
             groups.append(jnp.concatenate(pieces, axis=1))
         target[...] = jnp.concatenate(groups, axis=0).astype(jnp.bfloat16)
 
@@ -411,30 +451,41 @@
 
     sent = jnp.where(position == 0, atmosphere[1], atmosphere[0])
     got = lax.ppermute(sent, "sec", swap)
+    packed_shape = pltpu.VMEM((kept, (rows + 1) * LANES), bf16)
+    small = pl.CostEstimate(flops=1000000, bytes_accessed=1000000, transcendentals=0)
+    own = pl.pallas_call(
+        pack_own_kernel,
+        out_shape=packed_shape,
+        in_specs=vmem_specs(4),
+        out_specs=vmem_specs(1)[0],
+        scratch_shapes=[pltpu.VMEM((kept, rows, LANES), f32)],
+        cost_estimate=small,
+        name="pack_own",
+    )(atmosphere, ocean_state, fluxes, sea_mask)
     packed = pl.pallas_call(
-        pack_kernel,
-        out_shape=jax.ShapeDtypeStruct((kept, (rows + 1) * LANES), bf16),
-        in_specs=[pl.BlockSpec(memory_space=pltpu.SMEM)] + vmem_specs(5),
+        pack_got_kernel,
+        out_shape=packed_shape,
+        in_specs=vmem_specs(2),
         out_specs=vmem_specs(1)[0],
-        scratch_shapes=[pltpu.VMEM((kept + fields, rows, LANES), f32)],
-        cost_estimate=pl.CostEstimate(flops=100000, bytes_accessed=400000, transcendentals=0),
-        name="pack",
-    )(position.reshape(1), atmosphere, got, ocean_state, fluxes, sea_mask)
+        scratch_shapes=[pltpu.VMEM((fields, rows, LANES), f32)],
+        cost_estimate=small,
+        name="pack_got",
+    )(*in_vmem(own, got))
 
     weights = pl.pallas_call(
         weights_kernel,
         out_shape=(
-            jax.ShapeDtypeStruct((hidden, 9 * sea_entry.shape[2]), bf16),
-            jax.ShapeDtypeStruct((3 * surface, 3 * hidden_rows), bf16),
-            jax.ShapeDtypeStruct((hidden, 9 * air_entry.shape[2]), bf16),
-            jax.ShapeDtypeStruct((3 * hidden, 3 * hidden_rows), bf16),
-            jax.ShapeDtypeStruct((3 * (fields + flux_count), 3 * hidden_rows), bf16),
+            pltpu.VMEM((hidden, 9 * sea_entry.shape[2]), bf16),
+            pltpu.VMEM((3 * surface, 3 * hidden_rows), bf16),
+            pltpu.VMEM((hidden, 9 * air_entry.shape[2]), bf16),
+            pltpu.VMEM((3 * hidden, 3 * hidden_rows), bf16),
+            pltpu.VMEM((3 * (fields + flux_count), 3 * hidden_rows), bf16),
         ),
         in_specs=vmem_specs(5),
         out_specs=tuple(vmem_specs(5)),
         cost_estimate=pl.CostEstimate(flops=1000000, bytes_accessed=4000000, transcendentals=0),
         name="weights",
-    )(sea_entry, sea_exit, air_entry, air_middle, air_exit)
+    )(sea_entry, jnp.swapaxes(sea_exit, 2, 3), air_entry, air_middle, jnp.swapaxes(air_exit, 2, 3))
 
     frame = [None] * blocks
     for index in range(blocks):
@@ -448,7 +499,7 @@
     sizes = (fields, surface, flux_count, hidden, blocks, rows)
     made = pl.pallas_call(
         functools.partial(forecast_kernel, sizes),
-        out_shape=jax.ShapeDtypeStruct((fields + surface, rows, LANES), bf16),
+        out_shape=pltpu.VMEM((fields + surface, rows, LANES), bf16),
         in_specs=vmem_specs(blocks + 5),
         out_specs=vmem_specs(1)[0],
         scratch_shapes=[
@@ -467,15 +518,20 @@
             flops=4000000000, bytes_accessed=3000000, transcendentals=1000000
         ),
         name="forecast",
-    )(*frame, *weights)
+    )(*in_vmem(*frame, *weights))
 
     other = lax.ppermute(made, "sec", swap)
-    first = position == 0
-    low = jnp.where(first, made, other)
-    high = jnp.where(first, other, made)
-    both = jnp.stack([low, high])
-    air_final = jnp.where(first, both[:, :fields], atmosphere)
-    return (air_final, both[:, fields:])
+    return pl.pallas_call(
+        merge_kernel,
+        out_shape=(
+            jax.ShapeDtypeStruct(atmosphere.shape, bf16),
+            jax.ShapeDtypeStruct(ocean_state.shape, bf16),
+        ),
+        in_specs=vmem_specs(3),
+        out_specs=tuple(vmem_specs(2)),
+        cost_estimate=small,
+        name="merge",
+    )(*in_vmem(made, other, atmosphere))
 
 
 def belt_fits(mesh, atmosphere, ocean_state, fluxes, sea_entry, sea_exit):

time: 38.1 us -> 31.1 us (0.82)
  local copies, waits for them, and re-layouts: 3.39 us -> 0.01 us
  Pallas kernels: 15.1 us -> 12.3 us
  other arithmetic: 2.96 us -> 0.83 us
  waiting for transfers between devices: 5.89 us -> 7.23 us
    unnamed x16 -> x2, local copies, waits for them, and re-layouts: 3.39 us -> 0.01 us
    pallas_call x3 -> x5, Pallas kernels: 15.1 us -> 12.3 us  [the longest x1 8.32 us: belt_shards(): pl.pallas_call(functools.partial(forecast_kernel, sizes), out_shape=pltpu...]
    ppermute x3, waiting for transfers between devices: 0.93 us -> 3.65 us  [belt_shards(): frame[index] = lax.ppermute(packed, 'sp', pairs)]
    another operation x2 -> x0, other arithmetic: 1.47 us -> none  [belt_shards(): both = jnp.stack([low, high])]
    ppermute x1, waiting for transfers between devices: 2.07 us -> 0.9 us  [belt_shards(): got = lax.ppermute(sent, 'sec', swap)]
    select_n x1 -> x0, other arithmetic: 0.65 us -> none  [belt_shards(): air_final = jnp.where(first, both[:, :fields], atmosphere)]
  transfers between devices with their start and end apart: 5 -> 5, of which waited for: 3 -> 5; matrix products, arithmetic and copies ran while one was open for 5% -> 0% of each run, Pallas kernels for 8% -> 10%
where the time goes in v3:
time: 31.1 us; the launch traced here: 30.9 us
  Pallas kernels  12.3 us (40%)
  starting transfers between devices  9.83 us (32%)
  waiting for transfers between devices  7.23 us (23%)
  other arithmetic  0.83 us (3%)
  between operations  0.66 us (2%)
    pallas_call x1, Pallas kernels, belt_shards(): pl.pallas_call(functools.partial(forecast_kernel, sizes), out_shape=pltpu...  8.32 us
    ppermute x3, starting transfers between devices, belt_shards(): frame[index] = lax.ppermute(packed, 'sp', pairs)  5.21 us
    ppermute x3, waiting for transfers between devices, belt_shards(): frame[index] = lax.ppermute(packed, 'sp', pairs)  3.65 us
    ppermute x1, starting transfers between devices, belt_shards(): got = lax.ppermute(sent, 'sec', swap)  2.97 us
    ppermute x1, waiting for transfers between devices, belt_shards(): other = lax.ppermute(made, 'sec', swap)  2.68 us
    pallas_call x1, Pallas kernels, belt_shards(): pl.pallas_call(weights_kernel, out_shape=(pltpu.VMEM((hidden, 9 * sea_ent...  2.01 us
    ppermute x1, starting transfers between devices, belt_shards(): other = lax.ppermute(made, 'sec', swap)  1.66 us
    pallas_call x1, Pallas kernels, belt_shards(): pl.pallas_call(pack_own_kernel, out_shape=packed_shape, in_specs=vmem_spe...  1.16 us
  transfers between devices with their start and end apart: 5, of which 5 were waited for; matrix products, arithmetic and copies ran while one was open for 0% of the time, Pallas kernels for 10%

profile of v3, /device:TPU:0, one launch (start us, length us, event | category | flops | bytes accessed | tf_op | source)
XLA Modules:
  0.0 30.9 jit_solution(4681551078935665324)
XLA Ops:
  0.6 0.8 %select_bitcast_fusion = bf16[24,8,128]{2,1,0:T(8,128)(2,1)S(1)} fusion(bf16[2,24,8,128]{3,2,1,0:T(8,128)(2,1)} %air_ref.3, pred[]{:T(512)S(6)} %eq.3), kind=kLoop, calls=%fused_computation | loop fusion | flops 24576 | bytes 147457 | tf_op jit(solution)/shard_map/jit(_where)/select_n | solution.py:452
  1.5 3.0 %collective-permute-start = (bf16[24,8,128]{2,1,0:T(8,128)(2,1)S(1)}, bf16[24,8,128]{2,1,0:T(8,128)(2,1)S(1)}, u32[]{:S(2)}, u32[]{:S(2)}) collective-permute-start(bf16[24,8,128]{2,1,0:T(8,128)(2,1)S(1)} %select_bitcast_fusion), channel_id=1, source_target_pairs={{0,2},{2,0},{1,3},{3,1},{4,6},{6,4},{5,7},{7,5},{8,10},{10,8},{9,1... | collective-permute-start | bytes 147464 | tf_op jit(solution)/shard_map/ppermute | solution.py:453
  4.4 1.2 %pack_own.1.own_ref = bf16[40,1152]{1,0:T(8,128)(2,1)S(1)} custom-call(bf16[2,24,8,128]{3,2,1,0:T(8,128)(2,1)} %air_ref.3, bf16[2,8,8,128]{3,2,1,0:T(8,128)(2,1)} %sea_ref.1, bf16[2,8,8,128]{3,2,1,0:T(8,128)(2,1)} %flux_ref.1, s32[8,128]{1,0:T(8,128)} %mask_ref.1), custom_call_target="tpu_custom_call" | custom-call | flops 1000000 | bytes 1000000 | tf_op jit(solution)/shard_map/pack_own/pallas_call | solution.py:456
  5.6 0.9 %collective-permute-done.got_ref = bf16[24,8,128]{2,1,0:T(8,128)(2,1)S(1)} collective-permute-done((bf16[24,8,128]{2,1,0:T(8,128)(2,1)S(1)}, bf16[24,8,128]{2,1,0:T(8,128)(2,1)S(1)}, u32[]{:S(2)}, u32[]{:S(2)}) %collective-permute-start) | collective-permute-done | bytes 49184 | tf_op jit(solution)/shard_map/ppermute | solution.py:453
  6.5 0.2 pack_got.1.refs_1_
  6.7 3.2 %collective-permute-start.3 = (bf16[40,1152]{1,0:T(8,128)(2,1)S(1)}, bf16[40,1152]{1,0:T(8,128)(2,1)S(1)}, u32[]{:S(2)}, u32[]{:S(2)}) collective-permute-start(bf16[40,1152]{1,0:T(8,128)(2,1)S(1)} %pack_got.1.refs_1_), channel_id=1, source_target_pairs={{0,8},{4,12},{8,0},{12,4},{1,9},{5,13},{9,1},{13,5},{2,10},{6,14},... | collective-permute-start | bytes 276488 | tf_op jit(solution)/shard_map/ppermute | solution.py:497
  9.9 1.3 %collective-permute-start.2 = (bf16[40,1152]{1,0:T(8,128)(2,1)S(1)}, bf16[40,1152]{1,0:T(8,128)(2,1)S(1)}, u32[]{:S(2)}, u32[]{:S(2)}) collective-permute-start(bf16[40,1152]{1,0:T(8,128)(2,1)S(1)} %pack_got.1.refs_1_), channel_id=1, source_target_pairs={{0,12},{4,0},{8,4},{12,8},{1,13},{5,1},{9,5},{13,9},{2,14},{6,2},{... | collective-permute-start | bytes 276488 | tf_op jit(solution)/shard_map/ppermute | solution.py:497
  11.2 0.7 %collective-permute-start.1 = (bf16[40,1152]{1,0:T(8,128)(2,1)S(1)}, bf16[40,1152]{1,0:T(8,128)(2,1)S(1)}, u32[]{:S(2)}, u32[]{:S(2)}) collective-permute-start(bf16[40,1152]{1,0:T(8,128)(2,1)S(1)} %pack_got.1.refs_1_), channel_id=1, source_target_pairs={{0,4},{4,8},{8,12},{12,0},{1,5},{5,9},{9,13},{13,1},{2,6},{6,10},{... | collective-permute-start | bytes 276488 | tf_op jit(solution)/shard_map/ppermute | solution.py:497
  11.9 2.0 %weights.1 = (bf16[136,144]{1,0:T(8,128)(2,1)S(1)}, bf16[24,432]{1,0:T(8,128)(2,1)S(1)}, bf16[136,288]{1,0:T(8,128)(2,1)S(1)}, bf16[408,432]{1,0:T(8,128)(2,1)S(1)}, bf16[96,432]{1,0:T(8,128)(2,1)S(1)}) custom-call(bf16[3,3,16,136]{3,2,1,0:T(8,128)(2,1)} %se_ref.1, bf16[3,3,8,136]{3,2,1,0:T(8,128)(2,1)} %bitcast.5, bf16[3,3,32,136]{3,2,1,0:T(8,128)(2,1)} %ae_ref.1, ...), custom_call_target="tpu_custom_call" | custom-call | flops 1000000 | bytes 4000000 | tf_op jit(solution)/shard_map/weights/pallas_call | solution.py:475
  13.9 0.3 %collective-permute-done.3.refs_3_ = bf16[40,1152]{1,0:T(8,128)(2,1)S(1)} collective-permute-done((bf16[40,1152]{1,0:T(8,128)(2,1)S(1)}, bf16[40,1152]{1,0:T(8,128)(2,1)S(1)}, u32[]{:S(2)}, u32[]{:S(2)}) %collective-permute-start.3) | collective-permute-done | bytes 92192 | tf_op jit(solution)/shard_map/ppermute | solution.py:497
  14.2 1.0 %collective-permute-done.2.refs_2_ = bf16[40,1152]{1,0:T(8,128)(2,1)S(1)} collective-permute-done((bf16[40,1152]{1,0:T(8,128)(2,1)S(1)}, bf16[40,1152]{1,0:T(8,128)(2,1)S(1)}, u32[]{:S(2)}, u32[]{:S(2)}) %collective-permute-start.2) | collective-permute-done | bytes 92192 | tf_op jit(solution)/shard_map/ppermute | solution.py:497
  15.2 2.3 %collective-permute-done.1.refs_0_ = bf16[40,1152]{1,0:T(8,128)(2,1)S(1)} collective-permute-done((bf16[40,1152]{1,0:T(8,128)(2,1)S(1)}, bf16[40,1152]{1,0:T(8,128)(2,1)S(1)}, u32[]{:S(2)}, u32[]{:S(2)}) %collective-permute-start.1) | collective-permute-done | bytes 92192 | tf_op jit(solution)/shard_map/ppermute | solution.py:497
  17.6 0.0 copy-start
  17.6 8.3 %forecast.1.made_ref = bf16[32,8,128]{2,1,0:T(8,128)(2,1)S(1)} custom-call(bf16[40,1152]{1,0:T(8,128)(2,1)S(1)} %collective-permute-done.1.refs_0_, bf16[40,1152]{1,0:T(8,128)(2,1)S(1)} %pack_got.1.refs_1_, bf16[40,1152]{1,0:T(8,128)(2,1)S(1)} %collective-permute-done.2.refs_2_, bf16[40,1152]{1,0:T(8,128)(2,1)S(1)} %collective-permute-done.3.refs_3_, ...), custom_call_target="tpu_custom_call" | custom-call | flops 4000000000 | bytes 3000000 | tf_op jit(solution)/shard_map/forecast/pallas_call | solution.py:500
  25.9 1.7 %collective-permute-start.4 = (bf16[32,8,128]{2,1,0:T(8,128)(2,1)S(1)}, bf16[32,8,128]{2,1,0:T(8,128)(2,1)S(1)}, u32[]{:S(2)}, u32[]{:S(2)}) collective-permute-start(bf16[32,8,128]{2,1,0:T(8,128)(2,1)S(1)} %forecast.1.made_ref), channel_id=1, source_target_pairs={{0,2},{2,0},{1,3},{3,1},{4,6},{6,4},{5,7},{7,5},{8,10},{10,8},{9,1... | collective-permute-start | bytes 196616 | tf_op jit(solution)/shard_map/ppermute | solution.py:523
  27.5 2.7 %collective-permute-done.4.other_ref = bf16[32,8,128]{2,1,0:T(8,128)(2,1)S(1)} collective-permute-done((bf16[32,8,128]{2,1,0:T(8,128)(2,1)S(1)}, bf16[32,8,128]{2,1,0:T(8,128)(2,1)S(1)}, u32[]{:S(2)}, u32[]{:S(2)}) %collective-permute-start.4) | collective-permute-done | bytes 65568 | tf_op jit(solution)/shard_map/ppermute | solution.py:523
  30.2 0.0 copy-done
  30.2 0.7 %merge.1 = (bf16[2,24,8,128]{3,2,1,0:T(8,128)(2,1)}, bf16[2,8,8,128]{3,2,1,0:T(8,128)(2,1)}) custom-call(bf16[32,8,128]{2,1,0:T(8,128)(2,1)S(1)} %forecast.1.made_ref, bf16[32,8,128]{2,1,0:T(8,128)(2,1)S(1)} %collective-permute-done.4.other_ref, bf16[2,24,8,128]{3,2,1,0:T(8,128)(2,1)S(1)} %copy-done), custom_call_target="tpu_custom_call" | custom-call | flops 1000000 | bytes 1000000 | tf_op jit(solution)/shard_map/merge/pallas_call | solution.py:524
Async XLA Ops:
  1.5 5.0 %collective-permute-start = (bf16[24,8,128]{2,1,0:T(8,128)(2,1)S(1)}, bf16[24,8,128]{2,1,0:T(8,128)(2,1)S(1)}, u32[]{:S(2)}, u32[]{:S(2)}) collective-permute-start(bf16[24,8,128]{2,1,0:T(8,128)(2,1)S(1)} %select_bitcast_fusion), channel_id=1, source_target_pairs={{0,2},{2,0},{1,3},{3,1},{4,6},{6,4},{5,7},{7,5},{8,10},{10,8},{9,1... | collective-permute-start | bytes 147464 | tf_op jit(solution)/shard_map/ppermute | solution.py:453
  6.7 7.6 %collective-permute-start.3 = (bf16[40,1152]{1,0:T(8,128)(2,1)S(1)}, bf16[40,1152]{1,0:T(8,128)(2,1)S(1)}, u32[]{:S(2)}, u32[]{:S(2)}) collective-permute-start(bf16[40,1152]{1,0:T(8,128)(2,1)S(1)} %pack_got.1.refs_1_), channel_id=1, source_target_pairs={{0,8},{4,12},{8,0},{12,4},{1,9},{5,13},{9,1},{13,5},{2,10},{6,14},... | collective-permute-start | bytes 276488 | tf_op jit(solution)/shard_map/ppermute | solution.py:497
  9.9 5.4 %collective-permute-start.2 = (bf16[40,1152]{1,0:T(8,128)(2,1)S(1)}, bf16[40,1152]{1,0:T(8,128)(2,1)S(1)}, u32[]{:S(2)}, u32[]{:S(2)}) collective-permute-start(bf16[40,1152]{1,0:T(8,128)(2,1)S(1)} %pack_got.1.refs_1_), channel_id=1, source_target_pairs={{0,12},{4,0},{8,4},{12,8},{1,13},{5,1},{9,5},{13,9},{2,14},{6,2},{... | collective-permute-start | bytes 276488 | tf_op jit(solution)/shard_map/ppermute | solution.py:497
  11.2 6.3 %collective-permute-start.1 = (bf16[40,1152]{1,0:T(8,128)(2,1)S(1)}, bf16[40,1152]{1,0:T(8,128)(2,1)S(1)}, u32[]{:S(2)}, u32[]{:S(2)}) collective-permute-start(bf16[40,1152]{1,0:T(8,128)(2,1)S(1)} %pack_got.1.refs_1_), channel_id=1, source_target_pairs={{0,4},{4,8},{8,12},{12,0},{1,5},{5,9},{9,13},{13,1},{2,6},{6,10},{... | collective-permute-start | bytes 276488 | tf_op jit(solution)/shard_map/ppermute | solution.py:497
  17.6 12.7 %copy-start = (bf16[2,24,8,128]{3,2,1,0:T(8,128)(2,1)S(1)}, bf16[2,24,8,128]{3,2,1,0:T(8,128)(2,1)}, u32[]{:S(2)}) copy-start(bf16[2,24,8,128]{3,2,1,0:T(8,128)(2,1)} %air_ref.3) | copy-start | bytes 294916
  25.9 4.3 %collective-permute-start.4 = (bf16[32,8,128]{2,1,0:T(8,128)(2,1)S(1)}, bf16[32,8,128]{2,1,0:T(8,128)(2,1)S(1)}, u32[]{:S(2)}, u32[]{:S(2)}) collective-permute-start(bf16[32,8,128]{2,1,0:T(8,128)(2,1)S(1)} %forecast.1.made_ref), channel_id=1, source_target_pairs={{0,2},{2,0},{1,3},{3,1},{4,6},{6,4},{5,7},{7,5},{8,10},{10,8},{9,1... | collective-permute-start | bytes 196616 | tf_op jit(solution)/shard_map/ppermute | solution.py:523

commit v4 on v3

--- a/solution.py
+++ b/solution.py
@@ -196,10 +196,9 @@
     return total
 
 
-def gelu(v):
+def twice_gelu(v):
     inner = v * (0.7978845608028654 + (0.7978845608028654 * 0.044715) * (v * v))
-    half = 0.5 * v
-    return half + half * jnp.tanh(inner)
+    return v + v * jnp.tanh(inner)
 
 
 def lane_ids(rows):
@@ -301,60 +300,116 @@
         for b in range(3):
             pieces = []
             for a in range(3):
-                tap = source[a, b].astype(jnp.float32)
+                tap = 0.5 * source[a, b].astype(jnp.float32)
                 pieces += [tap if turned else tap.T, blank]
             groups.append(jnp.concatenate(pieces, axis=1))
         target[...] = jnp.concatenate(groups, axis=0).astype(jnp.bfloat16)
 
 
-def forecast_kernel(sizes, *refs):
+def ordered(tasks, ring, lag, stage):
+    depends = []
+    late = []
+    writer, readers = {}, {}
+    for index, (_, reads, writes, _) in enumerate(tasks):
+        needed = set()
+        reads = [(name, row % ring) for name, row in reads]
+        writes = [(name, row % ring) for name, row in writes]
+        for cell in reads:
+            if cell in writer:
+                needed.add(writer[cell])
+        for cell in writes:
+            needed.update(readers.pop(cell, ()))
+            if cell in writer:
+                needed.add(writer[cell])
+        for cell in reads:
+            readers.setdefault(cell, set()).add(index)
+        for cell in writes:
+            writer[cell] = index
+        needed.discard(index)
+        depends.append(needed)
+        late.append(tasks[index][0] == FAR_LOAD or any(late[i] for i in needed))
+    chosen_stage = [i for i in range(len(tasks)) if late[i] == bool(stage)]
+    placed = {i: -lag for i in range(len(tasks)) if stage and not late[i]}
+    order = []
+    while len(order) < len(chosen_stage):
+        ready = [i for i in chosen_stage if i not in placed and all(j in placed for j in depends[i])]
+        rested = [i for i in ready if all(placed[j] + lag <= len(order) for j in depends[i])]
+        if rested:
+            chosen = max(rested, key=lambda i: (tasks[i][0], -i))
+        else:
+            chosen = min(ready, key=lambda i: max((placed[j] for j in depends[i]), default=-1))
+        placed[chosen] = len(order)
+        order.append(chosen)
+    return [tasks[i][3] for i in order]
+
+
+CHUNK = 2
+LAG = 20
+NEAR = 3
+NEAR_LOAD = 0
+FAR_LOAD = -1
+HELD = 9
+VMEM_GRANT = 24 * 1024 * 1024
+PADS = {"sea_in": 2, "sea_hid": 2, "air_in": 2, "hid1": 2, "hid2": 4}
+
+
+def forecast_kernel(sizes, stage, *refs):
     fields, surface, flux_count, hidden, blocks, rows = sizes
-    block_refs = refs[:blocks]
-    se_ref, sx_ref, ae_ref, am_ref, ax_ref, out_ref = refs[blocks : blocks + 6]
-    sea_in, sea_hid, air_in, hid1, hid2, air_now, sea_now, edge_in, mask_in, planes = refs[blocks + 6 :]
+    loaded = range(NEAR, blocks) if stage else range(NEAR)
+    block_refs = dict(zip(loaded, refs, strict=False))
+    se_ref, sx_ref, ae_ref, am_ref, ax_ref = refs[len(loaded) : len(loaded) + 5]
+    rest = refs[len(loaded) + 5 :]
+    if stage:
+        out_ref, planes = rest[HELD], rest[-1]
+        rest = rest[HELD + 1 : -1]
+    held = dict(zip(("sea_in", "sea_hid", "air_in", "hid1", "hid2"), rest, strict=False))
+    air_now, sea_now, edge_in, mask_in = rest[5:]
     ring = blocks * rows
     kept = fields + surface + flux_count
-    hidden_pad = sea_hid.shape[0] - hidden
-    pads = {id(sea_in): 1, id(sea_hid): 1, id(air_in): 1, id(hid1): 2, id(hid2): 4}
-
-    def at(buffer, row, count):
-        start = row + pads.get(id(buffer), 0)
-        if isinstance(row, int):
-            return pl.ds(start * LANES, count * LANES)
-        return pl.ds(pl.multiple_of(start * LANES, LANES), count * LANES)
-
-    def close_ring(buffer):
-        pad = pads[id(buffer)]
-        buffer[:, 0 : pad * LANES] = buffer[:, ring * LANES : (ring + pad) * LANES]
-        buffer[:, (ring + pad) * LANES :] = buffer[:, pad * LANES : 2 * pad * LANES]
-
-    def store_sea_in(row, values):
+    hidden_pad = held["sea_hid"].shape[0] - hidden
+
+    def span(row, count):
+        return pl.ds(row * LANES, count * LANES)
+
+    def put(name, row, count, values):
+        row %= ring
+        pad = PADS[name]
+        places = [row]
+        if row < pad:
+            places.append(row + ring)
+        if row + count > ring - pad:
+            places.append(row - ring)
+        for place in places:
+            low, high = max(place, -pad), min(place + count, ring + pad)
+            piece = values[:, (low - place) * LANES : (high - place) * LANES]
+            held[name][:, span(low + pad, high - low)] = piece
+
+    def gather_rows(name, row, count, spread):
+        start = row % ring + PADS[name]
+        return jnp.concatenate(
+            [held[name][:, span(start + spread * (a - 1), count)] for a in range(3)], axis=0
+        )
+
+    def put_sea_in(row, values):
         left, right = from_left(values, 1), from_right(values, 1)
-        sea_in[:, at(sea_in, row, 1)] = jnp.concatenate([left, values, right], axis=0).astype(
-            jnp.bfloat16
-        )
-
-    def store_air_in(row, values, edge):
+        stacked = jnp.concatenate([left, values, right], axis=0).astype(jnp.bfloat16)
+        put("sea_in", row, 1, stacked)
+
+    def put_air_in(row, values, edge):
         fill = jnp.concatenate([edge, jnp.zeros((surface, LANES), jnp.float32)], axis=0)
         left, right = from_left(values, 1), from_right(values, 1, fill)
-        air_in[:, at(air_in, row, 1)] = jnp.concatenate([left, values, right], axis=0).astype(
-            jnp.bfloat16
-        )
-
-    def gather_rows(buffer, row, count, spread):
-        return jnp.concatenate(
-            [buffer[:, at(buffer, row + spread * (a - 1), count)] for a in range(3)], axis=0
-        )
+        stacked = jnp.concatenate([left, values, right], axis=0).astype(jnp.bfloat16)
+        put("air_in", row, 1, stacked)
 
     def product(weight_ref, inputs):
         return jnp.dot(weight_ref[...], inputs, preferred_element_type=jnp.float32)
 
-    def store_hidden(buffer, row, count, values):
-        values = gelu(values)
+    def put_hidden(name, row, count, values):
+        values = twice_gelu(values)
         if hidden_pad:
             blank = jnp.zeros((hidden_pad, values.shape[1]), jnp.float32)
             values = jnp.concatenate([values, blank], axis=0)
-        buffer[:, at(buffer, row, count)] = values.astype(jnp.bfloat16)
+        put(name, row, count, values.astype(jnp.bfloat16))
 
     def side_sum(made, width, spread, index):
         piece = made[:, index * LANES : (index + 1) * LANES]
@@ -362,77 +417,138 @@
         right = from_right(piece[2 * width : 3 * width], spread)
         return piece[width : 2 * width] + left + right
 
-    def over_rows(first, last, count, body):
-        for row in range(first, last, count):
-            body(row)
-
     def sea_entry(row, count):
-        store_hidden(sea_hid, row, count, product(se_ref, gather_rows(sea_in, row, count, 1)))
+        put_hidden("sea_hid", row, count, product(se_ref, gather_rows("sea_in", row, count, 1)))
 
     def sea_exit(row, count):
-        made = product(sx_ref, gather_rows(sea_hid, row, count, 1))
+        made = product(sx_ref, gather_rows("sea_hid", row, count, 1))
         for i in range(count):
+            at = (row + i) % ring
             change = side_sum(made, surface, 1, i)
-            weight = mask_in[pl.ds(row + i, 1), :]
-            old = sea_now[:, at(sea_now, row + i, 1)]
-            new = (old + weight * change).astype(jnp.bfloat16).astype(jnp.float32)
-            sea_now[:, at(sea_now, row + i, 1)] = new
-            air = air_now[:, at(air_now, row + i, 1)]
-            store_air_in(row + i, jnp.concatenate([air, new], axis=0), edge_in[:, at(edge_in, row + i, 1)])
+            old = sea_now[:, span(at, 1)]
+            new = (old + mask_in[at : at + 1, :] * change).astype(jnp.bfloat16).astype(jnp.float32)
+            sea_now[:, span(at, 1)] = new
+            values = jnp.concatenate([air_now[:, span(at, 1)], new], axis=0)
+            put_air_in(at, values, edge_in[:, span(at, 1)])
 
     def air_entry(row, count):
-        store_hidden(hid1, row, count, product(ae_ref, gather_rows(air_in, row, count, 1)))
+        put_hidden("hid1", row, count, product(ae_ref, gather_rows("air_in", row, count, 1)))
 
     def air_middle(row, count):
-        made = product(am_ref, gather_rows(hid1, row, count, 2))
+        made = product(am_ref, gather_rows("hid1", row, count, 2))
         sums = [side_sum(made, hidden, 2, i) for i in range(count)]
-        store_hidden(hid2, row, count, jnp.concatenate(sums, axis=1))
+        put_hidden("hid2", row, count, jnp.concatenate(sums, axis=1))
 
     def air_exit(row, count, last):
-        made = product(ax_ref, gather_rows(hid2, row, count, 4))
+        made = product(ax_ref, gather_rows("hid2", row, count, 4))
         for i in range(count):
+            at = (row + i) % ring
             change = side_sum(made, fields + flux_count, 4, i)
-            old = air_now[:, at(air_now, row + i, 1)]
+            old = air_now[:, span(at, 1)]
             new = (old + change[0:fields]).astype(jnp.bfloat16).astype(jnp.float32)
-            sea = sea_now[:, at(sea_now, row + i, 1)]
+            sea = sea_now[:, span(at, 1)]
             if last:
-                planes[:, row + i - rows, :] = jnp.concatenate([new, sea], axis=0)
+                planes[:, at - rows, :] = jnp.concatenate([new, sea], axis=0)
             else:
-                air_now[:, at(air_now, row + i, 1)] = new
+                air_now[:, span(at, 1)] = new
                 flux = change[fields:].astype(jnp.bfloat16).astype(jnp.float32)
-                store_sea_in(row + i, jnp.concatenate([sea, flux], axis=0))
-
-    for block, source in enumerate(block_refs):
-        tail = source[:, rows * LANES : (rows + 1) * LANES].astype(jnp.float32)
-        mask_in[block * rows : (block + 1) * rows, :] = tail[fields : fields + rows]
-        for i in range(rows):
-            row = block * rows + i
+                put_sea_in(at, jnp.concatenate([sea, flux], axis=0))
+
+    def load_rows(block, row, count):
+        source = block_refs[block]
+        for i in range(row, row + count):
             values = source[:, i * LANES : (i + 1) * LANES].astype(jnp.float32)
-            air_now[:, at(air_now, row, 1)] = values[0:fields]
-            sea_now[:, at(sea_now, row, 1)] = values[fields : fields + surface]
-            store_sea_in(row, values[fields:kept])
-            edge = jnp.broadcast_to(tail[0:fields, i : i + 1], (fields, LANES))
-            edge_in[:, at(edge_in, row, 1)] = edge
-    close_ring(sea_in)
-
-    over_rows(0, ring, 2, lambda r: sea_entry(r, 2))
-    close_ring(sea_hid)
-    over_rows(0, ring, 2, lambda r: sea_exit(r, 2))
-    close_ring(air_in)
-    over_rows(0, ring, 2, lambda r: air_entry(r, 2))
-    close_ring(hid1)
-    over_rows(0, ring, 2, lambda r: air_middle(r, 2))
-    close_ring(hid2)
-    over_rows(0, ring, 2, lambda r: air_exit(r, 2, False))
-    close_ring(sea_in)
-
-    over_rows(rows - 8, 2 * rows + 8, 2, lambda r: sea_entry(r, 2))
-    over_rows(rows - 7, 2 * rows + 7, 2, lambda r: sea_exit(r, 2))
-    over_rows(rows - 6, 2 * rows + 6, 2, lambda r: air_entry(r, 2))
-    over_rows(rows - 4, 2 * rows + 4, 2, lambda r: air_middle(r, 2))
-    for r in range(rows, 2 * rows, 2):
-        air_exit(r, 2, True)
-    out_ref[...] = planes[...].astype(jnp.bfloat16)
+            at = block * rows + i
+            air_now[:, span(at, 1)] = values[0:fields]
+            sea_now[:, span(at, 1)] = values[fields : fields + surface]
+            put_sea_in(at, values[fields:kept])
+            tail = source[0:fields, rows * LANES : (rows + 1) * LANES].astype(jnp.float32)
+            edge_in[:, span(at, 1)] = jnp.broadcast_to(tail[:, i : i + 1], (fields, LANES))
+
+    for block, source in block_refs.items():
+        tail = source[fields : fields + rows, rows * LANES : (rows + 1) * LANES]
+        mask_in[block * rows : (block + 1) * rows, :] = tail.astype(jnp.float32)
+
+    tasks = []
+
+    def add(depth, first, last, body, reads, writes, spread):
+        for row in range(first, last, CHUNK):
+            seen = range(row - spread, row + CHUNK + spread)
+            near = range(row, row + CHUNK)
+            tasks.append(
+                (
+                    depth,
+                    [(name, r) for name in reads for r in (near if name.endswith("now") else seen)],
+                    [(name, r) for name in writes for r in near],
+                    functools.partial(body, row, CHUNK),
+                )
+            )
+
+    for block in range(blocks):
+        for row in range(0, rows, CHUNK):
+            near = range(block * rows + row, block * rows + row + CHUNK)
+            writes = [(name, r) for name in ("sea_in", "air_now", "sea_now") for r in near]
+            depth = NEAR_LOAD if block < NEAR else FAR_LOAD
+            tasks.append((depth, [], writes, functools.partial(load_rows, block, row, CHUNK)))
+    for step in range(STEPS):
+        last = step == STEPS - 1
+        base = 10 * step
+
+        def reach(halo, last=last):
+            return (rows - halo, 2 * rows + halo) if last else (0, ring)
+
+        add(base + 1, *reach(8), sea_entry, ("sea_in",), ("sea_hid",), 1)
+        add(base + 2, *reach(7), sea_exit, ("sea_hid", "sea_now", "air_now"), ("sea_now", "air_in"), 1)
+        add(base + 3, *reach(6), air_entry, ("air_in",), ("hid1",), 1)
+        add(base + 4, *reach(4), air_middle, ("hid1",), ("hid2",), 2)
+        low, high = (rows, 2 * rows) if last else (rows - 10, 2 * rows + 10)
+        writes = ("planes",) if last else ("air_now", "sea_in")
+        body = functools.partial(air_exit, last=last)
+        add(base + 5, low, high, body, ("hid2", "air_now", "sea_now"), writes, 4)
+    for task in ordered(tasks, ring, LAG, stage):
+        task()
+    if stage:
+        out_ref[...] = planes[...].astype(jnp.bfloat16)
+
+
+def forecast(sizes, frame, weights):
+    fields, surface, flux_count, hidden, blocks, rows = sizes
+    ring = blocks * rows
+    hidden_rows = pad_to(hidden, PACKED)
+    held = []
+    for name, depth in (
+        ("sea_in", 3 * (surface + flux_count)),
+        ("sea_hid", hidden_rows),
+        ("air_in", 3 * (fields + surface)),
+        ("hid1", hidden_rows),
+        ("hid2", hidden_rows),
+    ):
+        held.append(pltpu.VMEM((depth, (ring + 2 * PADS[name]) * LANES), jnp.bfloat16))
+    for depth in (fields, surface, fields):
+        held.append(pltpu.VMEM((depth, ring * LANES), jnp.float32))
+    held.append(pltpu.VMEM((ring, LANES), jnp.float32))
+    cost = pl.CostEstimate(flops=2000000000, bytes_accessed=3000000, transcendentals=1000000)
+    state = pl.pallas_call(
+        functools.partial(forecast_kernel, sizes, 0),
+        out_shape=tuple(held),
+        in_specs=vmem_specs(NEAR + 5),
+        out_specs=tuple(vmem_specs(HELD)),
+        cost_estimate=pl.CostEstimate(flops=1000, bytes_accessed=1000, transcendentals=0),
+        compiler_params=pltpu.CompilerParams(vmem_limit_bytes=VMEM_GRANT),
+        name="forecast_near",
+    )(*in_vmem(*frame[:NEAR], *weights))
+    far = blocks - NEAR
+    return pl.pallas_call(
+        functools.partial(forecast_kernel, sizes, 1),
+        out_shape=(pltpu.VMEM((fields + surface, rows, LANES), jnp.bfloat16), *held),
+        in_specs=vmem_specs(far + 5 + HELD),
+        out_specs=tuple(vmem_specs(1 + HELD)),
+        scratch_shapes=[pltpu.VMEM((fields + surface, rows, LANES), jnp.float32)],
+        input_output_aliases={far + 5 + i: 1 + i for i in range(HELD)},
+        cost_estimate=cost,
+        compiler_params=pltpu.CompilerParams(vmem_limit_bytes=VMEM_GRANT),
+        name="forecast_far",
+    )(*in_vmem(*frame[NEAR:], *weights, *state))[0]
 
 
 def belt_shards(
@@ -445,7 +561,6 @@
     hidden = air_middle.shape[3]
     hidden_rows = pad_to(hidden, PACKED)
     kept = fields + surface + flux_count
-    ring = blocks * rows
     swap = [(0, 1), (1, 0)]
     bf16, f32 = jnp.bfloat16, jnp.float32
 
@@ -497,29 +612,7 @@
             frame[index] = lax.ppermute(packed, "sp", pairs)
 
     sizes = (fields, surface, flux_count, hidden, blocks, rows)
-    made = pl.pallas_call(
-        functools.partial(forecast_kernel, sizes),
-        out_shape=pltpu.VMEM((fields + surface, rows, LANES), bf16),
-        in_specs=vmem_specs(blocks + 5),
-        out_specs=vmem_specs(1)[0],
-        scratch_shapes=[
-            pltpu.VMEM((3 * (surface + flux_count), (ring + 2) * LANES), bf16),
-            pltpu.VMEM((hidden_rows, (ring + 2) * LANES), bf16),
-            pltpu.VMEM((3 * (fields + surface), (ring + 2) * LANES), bf16),
-            pltpu.VMEM((hidden_rows, (ring + 4) * LANES), bf16),
-            pltpu.VMEM((hidden_rows, (ring + 8) * LANES), bf16),
-            pltpu.VMEM((fields, ring * LANES), f32),
-            pltpu.VMEM((surface, ring * LANES), f32),
-            pltpu.VMEM((fields, ring * LANES), f32),
-            pltpu.VMEM((ring, LANES), f32),
-            pltpu.VMEM((fields + surface, rows, LANES), f32),
-        ],
-        cost_estimate=pl.CostEstimate(
-            flops=4000000000, bytes_accessed=3000000, transcendentals=1000000
-        ),
-        name="forecast",
-    )(*in_vmem(*frame, *weights))
-
+    made = forecast(sizes, frame, weights)
     other = lax.ppermute(made, "sec", swap)
     return pl.pallas_call(
         merge_kernel,
@@ -540,7 +633,6 @@
     rows = atmosphere.shape[2] // blocks
     band = atmosphere.shape[3] // sections
     fields, surface, flux_count = atmosphere.shape[1], ocean_state.shape[1], fluxes.shape[1]
-    halo = 9
     return (
         sections == 2
         and members == 2
@@ -548,9 +640,9 @@
         and ocean_state.shape[3] == band
         and rows % SUBLANES == 0
         and rows <= LANES
-        and rows >= halo - 1
-        and blocks > 1
-        and 2 * rows + halo <= blocks * rows
+        and rows >= 8
+        and blocks > NEAR
+        and 2 * rows + 10 <= blocks * rows
         and blocks * rows <= 64
         and rows <= surface + flux_count
         and all(c % SUBLANES == 0 for c in (fields, surface, flux_count, sea_entry.shape[3]))

time: 31.1 us -> 30.7 us (0.987)
    ppermute x3, waiting for transfers between devices: 3.65 us -> 3.31 us  [belt_shards(): frame[index] = lax.ppermute(packed, 'sp', pairs)]
    pallas_call x1 -> x2, Pallas kernels: 8.32 us -> 8.19 us  [the longest x1 6.25 us: forecast(): pl.pallas_call(functools.partial(forecast_kernel, sizes, 1), out_shape=(p...]
  transfers between devices with their start and end apart: 5 -> 5, of which waited for: 5 -> 3; matrix products, arithmetic and copies ran while one was open for 0% -> 0% of each run, Pallas kernels for 10% -> 17%
where the time goes in v4:
time: 30.7 us; the launch traced here: 30.4 us
  Pallas kernels  12.2 us (40%)
  starting transfers between devices  9.72 us (32%)
  waiting for transfers between devices  6.99 us (23%)
  other arithmetic  0.83 us (3%)
  between operations  0.69 us (2%)
    pallas_call x1, Pallas kernels, forecast(): pl.pallas_call(functools.partial(forecast_kernel, sizes, 1), out_shape=(p...  6.25 us
    ppermute x3, starting transfers between devices, belt_shards(): frame[index] = lax.ppermute(packed, 'sp', pairs)  5.2 us
    ppermute x3, waiting for transfers between devices, belt_shards(): frame[index] = lax.ppermute(packed, 'sp', pairs)  3.31 us
    ppermute x1, starting transfers between devices, belt_shards(): got = lax.ppermute(sent, 'sec', swap)  2.97 us
    ppermute x1, waiting for transfers between devices, belt_shards(): other = lax.ppermute(made, 'sec', swap)  2.77 us
    pallas_call x1, Pallas kernels, belt_shards(): pl.pallas_call(weights_kernel, out_shape=(pltpu.VMEM((hidden, 9 * sea_ent...  2.01 us
    pallas_call x1, Pallas kernels, forecast(): pl.pallas_call(functools.partial(forecast_kernel, sizes, 0), out_shape=tu...  1.94 us
    ppermute x1, starting transfers between devices, belt_shards(): other = lax.ppermute(made, 'sec', swap)  1.56 us
  transfers between devices with their start and end apart: 5, of which 3 were waited for; matrix products, arithmetic and copies ran while one was open for 0% of the time, Pallas kernels for 17%

profile of v4, /device:TPU:0, one launch (start us, length us, event | category | flops | bytes accessed | tf_op | source)
XLA Modules:
  0.0 30.4 jit_solution(16853226101254282643)
XLA Ops:
  0.6 0.8 %select_bitcast_fusion = bf16[24,8,128]{2,1,0:T(8,128)(2,1)S(1)} fusion(bf16[2,24,8,128]{3,2,1,0:T(8,128)(2,1)} %air_ref.3, pred[]{:T(512)S(6)} %eq.3), kind=kLoop, calls=%fused_computation | loop fusion | flops 24576 | bytes 147457 | tf_op jit(solution)/shard_map/jit(_where)/select_n | solution.py:567
  1.5 3.0 %collective-permute-start = (bf16[24,8,128]{2,1,0:T(8,128)(2,1)S(1)}, bf16[24,8,128]{2,1,0:T(8,128)(2,1)S(1)}, u32[]{:S(2)}, u32[]{:S(2)}) collective-permute-start(bf16[24,8,128]{2,1,0:T(8,128)(2,1)S(1)} %select_bitcast_fusion), channel_id=1, source_target_pairs={{0,2},{2,0},{1,3},{3,1},{4,6},{6,4},{5,7},{7,5},{8,10},{10,8},{9,1... | collective-permute-start | bytes 147464 | tf_op jit(solution)/shard_map/ppermute | solution.py:568
  4.4 1.2 %pack_own.1.own_ref = bf16[40,1152]{1,0:T(8,128)(2,1)S(1)} custom-call(bf16[2,24,8,128]{3,2,1,0:T(8,128)(2,1)} %air_ref.3, bf16[2,8,8,128]{3,2,1,0:T(8,128)(2,1)} %sea_ref.1, bf16[2,8,8,128]{3,2,1,0:T(8,128)(2,1)} %flux_ref.1, s32[8,128]{1,0:T(8,128)} %mask_ref.1), custom_call_target="tpu_custom_call" | custom-call | flops 1000000 | bytes 1000000 | tf_op jit(solution)/shard_map/pack_own/pallas_call | solution.py:571
  5.6 0.9 %collective-permute-done.got_ref = bf16[24,8,128]{2,1,0:T(8,128)(2,1)S(1)} collective-permute-done((bf16[24,8,128]{2,1,0:T(8,128)(2,1)S(1)}, bf16[24,8,128]{2,1,0:T(8,128)(2,1)S(1)}, u32[]{:S(2)}, u32[]{:S(2)}) %collective-permute-start) | collective-permute-done | bytes 49184 | tf_op jit(solution)/shard_map/ppermute | solution.py:568
  6.5 0.2 pack_got.1.refs_1_
  6.7 4.2 %collective-permute-start.3 = (bf16[40,1152]{1,0:T(8,128)(2,1)S(1)}, bf16[40,1152]{1,0:T(8,128)(2,1)S(1)}, u32[]{:S(2)}, u32[]{:S(2)}) collective-permute-start(bf16[40,1152]{1,0:T(8,128)(2,1)S(1)} %pack_got.1.refs_1_), channel_id=1, source_target_pairs={{0,12},{4,0},{8,4},{12,8},{1,13},{5,1},{9,5},{13,9},{2,14},{6,2},{... | collective-permute-start | bytes 276488 | tf_op jit(solution)/shard_map/ppermute | solution.py:612
  10.9 0.0 collective-permute-start.2
  10.9 1.0 %collective-permute-start.1 = (bf16[40,1152]{1,0:T(8,128)(2,1)S(1)}, bf16[40,1152]{1,0:T(8,128)(2,1)S(1)}, u32[]{:S(2)}, u32[]{:S(2)}) collective-permute-start(bf16[40,1152]{1,0:T(8,128)(2,1)S(1)} %pack_got.1.refs_1_), channel_id=1, source_target_pairs={{0,8},{4,12},{8,0},{12,4},{1,9},{5,13},{9,1},{13,5},{2,10},{6,14},... | collective-permute-start | bytes 276488 | tf_op jit(solution)/shard_map/ppermute | solution.py:612
  11.9 2.0 %weights.1 = (bf16[136,144]{1,0:T(8,128)(2,1)S(1)}, bf16[24,432]{1,0:T(8,128)(2,1)S(1)}, bf16[136,288]{1,0:T(8,128)(2,1)S(1)}, bf16[408,432]{1,0:T(8,128)(2,1)S(1)}, bf16[96,432]{1,0:T(8,128)(2,1)S(1)}) custom-call(bf16[3,3,16,136]{3,2,1,0:T(8,128)(2,1)} %se_ref.1, bf16[3,3,8,136]{3,2,1,0:T(8,128)(2,1)} %bitcast.5, bf16[3,3,32,136]{3,2,1,0:T(8,128)(2,1)} %ae_ref.1, ...), custom_call_target="tpu_custom_call" | custom-call | flops 1000000 | bytes 4000000 | tf_op jit(solution)/shard_map/weights/pallas_call | solution.py:590
  13.9 0.0 collective-permute-done.3.refs_2_
  13.9 3.3 %collective-permute-done.2.refs_0_ = bf16[40,1152]{1,0:T(8,128)(2,1)S(1)} collective-permute-done((bf16[40,1152]{1,0:T(8,128)(2,1)S(1)}, bf16[40,1152]{1,0:T(8,128)(2,1)S(1)}, u32[]{:S(2)}, u32[]{:S(2)}) %collective-permute-start.2) | collective-permute-done | bytes 92192 | tf_op jit(solution)/shard_map/ppermute | solution.py:612
  17.2 1.9 %forecast_near.1 = (bf16[48,4608]{1,0:T(8,128)(2,1)S(1)}, bf16[144,4608]{1,0:T(8,128)(2,1)S(1)}, bf16[96,4608]{1,0:T(8,128)(2,1)S(1)}, bf16[144,4608]{1,0:T(8,12...) custom-call(bf16[40,1152]{1,0:T(8,128)(2,1)S(1)} %collective-permute, ...), custom_call_target="tpu_custom_call" | custom-call | flops 1000 | bytes 1000 | tf_op jit(solution)/shard_map/forecast_near/pallas_call | solution.py:531
  19.2 0.0 collective-permute-done.1.refs_0_
  19.2 0.0 copy-start
  19.2 6.2 %forecast_far.1 = (bf16[32,8,128]{2,1,0:T(8,128)(2,1)S(1)}, bf16[48,4608]{1,0:T(8,128)(2,1)S(1)}, bf16[144,4608]{1,0:T(8,128)(2,1)S(1)}, bf16[96,4608]{1,0:T(8,1...) custom-call(bf16[40,1152]{1,0:T(8,128)(2,1)S(1)} %collective-permute, ...), custom_call_target="tpu_custom_call", output_to_operand_aliasing={{1}: (6, {}), {2}: (7, {}), {3}: (8, {}), {4}: (9, {}), {5}... | custom-call | flops 2000000000 | bytes 3000000 | tf_op jit(solution)/shard_map/forecast_far/pallas_call | solution.py:541
  25.4 1.6 %collective-permute-start.4 = (bf16[32,8,128]{2,1,0:T(8,128)(2,1)S(1)}, bf16[32,8,128]{2,1,0:T(8,128)(2,1)S(1)}, u32[]{:S(2)}, u32[]{:S(2)}) collective-permute-start(bf16[32,8,128]{2,1,0:T(8,128)(2,1)S(1)} %get-tuple-element.31.made_ref), channel_id=1, source_target_pairs={{0,2},{2,0},{1,3},{3,1},{4,6},{6,4},{5,7},{7,5},{8,10},{10,8},{9,1... | collective-permute-start | bytes 196616 | tf_op jit(solution)/shard_map/ppermute | solution.py:616
  27.0 2.8 %collective-permute-done.4.other_ref = bf16[32,8,128]{2,1,0:T(8,128)(2,1)S(1)} collective-permute-done((bf16[32,8,128]{2,1,0:T(8,128)(2,1)S(1)}, bf16[32,8,128]{2,1,0:T(8,128)(2,1)S(1)}, u32[]{:S(2)}, u32[]{:S(2)}) %collective-permute-start.4) | collective-permute-done | bytes 65568 | tf_op jit(solution)/shard_map/ppermute | solution.py:616
  29.8 0.0 copy-done
  29.8 0.7 %merge.1 = (bf16[2,24,8,128]{3,2,1,0:T(8,128)(2,1)}, bf16[2,8,8,128]{3,2,1,0:T(8,128)(2,1)}) custom-call(bf16[32,8,128]{2,1,0:T(8,128)(2,1)S(1)} %get-tuple-element.31.made_ref, bf16[32,8,128]{2,1,0:T(8,128)(2,1)S(1)} %collective-permute-done.4.other_ref, bf16[2,24,8,128]{3,2,1,0:T(8,128)(2,1)S(1)} %copy-done), custom_call_target="tpu_custom_call" | custom-call | flops 1000000 | bytes 1000000 | tf_op jit(solution)/shard_map/merge/pallas_call | solution.py:617
Async XLA Ops:
  1.5 5.0 %collective-permute-start = (bf16[24,8,128]{2,1,0:T(8,128)(2,1)S(1)}, bf16[24,8,128]{2,1,0:T(8,128)(2,1)S(1)}, u32[]{:S(2)}, u32[]{:S(2)}) collective-permute-start(bf16[24,8,128]{2,1,0:T(8,128)(2,1)S(1)} %select_bitcast_fusion), channel_id=1, source_target_pairs={{0,2},{2,0},{1,3},{3,1},{4,6},{6,4},{5,7},{7,5},{8,10},{10,8},{9,1... | collective-permute-start | bytes 147464 | tf_op jit(solution)/shard_map/ppermute | solution.py:568
  6.7 7.2 %collective-permute-start.3 = (bf16[40,1152]{1,0:T(8,128)(2,1)S(1)}, bf16[40,1152]{1,0:T(8,128)(2,1)S(1)}, u32[]{:S(2)}, u32[]{:S(2)}) collective-permute-start(bf16[40,1152]{1,0:T(8,128)(2,1)S(1)} %pack_got.1.refs_1_), channel_id=1, source_target_pairs={{0,12},{4,0},{8,4},{12,8},{1,13},{5,1},{9,5},{13,9},{2,14},{6,2},{... | collective-permute-start | bytes 276488 | tf_op jit(solution)/shard_map/ppermute | solution.py:612
  10.9 6.4 %collective-permute-start.2 = (bf16[40,1152]{1,0:T(8,128)(2,1)S(1)}, bf16[40,1152]{1,0:T(8,128)(2,1)S(1)}, u32[]{:S(2)}, u32[]{:S(2)}) collective-permute-start(bf16[40,1152]{1,0:T(8,128)(2,1)S(1)} %pack_got.1.refs_1_), channel_id=1, source_target_pairs={{0,4},{4,8},{8,12},{12,0},{1,5},{5,9},{9,13},{13,1},{2,6},{6,10},{... | collective-permute-start | bytes 276488 | tf_op jit(solution)/shard_map/ppermute | solution.py:612
  10.9 8.3 %collective-permute-start.1 = (bf16[40,1152]{1,0:T(8,128)(2,1)S(1)}, bf16[40,1152]{1,0:T(8,128)(2,1)S(1)}, u32[]{:S(2)}, u32[]{:S(2)}) collective-permute-start(bf16[40,1152]{1,0:T(8,128)(2,1)S(1)} %pack_got.1.refs_1_), channel_id=1, source_target_pairs={{0,8},{4,12},{8,0},{12,4},{1,9},{5,13},{9,1},{13,5},{2,10},{6,14},... | collective-permute-start | bytes 276488 | tf_op jit(solution)/shard_map/ppermute | solution.py:612
  19.2 10.6 %copy-start = (bf16[2,24,8,128]{3,2,1,0:T(8,128)(2,1)S(1)}, bf16[2,24,8,128]{3,2,1,0:T(8,128)(2,1)}, u32[]{:S(2)}) copy-start(bf16[2,24,8,128]{3,2,1,0:T(8,128)(2,1)} %air_ref.3) | copy-start | bytes 294916
  25.4 4.3 %collective-permute-start.4 = (bf16[32,8,128]{2,1,0:T(8,128)(2,1)S(1)}, bf16[32,8,128]{2,1,0:T(8,128)(2,1)S(1)}, u32[]{:S(2)}, u32[]{:S(2)}) collective-permute-start(bf16[32,8,128]{2,1,0:T(8,128)(2,1)S(1)} %get-tuple-element.31.made_ref), channel_id=1, source_target_pairs={{0,2},{2,0},{1,3},{3,1},{4,6},{6,4},{5,7},{7,5},{8,10},{10,8},{9,1... | collective-permute-start | bytes 196616 | tf_op jit(solution)/shard_map/ppermute | solution.py:616

commit v5 on v4

--- a/solution.py
+++ b/solution.py
@@ -327,7 +327,7 @@
             writer[cell] = index
         needed.discard(index)
         depends.append(needed)
-        late.append(tasks[index][0] == FAR_LOAD or any(late[i] for i in needed))
+        late.append(tasks[index][0] == LATE_LOAD or any(late[i] for i in needed))
     chosen_stage = [i for i in range(len(tasks)) if late[i] == bool(stage)]
     placed = {i: -lag for i in range(len(tasks)) if stage and not late[i]}
     order = []
@@ -345,9 +345,8 @@
 
 CHUNK = 2
 LAG = 20
-NEAR = 3
-NEAR_LOAD = 0
-FAR_LOAD = -1
+LOAD = 0
+LATE_LOAD = -1
 HELD = 9
 VMEM_GRANT = 24 * 1024 * 1024
 PADS = {"sea_in": 2, "sea_hid": 2, "air_in": 2, "hid1": 2, "hid2": 4}
@@ -355,7 +354,7 @@
 
 def forecast_kernel(sizes, stage, *refs):
     fields, surface, flux_count, hidden, blocks, rows = sizes
-    loaded = range(NEAR, blocks) if stage else range(NEAR)
+    loaded = range(1) if stage else range(1, blocks)
     block_refs = dict(zip(loaded, refs, strict=False))
     se_ref, sx_ref, ae_ref, am_ref, ax_ref = refs[len(loaded) : len(loaded) + 5]
     rest = refs[len(loaded) + 5 :]
@@ -488,7 +487,7 @@
         for row in range(0, rows, CHUNK):
             near = range(block * rows + row, block * rows + row + CHUNK)
             writes = [(name, r) for name in ("sea_in", "air_now", "sea_now") for r in near]
-            depth = NEAR_LOAD if block < NEAR else FAR_LOAD
+            depth = LATE_LOAD if block == 0 else LOAD
             tasks.append((depth, [], writes, functools.partial(load_rows, block, row, CHUNK)))
     for step in range(STEPS):
         last = step == STEPS - 1
@@ -531,24 +530,23 @@
     state = pl.pallas_call(
         functools.partial(forecast_kernel, sizes, 0),
         out_shape=tuple(held),
-        in_specs=vmem_specs(NEAR + 5),
+        in_specs=vmem_specs(blocks - 1 + 5),
         out_specs=tuple(vmem_specs(HELD)),
         cost_estimate=pl.CostEstimate(flops=1000, bytes_accessed=1000, transcendentals=0),
         compiler_params=pltpu.CompilerParams(vmem_limit_bytes=VMEM_GRANT),
-        name="forecast_near",
-    )(*in_vmem(*frame[:NEAR], *weights))
-    far = blocks - NEAR
+        name="forecast_early",
+    )(*in_vmem(*frame[1:], *weights))
     return pl.pallas_call(
         functools.partial(forecast_kernel, sizes, 1),
         out_shape=(pltpu.VMEM((fields + surface, rows, LANES), jnp.bfloat16), *held),
-        in_specs=vmem_specs(far + 5 + HELD),
+        in_specs=vmem_specs(1 + 5 + HELD),
         out_specs=tuple(vmem_specs(1 + HELD)),
         scratch_shapes=[pltpu.VMEM((fields + surface, rows, LANES), jnp.float32)],
-        input_output_aliases={far + 5 + i: 1 + i for i in range(HELD)},
+        input_output_aliases={1 + 5 + i: 1 + i for i in range(HELD)},
         cost_estimate=cost,
         compiler_params=pltpu.CompilerParams(vmem_limit_bytes=VMEM_GRANT),
-        name="forecast_far",
-    )(*in_vmem(*frame[NEAR:], *weights, *state))[0]
+        name="forecast_late",
+    )(*in_vmem(frame[0], *weights, *state))[0]
 
 
 def belt_shards(
@@ -641,7 +639,6 @@
         and rows % SUBLANES == 0
         and rows <= LANES
         and rows >= 8
-        and blocks > NEAR
         and 2 * rows + 10 <= blocks * rows
         and blocks * rows <= 64
         and rows <= surface + flux_count

time: 30.7 us -> 28.9 us (0.941)
  waiting for transfers between devices: 6.99 us -> 5.18 us
    ppermute x3, waiting for transfers between devices: 3.31 us -> 1.7 us  [belt_shards(): frame[index] = lax.ppermute(packed, 'sp', pairs)]
  transfers between devices with their start and end apart: 5 -> 5, of which waited for: 3 -> 5; matrix products, arithmetic and copies ran while one was open for 0% -> 0% of each run, Pallas kernels for 17% -> 18%
where the time goes in v5:
time: 28.9 us; the launch traced here: 28.6 us
  Pallas kernels  12 us (42%)
  starting transfers between devices  9.93 us (34%)
  waiting for transfers between devices  5.18 us (18%)
  other arithmetic  0.83 us (3%)
  between operations  0.67 us (2%)
    pallas_call x1, Pallas kernels, forecast(): pl.pallas_call(functools.partial(forecast_kernel, sizes, 1), out_shape=(p...  6.08 us
    ppermute x3, starting transfers between devices, belt_shards(): frame[index] = lax.ppermute(packed, 'sp', pairs)  5.21 us
    ppermute x1, starting transfers between devices, belt_shards(): got = lax.ppermute(sent, 'sec', swap)  2.97 us
    ppermute x1, waiting for transfers between devices, belt_shards(): other = lax.ppermute(made, 'sec', swap)  2.58 us
    pallas_call x1, Pallas kernels, belt_shards(): pl.pallas_call(weights_kernel, out_shape=(pltpu.VMEM((hidden, 9 * sea_ent...  2.01 us
    pallas_call x1, Pallas kernels, forecast(): pl.pallas_call(functools.partial(forecast_kernel, sizes, 0), out_shape=tu...  1.94 us
    ppermute x1, starting transfers between devices, belt_shards(): other = lax.ppermute(made, 'sec', swap)  1.75 us
    ppermute x3, waiting for transfers between devices, belt_shards(): frame[index] = lax.ppermute(packed, 'sp', pairs)  1.7 us
  transfers between devices with their start and end apart: 5, of which 5 were waited for; matrix products, arithmetic and copies ran while one was open for 0% of the time, Pallas kernels for 18%

profile of v5, /device:TPU:0, one launch (start us, length us, event | category | flops | bytes accessed | tf_op | source)
XLA Modules:
  0.0 28.6 jit_solution(1041914627576874201)
XLA Ops:
  0.6 0.8 %select_bitcast_fusion = bf16[24,8,128]{2,1,0:T(8,128)(2,1)S(1)} fusion(bf16[2,24,8,128]{3,2,1,0:T(8,128)(2,1)} %air_ref.3, pred[]{:T(512)S(6)} %eq.3), kind=kLoop, calls=%fused_computation | loop fusion | flops 24576 | bytes 147457 | tf_op jit(solution)/shard_map/jit(_where)/select_n | solution.py:565
  1.5 3.0 %collective-permute-start = (bf16[24,8,128]{2,1,0:T(8,128)(2,1)S(1)}, bf16[24,8,128]{2,1,0:T(8,128)(2,1)S(1)}, u32[]{:S(2)}, u32[]{:S(2)}) collective-permute-start(bf16[24,8,128]{2,1,0:T(8,128)(2,1)S(1)} %select_bitcast_fusion), channel_id=1, source_target_pairs={{0,2},{2,0},{1,3},{3,1},{4,6},{6,4},{5,7},{7,5},{8,10},{10,8},{9,1... | collective-permute-start | bytes 147464 | tf_op jit(solution)/shard_map/ppermute | solution.py:566
  4.4 1.2 %pack_own.1.own_ref = bf16[40,1152]{1,0:T(8,128)(2,1)S(1)} custom-call(bf16[2,24,8,128]{3,2,1,0:T(8,128)(2,1)} %air_ref.3, bf16[2,8,8,128]{3,2,1,0:T(8,128)(2,1)} %sea_ref.1, bf16[2,8,8,128]{3,2,1,0:T(8,128)(2,1)} %flux_ref.1, s32[8,128]{1,0:T(8,128)} %mask_ref.1), custom_call_target="tpu_custom_call" | custom-call | flops 1000000 | bytes 1000000 | tf_op jit(solution)/shard_map/pack_own/pallas_call | solution.py:569
  5.6 0.9 %collective-permute-done.got_ref = bf16[24,8,128]{2,1,0:T(8,128)(2,1)S(1)} collective-permute-done((bf16[24,8,128]{2,1,0:T(8,128)(2,1)S(1)}, bf16[24,8,128]{2,1,0:T(8,128)(2,1)S(1)}, u32[]{:S(2)}, u32[]{:S(2)}) %collective-permute-start) | collective-permute-done | bytes 49184 | tf_op jit(solution)/shard_map/ppermute | solution.py:566
  6.5 0.2 pack_got.1.refs_0_
  6.7 3.2 %collective-permute-start.3 = (bf16[40,1152]{1,0:T(8,128)(2,1)S(1)}, bf16[40,1152]{1,0:T(8,128)(2,1)S(1)}, u32[]{:S(2)}, u32[]{:S(2)}) collective-permute-start(bf16[40,1152]{1,0:T(8,128)(2,1)S(1)} %pack_got.1.refs_0_), channel_id=1, source_target_pairs={{0,8},{4,12},{8,0},{12,4},{1,9},{5,13},{9,1},{13,5},{2,10},{6,14},... | collective-permute-start | bytes 276488 | tf_op jit(solution)/shard_map/ppermute | solution.py:610
  9.9 1.3 %collective-permute-start.2 = (bf16[40,1152]{1,0:T(8,128)(2,1)S(1)}, bf16[40,1152]{1,0:T(8,128)(2,1)S(1)}, u32[]{:S(2)}, u32[]{:S(2)}) collective-permute-start(bf16[40,1152]{1,0:T(8,128)(2,1)S(1)} %pack_got.1.refs_0_), channel_id=1, source_target_pairs={{0,12},{4,0},{8,4},{12,8},{1,13},{5,1},{9,5},{13,9},{2,14},{6,2},{... | collective-permute-start | bytes 276488 | tf_op jit(solution)/shard_map/ppermute | solution.py:610
  11.2 0.7 %collective-permute-start.1 = (bf16[40,1152]{1,0:T(8,128)(2,1)S(1)}, bf16[40,1152]{1,0:T(8,128)(2,1)S(1)}, u32[]{:S(2)}, u32[]{:S(2)}) collective-permute-start(bf16[40,1152]{1,0:T(8,128)(2,1)S(1)} %pack_got.1.refs_0_), channel_id=1, source_target_pairs={{0,4},{4,8},{8,12},{12,0},{1,5},{5,9},{9,13},{13,1},{2,6},{6,10},{... | collective-permute-start | bytes 276488 | tf_op jit(solution)/shard_map/ppermute | solution.py:610
  11.9 2.0 %weights.1 = (bf16[136,144]{1,0:T(8,128)(2,1)S(1)}, bf16[24,432]{1,0:T(8,128)(2,1)S(1)}, bf16[136,288]{1,0:T(8,128)(2,1)S(1)}, bf16[408,432]{1,0:T(8,128)(2,1)S(1)}, bf16[96,432]{1,0:T(8,128)(2,1)S(1)}) custom-call(bf16[3,3,16,136]{3,2,1,0:T(8,128)(2,1)} %se_ref.1, bf16[3,3,8,136]{3,2,1,0:T(8,128)(2,1)} %bitcast.5, bf16[3,3,32,136]{3,2,1,0:T(8,128)(2,1)} %ae_ref.1, ...), custom_call_target="tpu_custom_call" | custom-call | flops 1000000 | bytes 4000000 | tf_op jit(solution)/shard_map/weights/pallas_call | solution.py:588
  13.9 0.3 %collective-permute-done.3.refs_2_ = bf16[40,1152]{1,0:T(8,128)(2,1)S(1)} collective-permute-done((bf16[40,1152]{1,0:T(8,128)(2,1)S(1)}, bf16[40,1152]{1,0:T(8,128)(2,1)S(1)}, u32[]{:S(2)}, u32[]{:S(2)}) %collective-permute-start.3) | collective-permute-done | bytes 92192 | tf_op jit(solution)/shard_map/ppermute | solution.py:610
  14.2 1.0 %collective-permute-done.2.refs_1_ = bf16[40,1152]{1,0:T(8,128)(2,1)S(1)} collective-permute-done((bf16[40,1152]{1,0:T(8,128)(2,1)S(1)}, bf16[40,1152]{1,0:T(8,128)(2,1)S(1)}, u32[]{:S(2)}, u32[]{:S(2)}) %collective-permute-start.2) | collective-permute-done | bytes 92192 | tf_op jit(solution)/shard_map/ppermute | solution.py:610
  15.2 1.9 %forecast_early.1 = (bf16[48,4608]{1,0:T(8,128)(2,1)S(1)}, bf16[144,4608]{1,0:T(8,128)(2,1)S(1)}, bf16[96,4608]{1,0:T(8,128)(2,1)S(1)}, bf16[144,4608]{1,0:T(8,1...) custom-call(bf16[40,1152]{1,0:T(8,128)(2,1)S(1)} %pack_got.1.refs_0_, ...), custom_call_target="tpu_custom_call" | custom-call | flops 1000 | bytes 1000 | tf_op jit(solution)/shard_map/forecast_early/pallas_call | solution.py:530
  17.2 0.4 %collective-permute-done.1.refs_0_ = bf16[40,1152]{1,0:T(8,128)(2,1)S(1)} collective-permute-done((bf16[40,1152]{1,0:T(8,128)(2,1)S(1)}, bf16[40,1152]{1,0:T(8,128)(2,1)S(1)}, u32[]{:S(2)}, u32[]{:S(2)}) %collective-permute-start.1) | collective-permute-done | bytes 92192 | tf_op jit(solution)/shard_map/ppermute | solution.py:610
  17.6 0.0 copy-start
  17.6 6.1 %forecast_late.1 = (bf16[32,8,128]{2,1,0:T(8,128)(2,1)S(1)}, bf16[48,4608]{1,0:T(8,128)(2,1)S(1)}, bf16[144,4608]{1,0:T(8,128)(2,1)S(1)}, bf16[96,4608]{1,0:T(8,...) custom-call(bf16[40,1152]{1,0:T(8,128)(2,1)S(1)} %collective-permute, ...), custom_call_target="tpu_custom_call", output_to_operand_aliasing={{1}: (6, {}), {2}: (7, {}), {3}: (8, {}), {4}: (9, {}), {5}... | custom-call | flops 2000000000 | bytes 3000000 | tf_op jit(solution)/shard_map/forecast_late/pallas_call | solution.py:539
  23.7 1.8 %collective-permute-start.4 = (bf16[32,8,128]{2,1,0:T(8,128)(2,1)S(1)}, bf16[32,8,128]{2,1,0:T(8,128)(2,1)S(1)}, u32[]{:S(2)}, u32[]{:S(2)}) collective-permute-start(bf16[32,8,128]{2,1,0:T(8,128)(2,1)S(1)} %get-tuple-element.31.made_ref), channel_id=1, source_target_pairs={{0,2},{2,0},{1,3},{3,1},{4,6},{6,4},{5,7},{7,5},{8,10},{10,8},{9,1... | collective-permute-start | bytes 196616 | tf_op jit(solution)/shard_map/ppermute | solution.py:614
  25.4 2.6 %collective-permute-done.4.other_ref = bf16[32,8,128]{2,1,0:T(8,128)(2,1)S(1)} collective-permute-done((bf16[32,8,128]{2,1,0:T(8,128)(2,1)S(1)}, bf16[32,8,128]{2,1,0:T(8,128)(2,1)S(1)}, u32[]{:S(2)}, u32[]{:S(2)}) %collective-permute-start.4) | collective-permute-done | bytes 65568 | tf_op jit(solution)/shard_map/ppermute | solution.py:614
  28.0 0.0 copy-done
  28.0 0.7 %merge.1 = (bf16[2,24,8,128]{3,2,1,0:T(8,128)(2,1)}, bf16[2,8,8,128]{3,2,1,0:T(8,128)(2,1)}) custom-call(bf16[32,8,128]{2,1,0:T(8,128)(2,1)S(1)} %get-tuple-element.31.made_ref, bf16[32,8,128]{2,1,0:T(8,128)(2,1)S(1)} %collective-permute-done.4.other_ref, bf16[2,24,8,128]{3,2,1,0:T(8,128)(2,1)S(1)} %copy-done), custom_call_target="tpu_custom_call" | custom-call | flops 1000000 | bytes 1000000 | tf_op jit(solution)/shard_map/merge/pallas_call | solution.py:615
Async XLA Ops:
  1.5 5.0 %collective-permute-start = (bf16[24,8,128]{2,1,0:T(8,128)(2,1)S(1)}, bf16[24,8,128]{2,1,0:T(8,128)(2,1)S(1)}, u32[]{:S(2)}, u32[]{:S(2)}) collective-permute-start(bf16[24,8,128]{2,1,0:T(8,128)(2,1)S(1)} %select_bitcast_fusion), channel_id=1, source_target_pairs={{0,2},{2,0},{1,3},{3,1},{4,6},{6,4},{5,7},{7,5},{8,10},{10,8},{9,1... | collective-permute-start | bytes 147464 | tf_op jit(solution)/shard_map/ppermute | solution.py:566
  6.7 7.6 %collective-permute-start.3 = (bf16[40,1152]{1,0:T(8,128)(2,1)S(1)}, bf16[40,1152]{1,0:T(8,128)(2,1)S(1)}, u32[]{:S(2)}, u32[]{:S(2)}) collective-permute-start(bf16[40,1152]{1,0:T(8,128)(2,1)S(1)} %pack_got.1.refs_0_), channel_id=1, source_target_pairs={{0,8},{4,12},{8,0},{12,4},{1,9},{5,13},{9,1},{13,5},{2,10},{6,14},... | collective-permute-start | bytes 276488 | tf_op jit(solution)/shard_map/ppermute | solution.py:610
  9.9 5.4 %collective-permute-start.2 = (bf16[40,1152]{1,0:T(8,128)(2,1)S(1)}, bf16[40,1152]{1,0:T(8,128)(2,1)S(1)}, u32[]{:S(2)}, u32[]{:S(2)}) collective-permute-start(bf16[40,1152]{1,0:T(8,128)(2,1)S(1)} %pack_got.1.refs_0_), channel_id=1, source_target_pairs={{0,12},{4,0},{8,4},{12,8},{1,13},{5,1},{9,5},{13,9},{2,14},{6,2},{... | collective-permute-start | bytes 276488 | tf_op jit(solution)/shard_map/ppermute | solution.py:610
  11.2 6.3 %collective-permute-start.1 = (bf16[40,1152]{1,0:T(8,128)(2,1)S(1)}, bf16[40,1152]{1,0:T(8,128)(2,1)S(1)}, u32[]{:S(2)}, u32[]{:S(2)}) collective-permute-start(bf16[40,1152]{1,0:T(8,128)(2,1)S(1)} %pack_got.1.refs_0_), channel_id=1, source_target_pairs={{0,4},{4,8},{8,12},{12,0},{1,5},{5,9},{9,13},{13,1},{2,6},{6,10},{... | collective-permute-start | bytes 276488 | tf_op jit(solution)/shard_map/ppermute | solution.py:610
  17.6 10.4 %copy-start = (bf16[2,24,8,128]{3,2,1,0:T(8,128)(2,1)S(1)}, bf16[2,24,8,128]{3,2,1,0:T(8,128)(2,1)}, u32[]{:S(2)}) copy-start(bf16[2,24,8,128]{3,2,1,0:T(8,128)(2,1)} %air_ref.3) | copy-start | bytes 294916
  23.7 4.3 %collective-permute-start.4 = (bf16[32,8,128]{2,1,0:T(8,128)(2,1)S(1)}, bf16[32,8,128]{2,1,0:T(8,128)(2,1)S(1)}, u32[]{:S(2)}, u32[]{:S(2)}) collective-permute-start(bf16[32,8,128]{2,1,0:T(8,128)(2,1)S(1)} %get-tuple-element.31.made_ref), channel_id=1, source_target_pairs={{0,2},{2,0},{1,3},{3,1},{4,6},{6,4},{5,7},{7,5},{8,10},{10,8},{9,1... | collective-permute-start | bytes 196616 | tf_op jit(solution)/shard_map/ppermute | solution.py:614

commit v6 on v5

--- a/solution.py
+++ b/solution.py
@@ -251,9 +251,10 @@
 
 
 def pack_got_kernel(own_ref, got_ref, out_ref, planes):
-    fields, rows = got_ref.shape[:2]
-    first = lax.axis_index("sec") == 0
-    planes[...] = got_ref[...].astype(jnp.float32)
+    fields, rows = got_ref.shape[1:3]
+    section = lax.axis_index("sec")
+    first = section == 0
+    planes[...] = got_ref[section].astype(jnp.float32)
     bands = [planes[:, row, :] for row in range(rows)]
     out_ref[fields:, :] = own_ref[fields:, :]
 
@@ -304,6 +305,25 @@
                 pieces += [tap if turned else tap.T, blank]
             groups.append(jnp.concatenate(pieces, axis=1))
         target[...] = jnp.concatenate(groups, axis=0).astype(jnp.bfloat16)
+
+
+def prepare_weights(sea_entry, sea_exit, air_entry, air_middle, air_exit):
+    hidden, surface, produced = air_middle.shape[3], sea_exit.shape[3], air_exit.shape[3]
+    hidden_rows = pad_to(hidden, PACKED)
+    return pl.pallas_call(
+        weights_kernel,
+        out_shape=(
+            pltpu.VMEM((hidden, 9 * sea_entry.shape[2]), jnp.bfloat16),
+            pltpu.VMEM((3 * surface, 3 * hidden_rows), jnp.bfloat16),
+            pltpu.VMEM((hidden, 9 * air_entry.shape[2]), jnp.bfloat16),
+            pltpu.VMEM((3 * hidden, 3 * hidden_rows), jnp.bfloat16),
+            pltpu.VMEM((3 * produced, 3 * hidden_rows), jnp.bfloat16),
+        ),
+        in_specs=vmem_specs(5),
+        out_specs=tuple(vmem_specs(5)),
+        cost_estimate=pl.CostEstimate(flops=1000000, bytes_accessed=4000000, transcendentals=0),
+        name="weights",
+    )(sea_entry, jnp.swapaxes(sea_exit, 2, 3), air_entry, air_middle, jnp.swapaxes(air_exit, 2, 3))
 
 
 def ordered(tasks, ring, lag, stage):
@@ -553,17 +573,14 @@
     atmosphere, ocean_state, fluxes, sea_mask, air_entry, air_middle, air_exit, sea_entry, sea_exit
 ):
     blocks = lax.axis_size("sp")
-    position = lax.axis_index("sec")
-    members, fields, rows, cols = atmosphere.shape
+    fields, rows = atmosphere.shape[1:3]
     surface, flux_count = ocean_state.shape[1], fluxes.shape[1]
     hidden = air_middle.shape[3]
-    hidden_rows = pad_to(hidden, PACKED)
     kept = fields + surface + flux_count
     swap = [(0, 1), (1, 0)]
     bf16, f32 = jnp.bfloat16, jnp.float32
 
-    sent = jnp.where(position == 0, atmosphere[1], atmosphere[0])
-    got = lax.ppermute(sent, "sec", swap)
+    got = lax.ppermute(atmosphere, "sec", swap)
     packed_shape = pltpu.VMEM((kept, (rows + 1) * LANES), bf16)
     small = pl.CostEstimate(flops=1000000, bytes_accessed=1000000, transcendentals=0)
     own = pl.pallas_call(
@@ -585,20 +602,7 @@
         name="pack_got",
     )(*in_vmem(own, got))
 
-    weights = pl.pallas_call(
-        weights_kernel,
-        out_shape=(
-            pltpu.VMEM((hidden, 9 * sea_entry.shape[2]), bf16),
-            pltpu.VMEM((3 * surface, 3 * hidden_rows), bf16),
-            pltpu.VMEM((hidden, 9 * air_entry.shape[2]), bf16),
-            pltpu.VMEM((3 * hidden, 3 * hidden_rows), bf16),
-            pltpu.VMEM((3 * (fields + flux_count), 3 * hidden_rows), bf16),
-        ),
-        in_specs=vmem_specs(5),
-        out_specs=tuple(vmem_specs(5)),
-        cost_estimate=pl.CostEstimate(flops=1000000, bytes_accessed=4000000, transcendentals=0),
-        name="weights",
-    )(sea_entry, jnp.swapaxes(sea_exit, 2, 3), air_entry, air_middle, jnp.swapaxes(air_exit, 2, 3))
+    weights = prepare_weights(sea_entry, sea_exit, air_entry, air_middle, air_exit)
 
     frame = [None] * blocks
     for index in range(blocks):

time: 28.9 us -> 28.9 us (level)
  waiting for transfers between devices: 5.18 us -> 6.25 us
  other arithmetic: 0.83 us -> 0 us
    ppermute x1, waiting for transfers between devices: 0.9 us -> 1.83 us  [belt_shards(): got = lax.ppermute(atmosphere, 'sec', swap)]
    select_n x1 -> x0, other arithmetic: 0.83 us -> none  [belt_shards(): sent = jnp.where(position == 0, atmosphere[1], atmosphere[0])]
  transfers between devices with their start and end apart: 5 -> 5, of which waited for: 5 -> 4; matrix products, arithmetic and copies ran while one was open for 0% -> 0% of each run, Pallas kernels for 18% -> 18%
where the time goes in v6:
time: 28.9 us; the launch traced here: 28.7 us
  Pallas kernels  12.1 us (42%)
  starting transfers between devices  9.7 us (34%)
  waiting for transfers between devices  6.25 us (22%)
  between operations  0.68 us (2%)
    pallas_call x1, Pallas kernels, forecast(): pl.pallas_call(functools.partial(forecast_kernel, sizes, 1), out_shape=(p...  6.11 us
    ppermute x3, starting transfers between devices, belt_shards(): frame[index] = lax.ppermute(packed, 'sp', pairs)  5.01 us
    ppermute x1, starting transfers between devices, belt_shards(): got = lax.ppermute(atmosphere, 'sec', swap)  3.03 us
    ppermute x1, waiting for transfers between devices, belt_shards(): other = lax.ppermute(made, 'sec', swap)  2.68 us
    pallas_call x1, Pallas kernels, prepare_weights(): pl.pallas_call(weights_kernel, out_shape=(pltpu.VMEM((hidden, 9 * sea_ent...  2.01 us
    pallas_call x1, Pallas kernels, forecast(): pl.pallas_call(functools.partial(forecast_kernel, sizes, 0), out_shape=tu...  1.94 us
    ppermute x1, waiting for transfers between devices, belt_shards(): got = lax.ppermute(atmosphere, 'sec', swap)  1.83 us
    ppermute x3, waiting for transfers between devices, belt_shards(): frame[index] = lax.ppermute(packed, 'sp', pairs)  1.75 us
  transfers between devices with their start and end apart: 5, of which 4 were waited for; matrix products, arithmetic and copies ran while one was open for 0% of the time, Pallas kernels for 18%

profile of v6, /device:TPU:0, one launch (start us, length us, event | category | flops | bytes accessed | tf_op | source)
XLA Modules:
  0.0 28.7 jit_solution(9985024561950626623)
XLA Ops:
  0.6 3.0 %collective-permute-start = (bf16[2,24,8,128]{3,2,1,0:T(8,128)(2,1)}, bf16[2,24,8,128]{3,2,1,0:T(8,128)(2,1)S(1)}, u32[]{:S(2)}, u32[]{:S(2)}) collective-permute-start(bf16[2,24,8,128]{3,2,1,0:T(8,128)(2,1)} %air_ref.3), channel_id=1, source_target_pairs={{0,2},{2,0},{1,3},{3,1},{4,6},{6,4},{5,7},{7,5},{8,10},{10,8},{9,1... | collective-permute-start | bytes 294920 | tf_op jit(solution)/shard_map/ppermute | solution.py:583
  3.7 1.2 %pack_own.1.own_ref = bf16[40,1152]{1,0:T(8,128)(2,1)S(1)} custom-call(bf16[2,24,8,128]{3,2,1,0:T(8,128)(2,1)} %air_ref.3, bf16[2,8,8,128]{3,2,1,0:T(8,128)(2,1)} %sea_ref.1, bf16[2,8,8,128]{3,2,1,0:T(8,128)(2,1)} %flux_ref.1, s32[8,128]{1,0:T(8,128)} %mask_ref.1), custom_call_target="tpu_custom_call" | custom-call | flops 1000000 | bytes 1000000 | tf_op jit(solution)/shard_map/pack_own/pallas_call | solution.py:586
  4.8 1.8 %collective-permute-done.got_ref = bf16[2,24,8,128]{3,2,1,0:T(8,128)(2,1)S(1)} collective-permute-done((bf16[2,24,8,128]{3,2,1,0:T(8,128)(2,1)}, bf16[2,24,8,128]{3,2,1,0:T(8,128)(2,1)S(1)}, u32[]{:S(2)}, u32[]{:S(2)}) %collective-permute-start) | collective-permute-done | bytes 98336 | tf_op jit(solution)/shard_map/ppermute | solution.py:583
  6.7 0.2 pack_got.1.refs_0_
  6.8 3.0 %collective-permute-start.3 = (bf16[40,1152]{1,0:T(8,128)(2,1)S(1)}, bf16[40,1152]{1,0:T(8,128)(2,1)S(1)}, u32[]{:S(2)}, u32[]{:S(2)}) collective-permute-start(bf16[40,1152]{1,0:T(8,128)(2,1)S(1)} %pack_got.1.refs_0_), channel_id=1, source_target_pairs={{0,8},{4,12},{8,0},{12,4},{1,9},{5,13},{9,1},{13,5},{2,10},{6,14},... | collective-permute-start | bytes 276488 | tf_op jit(solution)/shard_map/ppermute | solution.py:614
  9.8 1.3 %collective-permute-start.2 = (bf16[40,1152]{1,0:T(8,128)(2,1)S(1)}, bf16[40,1152]{1,0:T(8,128)(2,1)S(1)}, u32[]{:S(2)}, u32[]{:S(2)}) collective-permute-start(bf16[40,1152]{1,0:T(8,128)(2,1)S(1)} %pack_got.1.refs_0_), channel_id=1, source_target_pairs={{0,12},{4,0},{8,4},{12,8},{1,13},{5,1},{9,5},{13,9},{2,14},{6,2},{... | collective-permute-start | bytes 276488 | tf_op jit(solution)/shard_map/ppermute | solution.py:614
  11.2 0.7 %collective-permute-start.1 = (bf16[40,1152]{1,0:T(8,128)(2,1)S(1)}, bf16[40,1152]{1,0:T(8,128)(2,1)S(1)}, u32[]{:S(2)}, u32[]{:S(2)}) collective-permute-start(bf16[40,1152]{1,0:T(8,128)(2,1)S(1)} %pack_got.1.refs_0_), channel_id=1, source_target_pairs={{0,4},{4,8},{8,12},{12,0},{1,5},{5,9},{9,13},{13,1},{2,6},{6,10},{... | collective-permute-start | bytes 276488 | tf_op jit(solution)/shard_map/ppermute | solution.py:614
  11.9 2.0 %weights.1 = (bf16[136,144]{1,0:T(8,128)(2,1)S(1)}, bf16[24,432]{1,0:T(8,128)(2,1)S(1)}, bf16[136,288]{1,0:T(8,128)(2,1)S(1)}, bf16[408,432]{1,0:T(8,128)(2,1)S(1)}, bf16[96,432]{1,0:T(8,128)(2,1)S(1)}) custom-call(bf16[3,3,16,136]{3,2,1,0:T(8,128)(2,1)} %se_ref.1, bf16[3,3,8,136]{3,2,1,0:T(8,128)(2,1)} %bitcast.3, bf16[3,3,32,136]{3,2,1,0:T(8,128)(2,1)} %ae_ref.1, ...), custom_call_target="tpu_custom_call" | custom-call | flops 1000000 | bytes 4000000 | tf_op jit(solution)/shard_map/weights/pallas_call | solution.py:313
  13.9 1.2 %collective-permute-done.3.refs_2_ = bf16[40,1152]{1,0:T(8,128)(2,1)S(1)} collective-permute-done((bf16[40,1152]{1,0:T(8,128)(2,1)S(1)}, bf16[40,1152]{1,0:T(8,128)(2,1)S(1)}, u32[]{:S(2)}, u32[]{:S(2)}) %collective-permute-start.3) | collective-permute-done | bytes 92192 | tf_op jit(solution)/shard_map/ppermute | solution.py:614
  15.1 0.5 %collective-permute-done.2.refs_1_ = bf16[40,1152]{1,0:T(8,128)(2,1)S(1)} collective-permute-done((bf16[40,1152]{1,0:T(8,128)(2,1)S(1)}, bf16[40,1152]{1,0:T(8,128)(2,1)S(1)}, u32[]{:S(2)}, u32[]{:S(2)}) %collective-permute-start.2) | collective-permute-done | bytes 92192 | tf_op jit(solution)/shard_map/ppermute | solution.py:614
  15.6 1.9 %forecast_early.1 = (bf16[48,4608]{1,0:T(8,128)(2,1)S(1)}, bf16[144,4608]{1,0:T(8,128)(2,1)S(1)}, bf16[96,4608]{1,0:T(8,128)(2,1)S(1)}, bf16[144,4608]{1,0:T(8,1...) custom-call(bf16[40,1152]{1,0:T(8,128)(2,1)S(1)} %pack_got.1.refs_0_, ...), custom_call_target="tpu_custom_call" | custom-call | flops 1000 | bytes 1000 | tf_op jit(solution)/shard_map/forecast_early/pallas_call | solution.py:550
  17.6 0.0 collective-permute-done.1.refs_0_
  17.6 0.0 copy-start
  17.6 6.1 %forecast_late.1 = (bf16[32,8,128]{2,1,0:T(8,128)(2,1)S(1)}, bf16[48,4608]{1,0:T(8,128)(2,1)S(1)}, bf16[144,4608]{1,0:T(8,128)(2,1)S(1)}, bf16[96,4608]{1,0:T(8,...) custom-call(bf16[40,1152]{1,0:T(8,128)(2,1)S(1)} %collective-permute, ...), custom_call_target="tpu_custom_call", output_to_operand_aliasing={{1}: (6, {}), {2}: (7, {}), {3}: (8, {}), {4}: (9, {}), {5}... | custom-call | flops 2000000000 | bytes 3000000 | tf_op jit(solution)/shard_map/forecast_late/pallas_call | solution.py:559
  23.7 1.7 %collective-permute-start.4 = (bf16[32,8,128]{2,1,0:T(8,128)(2,1)S(1)}, bf16[32,8,128]{2,1,0:T(8,128)(2,1)S(1)}, u32[]{:S(2)}, u32[]{:S(2)}) collective-permute-start(bf16[32,8,128]{2,1,0:T(8,128)(2,1)S(1)} %get-tuple-element.31.made_ref), channel_id=1, source_target_pairs={{0,2},{2,0},{1,3},{3,1},{4,6},{6,4},{5,7},{7,5},{8,10},{10,8},{9,1... | collective-permute-start | bytes 196616 | tf_op jit(solution)/shard_map/ppermute | solution.py:618
  25.4 2.7 %collective-permute-done.4.other_ref = bf16[32,8,128]{2,1,0:T(8,128)(2,1)S(1)} collective-permute-done((bf16[32,8,128]{2,1,0:T(8,128)(2,1)S(1)}, bf16[32,8,128]{2,1,0:T(8,128)(2,1)S(1)}, u32[]{:S(2)}, u32[]{:S(2)}) %collective-permute-start.4) | collective-permute-done | bytes 65568 | tf_op jit(solution)/shard_map/ppermute | solution.py:618
  28.0 0.0 copy-done
  28.0 0.7 %merge.1 = (bf16[2,24,8,128]{3,2,1,0:T(8,128)(2,1)}, bf16[2,8,8,128]{3,2,1,0:T(8,128)(2,1)}) custom-call(bf16[32,8,128]{2,1,0:T(8,128)(2,1)S(1)} %get-tuple-element.31.made_ref, bf16[32,8,128]{2,1,0:T(8,128)(2,1)S(1)} %collective-permute-done.4.other_ref, bf16[2,24,8,128]{3,2,1,0:T(8,128)(2,1)S(1)} %copy-done), custom_call_target="tpu_custom_call" | custom-call | flops 1000000 | bytes 1000000 | tf_op jit(solution)/shard_map/merge/pallas_call | solution.py:619
Async XLA Ops:
  0.6 6.0 %collective-permute-start = (bf16[2,24,8,128]{3,2,1,0:T(8,128)(2,1)}, bf16[2,24,8,128]{3,2,1,0:T(8,128)(2,1)S(1)}, u32[]{:S(2)}, u32[]{:S(2)}) collective-permute-start(bf16[2,24,8,128]{3,2,1,0:T(8,128)(2,1)} %air_ref.3), channel_id=1, source_target_pairs={{0,2},{2,0},{1,3},{3,1},{4,6},{6,4},{5,7},{7,5},{8,10},{10,8},{9,1... | collective-permute-start | bytes 294920 | tf_op jit(solution)/shard_map/ppermute | solution.py:583
  6.8 8.2 %collective-permute-start.3 = (bf16[40,1152]{1,0:T(8,128)(2,1)S(1)}, bf16[40,1152]{1,0:T(8,128)(2,1)S(1)}, u32[]{:S(2)}, u32[]{:S(2)}) collective-permute-start(bf16[40,1152]{1,0:T(8,128)(2,1)S(1)} %pack_got.1.refs_0_), channel_id=1, source_target_pairs={{0,8},{4,12},{8,0},{12,4},{1,9},{5,13},{9,1},{13,5},{2,10},{6,14},... | collective-permute-start | bytes 276488 | tf_op jit(solution)/shard_map/ppermute | solution.py:614
  9.8 5.8 %collective-permute-start.2 = (bf16[40,1152]{1,0:T(8,128)(2,1)S(1)}, bf16[40,1152]{1,0:T(8,128)(2,1)S(1)}, u32[]{:S(2)}, u32[]{:S(2)}) collective-permute-start(bf16[40,1152]{1,0:T(8,128)(2,1)S(1)} %pack_got.1.refs_0_), channel_id=1, source_target_pairs={{0,12},{4,0},{8,4},{12,8},{1,13},{5,1},{9,5},{13,9},{2,14},{6,2},{... | collective-permute-start | bytes 276488 | tf_op jit(solution)/shard_map/ppermute | solution.py:614
  11.2 6.4 %collective-permute-start.1 = (bf16[40,1152]{1,0:T(8,128)(2,1)S(1)}, bf16[40,1152]{1,0:T(8,128)(2,1)S(1)}, u32[]{:S(2)}, u32[]{:S(2)}) collective-permute-start(bf16[40,1152]{1,0:T(8,128)(2,1)S(1)} %pack_got.1.refs_0_), channel_id=1, source_target_pairs={{0,4},{4,8},{8,12},{12,0},{1,5},{5,9},{9,13},{13,1},{2,6},{6,10},{... | collective-permute-start | bytes 276488 | tf_op jit(solution)/shard_map/ppermute | solution.py:614
  17.6 10.5 %copy-start = (bf16[2,24,8,128]{3,2,1,0:T(8,128)(2,1)S(1)}, bf16[2,24,8,128]{3,2,1,0:T(8,128)(2,1)}, u32[]{:S(2)}) copy-start(bf16[2,24,8,128]{3,2,1,0:T(8,128)(2,1)} %air_ref.3) | copy-start | bytes 294916
  23.7 4.3 %collective-permute-start.4 = (bf16[32,8,128]{2,1,0:T(8,128)(2,1)S(1)}, bf16[32,8,128]{2,1,0:T(8,128)(2,1)S(1)}, u32[]{:S(2)}, u32[]{:S(2)}) collective-permute-start(bf16[32,8,128]{2,1,0:T(8,128)(2,1)S(1)} %get-tuple-element.31.made_ref), channel_id=1, source_target_pairs={{0,2},{2,0},{1,3},{3,1},{4,6},{6,4},{5,7},{7,5},{8,10},{10,8},{9,1... | collective-permute-start | bytes 196616 | tf_op jit(solution)/shard_map/ppermute | solution.py:618

commit v7 on v6

--- a/solution.py
+++ b/solution.py
@@ -222,11 +222,25 @@
     return tuple(pltpu.with_memory_space_constraint(value, pltpu.VMEM) for value in values)
 
 
+def pick_kernel(air_ref, out_ref, done):
+    copy = pltpu.make_async_copy(air_ref.at[1 - lax.axis_index("sec")], out_ref, done)
+    copy.start()
+    copy.wait()
+
+
+def tile(group, rows, row):
+    return pl.ds((group * rows + row) * LANES, LANES)
+
+
 def edge_of(bands):
-    lanes = lane_ids(bands[0].shape[0])
-    edge = jnp.where(lanes == 0, bands[0], 0.0)
-    for row, band in enumerate(bands[1:], 1):
-        edge = jnp.where(lanes == row, pltpu.roll(band, row, 1), edge)
+    groups = bands[0].shape[0] // SUBLANES
+    lanes = lane_ids(SUBLANES)
+    edge = jnp.zeros((SUBLANES, LANES), jnp.float32)
+    for row, band in enumerate(bands):
+        for group in range(groups):
+            place = group * len(bands) + row
+            part = band[group * SUBLANES : (group + 1) * SUBLANES]
+            edge = jnp.where(lanes == place, pltpu.roll(part, place, 1) if place else part, edge)
     return edge
 
 
@@ -235,6 +249,7 @@
     surface = sea_ref.shape[1]
     rows = air_ref.shape[2]
     kept = fields + surface + flux_ref.shape[1]
+    groups = kept // SUBLANES
     section = lax.axis_index("sec")
     planes[0:fields] = air_ref[section].astype(jnp.float32)
     planes[fields : fields + surface] = sea_ref[section].astype(jnp.float32)
@@ -242,32 +257,36 @@
     bands = []
     for row in range(rows):
         values = planes[:, row, :]
-        out_ref[:, row * LANES : (row + 1) * LANES] = values.astype(jnp.bfloat16)
+        for group in range(groups):
+            part = values[group * SUBLANES : (group + 1) * SUBLANES]
+            out_ref[:, tile(group, rows, row)] = part.astype(jnp.bfloat16)
         bands.append(values[0:fields])
-    mask = mask_ref[...].astype(jnp.float32)
-    rest = jnp.zeros((kept - fields - rows, LANES), jnp.float32)
-    tail = jnp.concatenate([edge_of(bands), mask, rest], axis=0)
-    out_ref[:, rows * LANES : (rows + 1) * LANES] = tail.astype(jnp.bfloat16)
+    out_ref[:, tile(groups, rows, 0)] = mask_ref[...].astype(jnp.bfloat16)
+    out_ref[:, tile(groups, rows, 1)] = edge_of(bands).astype(jnp.bfloat16)
 
 
 def pack_got_kernel(own_ref, got_ref, out_ref, planes):
-    fields, rows = got_ref.shape[1:3]
-    section = lax.axis_index("sec")
-    first = section == 0
-    planes[...] = got_ref[section].astype(jnp.float32)
+    fields, rows = got_ref.shape[:2]
+    groups = fields // SUBLANES
+    last = own_ref.shape[1] - LANES
+    first = lax.axis_index("sec") == 0
+    planes[...] = got_ref[...].astype(jnp.float32)
     bands = [planes[:, row, :] for row in range(rows)]
-    out_ref[fields:, :] = own_ref[fields:, :]
+    air = groups * rows * LANES
+    out_ref[:, air:last] = own_ref[:, air:last]
 
     @pl.when(first)
     def _():
-        out_ref[0:fields, 0 : rows * LANES] = own_ref[0:fields, 0 : rows * LANES]
-        out_ref[0:fields, rows * LANES :] = edge_of(bands).astype(jnp.bfloat16)
+        out_ref[:, 0:air] = own_ref[:, 0:air]
+        out_ref[:, last:] = edge_of(bands).astype(jnp.bfloat16)
 
     @pl.when(jnp.logical_not(first))
     def _():
-        out_ref[0:fields, rows * LANES :] = own_ref[0:fields, rows * LANES :]
+        out_ref[:, last:] = own_ref[:, last:]
         for row, band in enumerate(bands):
-            out_ref[0:fields, row * LANES : (row + 1) * LANES] = band.astype(jnp.bfloat16)
+            for group in range(groups):
+                part = band[group * SUBLANES : (group + 1) * SUBLANES]
+                out_ref[:, tile(group, rows, row)] = part.astype(jnp.bfloat16)
 
 
 def merge_kernel(made_ref, other_ref, air_ref, air_out, sea_out):
@@ -473,20 +492,27 @@
                 flux = change[fields:].astype(jnp.bfloat16).astype(jnp.float32)
                 put_sea_in(at, jnp.concatenate([sea, flux], axis=0))
 
+    groups = kept // SUBLANES
+    tail = groups * rows * LANES
+
     def load_rows(block, row, count):
         source = block_refs[block]
         for i in range(row, row + count):
-            values = source[:, i * LANES : (i + 1) * LANES].astype(jnp.float32)
+            parts = [source[:, tile(group, rows, i)] for group in range(groups)]
+            values = jnp.concatenate([part.astype(jnp.float32) for part in parts], axis=0)
             at = block * rows + i
             air_now[:, span(at, 1)] = values[0:fields]
             sea_now[:, span(at, 1)] = values[fields : fields + surface]
             put_sea_in(at, values[fields:kept])
-            tail = source[0:fields, rows * LANES : (rows + 1) * LANES].astype(jnp.float32)
-            edge_in[:, span(at, 1)] = jnp.broadcast_to(tail[:, i : i + 1], (fields, LANES))
+            edge = source[:, tail + LANES : tail + 2 * LANES].astype(jnp.float32)
+            places = [group * rows + i for group in range(fields // SUBLANES)]
+            columns = [edge[:, place : place + 1] for place in places]
+            columns = [jnp.broadcast_to(column, (SUBLANES, LANES)) for column in columns]
+            edge_in[:, span(at, 1)] = jnp.concatenate(columns, axis=0)
 
     for block, source in block_refs.items():
-        tail = source[fields : fields + rows, rows * LANES : (rows + 1) * LANES]
-        mask_in[block * rows : (block + 1) * rows, :] = tail.astype(jnp.float32)
+        mask = source[:, tail : tail + LANES].astype(jnp.float32)
+        mask_in[block * rows : (block + 1) * rows, :] = mask
 
     tasks = []
 
@@ -580,8 +606,16 @@
     swap = [(0, 1), (1, 0)]
     bf16, f32 = jnp.bfloat16, jnp.float32
 
-    got = lax.ppermute(atmosphere, "sec", swap)
-    packed_shape = pltpu.VMEM((kept, (rows + 1) * LANES), bf16)
+    sent = pl.pallas_call(
+        pick_kernel,
+        out_shape=pltpu.VMEM(atmosphere.shape[1:], bf16),
+        in_specs=[pl.BlockSpec(memory_space=pl.ANY)],
+        out_specs=vmem_specs(1)[0],
+        scratch_shapes=[pltpu.SemaphoreType.DMA(())],
+        name="pick",
+    )(atmosphere)
+    got = lax.ppermute(sent, "sec", swap)
+    packed_shape = pltpu.VMEM((SUBLANES, (kept // SUBLANES * rows + 2) * LANES), bf16)
     small = pl.CostEstimate(flops=1000000, bytes_accessed=1000000, transcendentals=0)
     own = pl.pallas_call(
         pack_own_kernel,
@@ -640,12 +674,10 @@
         and members == 2
         and band == LANES
         and ocean_state.shape[3] == band
-        and rows % SUBLANES == 0
-        and rows <= LANES
-        and rows >= 8
+        and rows == SUBLANES
+        and atmosphere.shape[1] <= LANES
         and 2 * rows + 10 <= blocks * rows
         and blocks * rows <= 64
-        and rows <= surface + flux_count
         and all(c % SUBLANES == 0 for c in (fields, surface, flux_count, sea_entry.shape[3]))
         and (surface + flux_count) % PACKED == 0
         and (fields + surface) % PACKED == 0

time: 28.9 us -> 28.9 us (level)
  waiting for transfers between devices: 6.25 us -> 5.2 us
  Pallas kernels: 12.1 us -> 12.9 us
    ppermute x1, waiting for transfers between devices: 1.83 us -> 0.87 us  [belt_shards(): got = lax.ppermute(sent, 'sec', swap)]
    pallas_call x0 -> x1, Pallas kernels: none -> 0.82 us  [belt_shards(): pl.pallas_call(pick_kernel, out_shape=pltpu.VMEM(atmosphere.shape[1:], bf...]
where the time goes in v7:
time: 28.9 us; the launch traced here: 28.7 us
  Pallas kernels  12.9 us (45%)
  starting transfers between devices  9.86 us (34%)
  waiting for transfers between devices  5.2 us (18%)
  between operations  0.67 us (2%)
    pallas_call x1, Pallas kernels, forecast(): pl.pallas_call(functools.partial(forecast_kernel, sizes, 1), out_shape=(p...  6.13 us
    ppermute x3, starting transfers between devices, belt_shards(): frame[index] = lax.ppermute(packed, 'sp', pairs)  5.21 us
    ppermute x1, starting transfers between devices, belt_shards(): got = lax.ppermute(sent, 'sec', swap)  3.03 us
    ppermute x1, waiting for transfers between devices, belt_shards(): other = lax.ppermute(made, 'sec', swap)  2.72 us
    pallas_call x1, Pallas kernels, prepare_weights(): pl.pallas_call(weights_kernel, out_shape=(pltpu.VMEM((hidden, 9 * sea_ent...  2.01 us
    pallas_call x1, Pallas kernels, forecast(): pl.pallas_call(functools.partial(forecast_kernel, sizes, 0), out_shape=tu...  1.95 us
    ppermute x3, waiting for transfers between devices, belt_shards(): frame[index] = lax.ppermute(packed, 'sp', pairs)  1.62 us
    ppermute x1, starting transfers between devices, belt_shards(): other = lax.ppermute(made, 'sec', swap)  1.61 us
  transfers between devices with their start and end apart: 5, of which 4 were waited for; matrix products, arithmetic and copies ran while one was open for 0% of the time, Pallas kernels for 18%

profile of v7, /device:TPU:0, one launch (start us, length us, event | category | flops | bytes accessed | tf_op | source)
XLA Modules:
  0.0 28.7 jit_solution(14831358677785132441)
XLA Ops:
  0.6 0.8 %pick.1 = bf16[24,8,128]{2,1,0:T(8,128)(2,1)S(1)} custom-call(bf16[2,24,8,128]{3,2,1,0:T(8,128)(2,1)} %air_ref.5), custom_call_target="tpu_custom_call" | custom-call | tf_op jit(solution)/shard_map/pick/pallas_call | solution.py:609
  1.5 3.0 %collective-permute-start = (bf16[24,8,128]{2,1,0:T(8,128)(2,1)S(1)}, bf16[24,8,128]{2,1,0:T(8,128)(2,1)S(1)}, u32[]{:S(2)}, u32[]{:S(2)}) collective-permute-start(bf16[24,8,128]{2,1,0:T(8,128)(2,1)S(1)} %pick.1), channel_id=1, source_target_pairs={{0,2},{2,0},{1,3},{3,1},{4,6},{6,4},{5,7},{7,5},{8,10},{10,8},{9,1... | collective-permute-start | bytes 147464 | tf_op jit(solution)/shard_map/ppermute | solution.py:617
  4.5 1.2 %pack_own.1.own_ref = bf16[8,5376]{1,0:T(8,128)(2,1)S(1)} custom-call(bf16[2,24,8,128]{3,2,1,0:T(8,128)(2,1)} %air_ref.5, bf16[2,8,8,128]{3,2,1,0:T(8,128)(2,1)} %sea_ref.1, bf16[2,8,8,128]{3,2,1,0:T(8,128)(2,1)} %flux_ref.1, s32[8,128]{1,0:T(8,128)} %mask_ref.1), custom_call_target="tpu_custom_call" | custom-call | flops 1000000 | bytes 1000000 | tf_op jit(solution)/shard_map/pack_own/pallas_call | solution.py:620
  5.7 0.9 %collective-permute-done.got_ref = bf16[24,8,128]{2,1,0:T(8,128)(2,1)S(1)} collective-permute-done((bf16[24,8,128]{2,1,0:T(8,128)(2,1)S(1)}, bf16[24,8,128]{2,1,0:T(8,128)(2,1)S(1)}, u32[]{:S(2)}, u32[]{:S(2)}) %collective-permute-start) | collective-permute-done | bytes 49184 | tf_op jit(solution)/shard_map/ppermute | solution.py:617
  6.6 0.2 pack_got.1.refs_0_
  6.7 3.2 %collective-permute-start.3 = (bf16[8,5376]{1,0:T(8,128)(2,1)S(1)}, bf16[8,5376]{1,0:T(8,128)(2,1)S(1)}, u32[]{:S(2)}, u32[]{:S(2)}) collective-permute-start(bf16[8,5376]{1,0:T(8,128)(2,1)S(1)} %pack_got.1.refs_0_), channel_id=1, source_target_pairs={{0,8},{4,12},{8,0},{12,4},{1,9},{5,13},{9,1},{13,5},{2,10},{6,14},... | collective-permute-start | bytes 258056 | tf_op jit(solution)/shard_map/ppermute | solution.py:648
  9.9 1.3 %collective-permute-start.2 = (bf16[8,5376]{1,0:T(8,128)(2,1)S(1)}, bf16[8,5376]{1,0:T(8,128)(2,1)S(1)}, u32[]{:S(2)}, u32[]{:S(2)}) collective-permute-start(bf16[8,5376]{1,0:T(8,128)(2,1)S(1)} %pack_got.1.refs_0_), channel_id=1, source_target_pairs={{0,12},{4,0},{8,4},{12,8},{1,13},{5,1},{9,5},{13,9},{2,14},{6,2},{... | collective-permute-start | bytes 258056 | tf_op jit(solution)/shard_map/ppermute | solution.py:648
  11.3 0.7 %collective-permute-start.1 = (bf16[8,5376]{1,0:T(8,128)(2,1)S(1)}, bf16[8,5376]{1,0:T(8,128)(2,1)S(1)}, u32[]{:S(2)}, u32[]{:S(2)}) collective-permute-start(bf16[8,5376]{1,0:T(8,128)(2,1)S(1)} %pack_got.1.refs_0_), channel_id=1, source_target_pairs={{0,4},{4,8},{8,12},{12,0},{1,5},{5,9},{9,13},{13,1},{2,6},{6,10},{... | collective-permute-start | bytes 258056 | tf_op jit(solution)/shard_map/ppermute | solution.py:648
  11.9 2.0 %weights.1 = (bf16[136,144]{1,0:T(8,128)(2,1)S(1)}, bf16[24,432]{1,0:T(8,128)(2,1)S(1)}, bf16[136,288]{1,0:T(8,128)(2,1)S(1)}, bf16[408,432]{1,0:T(8,128)(2,1)S(1)}, bf16[96,432]{1,0:T(8,128)(2,1)S(1)}) custom-call(bf16[3,3,16,136]{3,2,1,0:T(8,128)(2,1)} %se_ref.1, bf16[3,3,8,136]{3,2,1,0:T(8,128)(2,1)} %bitcast.3, bf16[3,3,32,136]{3,2,1,0:T(8,128)(2,1)} %ae_ref.1, ...), custom_call_target="tpu_custom_call" | custom-call | flops 1000000 | bytes 4000000 | tf_op jit(solution)/shard_map/weights/pallas_call | solution.py:332
  14.0 0.0 collective-permute-done.3.refs_2_
  14.0 1.0 %collective-permute-done.2.refs_1_ = bf16[8,5376]{1,0:T(8,128)(2,1)S(1)} collective-permute-done((bf16[8,5376]{1,0:T(8,128)(2,1)S(1)}, bf16[8,5376]{1,0:T(8,128)(2,1)S(1)}, u32[]{:S(2)}, u32[]{:S(2)}) %collective-permute-start.2) | collective-permute-done | bytes 86048 | tf_op jit(solution)/shard_map/ppermute | solution.py:648
  15.0 1.9 %forecast_early.1 = (bf16[48,4608]{1,0:T(8,128)(2,1)S(1)}, bf16[144,4608]{1,0:T(8,128)(2,1)S(1)}, bf16[96,4608]{1,0:T(8,128)(2,1)S(1)}, bf16[144,4608]{1,0:T(8,1...) custom-call(bf16[8,5376]{1,0:T(8,128)(2,1)S(1)} %pack_got.1.refs_0_,, ...), custom_call_target="tpu_custom_call" | custom-call | flops 1000 | bytes 1000 | tf_op jit(solution)/shard_map/forecast_early/pallas_call | solution.py:576
  17.0 0.6 %collective-permute-done.1.refs_0_ = bf16[8,5376]{1,0:T(8,128)(2,1)S(1)} collective-permute-done((bf16[8,5376]{1,0:T(8,128)(2,1)S(1)}, bf16[8,5376]{1,0:T(8,128)(2,1)S(1)}, u32[]{:S(2)}, u32[]{:S(2)}) %collective-permute-start.1) | collective-permute-done | bytes 86048 | tf_op jit(solution)/shard_map/ppermute | solution.py:648
  17.6 0.0 copy-start
  17.6 6.1 %forecast_late.1 = (bf16[32,8,128]{2,1,0:T(8,128)(2,1)S(1)}, bf16[48,4608]{1,0:T(8,128)(2,1)S(1)}, bf16[144,4608]{1,0:T(8,128)(2,1)S(1)}, bf16[96,4608]{1,0:T(8,...) custom-call(bf16[8,5376]{1,0:T(8,128)(2,1)S(1)} %collective-permute-, ...), custom_call_target="tpu_custom_call", output_to_operand_aliasing={{1}: (6, {}), {2}: (7, {}), {3}: (8, {}), {4}: (9, {}), {5}... | custom-call | flops 2000000000 | bytes 3000000 | tf_op jit(solution)/shard_map/forecast_late/pallas_call | solution.py:585
  23.7 1.6 %collective-permute-start.4 = (bf16[32,8,128]{2,1,0:T(8,128)(2,1)S(1)}, bf16[32,8,128]{2,1,0:T(8,128)(2,1)S(1)}, u32[]{:S(2)}, u32[]{:S(2)}) collective-permute-start(bf16[32,8,128]{2,1,0:T(8,128)(2,1)S(1)} %get-tuple-element.31.made_ref), channel_id=1, source_target_pairs={{0,2},{2,0},{1,3},{3,1},{4,6},{6,4},{5,7},{7,5},{8,10},{10,8},{9,1... | collective-permute-start | bytes 196616 | tf_op jit(solution)/shard_map/ppermute | solution.py:652
  25.3 2.7 %collective-permute-done.4.other_ref = bf16[32,8,128]{2,1,0:T(8,128)(2,1)S(1)} collective-permute-done((bf16[32,8,128]{2,1,0:T(8,128)(2,1)S(1)}, bf16[32,8,128]{2,1,0:T(8,128)(2,1)S(1)}, u32[]{:S(2)}, u32[]{:S(2)}) %collective-permute-start.4) | collective-permute-done | bytes 65568 | tf_op jit(solution)/shard_map/ppermute | solution.py:652
  28.0 0.0 copy-done
  28.0 0.7 %merge.1 = (bf16[2,24,8,128]{3,2,1,0:T(8,128)(2,1)}, bf16[2,8,8,128]{3,2,1,0:T(8,128)(2,1)}) custom-call(bf16[32,8,128]{2,1,0:T(8,128)(2,1)S(1)} %get-tuple-element.31.made_ref, bf16[32,8,128]{2,1,0:T(8,128)(2,1)S(1)} %collective-permute-done.4.other_ref, bf16[2,24,8,128]{3,2,1,0:T(8,128)(2,1)S(1)} %copy-done), custom_call_target="tpu_custom_call" | custom-call | flops 1000000 | bytes 1000000 | tf_op jit(solution)/shard_map/merge/pallas_call | solution.py:653
Async XLA Ops:
  1.5 5.1 %collective-permute-start = (bf16[24,8,128]{2,1,0:T(8,128)(2,1)S(1)}, bf16[24,8,128]{2,1,0:T(8,128)(2,1)S(1)}, u32[]{:S(2)}, u32[]{:S(2)}) collective-permute-start(bf16[24,8,128]{2,1,0:T(8,128)(2,1)S(1)} %pick.1), channel_id=1, source_target_pairs={{0,2},{2,0},{1,3},{3,1},{4,6},{6,4},{5,7},{7,5},{8,10},{10,8},{9,1... | collective-permute-start | bytes 147464 | tf_op jit(solution)/shard_map/ppermute | solution.py:617
  6.7 7.2 %collective-permute-start.3 = (bf16[8,5376]{1,0:T(8,128)(2,1)S(1)}, bf16[8,5376]{1,0:T(8,128)(2,1)S(1)}, u32[]{:S(2)}, u32[]{:S(2)}) collective-permute-start(bf16[8,5376]{1,0:T(8,128)(2,1)S(1)} %pack_got.1.refs_0_), channel_id=1, source_target_pairs={{0,8},{4,12},{8,0},{12,4},{1,9},{5,13},{9,1},{13,5},{2,10},{6,14},... | collective-permute-start | bytes 258056 | tf_op jit(solution)/shard_map/ppermute | solution.py:648
  9.9 5.1 %collective-permute-start.2 = (bf16[8,5376]{1,0:T(8,128)(2,1)S(1)}, bf16[8,5376]{1,0:T(8,128)(2,1)S(1)}, u32[]{:S(2)}, u32[]{:S(2)}) collective-permute-start(bf16[8,5376]{1,0:T(8,128)(2,1)S(1)} %pack_got.1.refs_0_), channel_id=1, source_target_pairs={{0,12},{4,0},{8,4},{12,8},{1,13},{5,1},{9,5},{13,9},{2,14},{6,2},{... | collective-permute-start | bytes 258056 | tf_op jit(solution)/shard_map/ppermute | solution.py:648
  11.3 6.3 %collective-permute-start.1 = (bf16[8,5376]{1,0:T(8,128)(2,1)S(1)}, bf16[8,5376]{1,0:T(8,128)(2,1)S(1)}, u32[]{:S(2)}, u32[]{:S(2)}) collective-permute-start(bf16[8,5376]{1,0:T(8,128)(2,1)S(1)} %pack_got.1.refs_0_), channel_id=1, source_target_pairs={{0,4},{4,8},{8,12},{12,0},{1,5},{5,9},{9,13},{13,1},{2,6},{6,10},{... | collective-permute-start | bytes 258056 | tf_op jit(solution)/shard_map/ppermute | solution.py:648
  17.6 10.5 %copy-start = (bf16[2,24,8,128]{3,2,1,0:T(8,128)(2,1)S(1)}, bf16[2,24,8,128]{3,2,1,0:T(8,128)(2,1)}, u32[]{:S(2)}) copy-start(bf16[2,24,8,128]{3,2,1,0:T(8,128)(2,1)} %air_ref.5) | copy-start | bytes 294916
  23.7 4.3 %collective-permute-start.4 = (bf16[32,8,128]{2,1,0:T(8,128)(2,1)S(1)}, bf16[32,8,128]{2,1,0:T(8,128)(2,1)S(1)}, u32[]{:S(2)}, u32[]{:S(2)}) collective-permute-start(bf16[32,8,128]{2,1,0:T(8,128)(2,1)S(1)} %get-tuple-element.31.made_ref), channel_id=1, source_target_pairs={{0,2},{2,0},{1,3},{3,1},{4,6},{6,4},{5,7},{7,5},{8,10},{10,8},{9,1... | collective-permute-start | bytes 196616 | tf_op jit(solution)/shard_map/ppermute | solution.py:652

commit v8 on v7

--- a/solution.py
+++ b/solution.py
@@ -222,12 +222,6 @@
     return tuple(pltpu.with_memory_space_constraint(value, pltpu.VMEM) for value in values)
 
 
-def pick_kernel(air_ref, out_ref, done):
-    copy = pltpu.make_async_copy(air_ref.at[1 - lax.axis_index("sec")], out_ref, done)
-    copy.start()
-    copy.wait()
-
-
 def tile(group, rows, row):
     return pl.ds((group * rows + row) * LANES, LANES)
 
@@ -266,11 +260,12 @@
 
 
 def pack_got_kernel(own_ref, got_ref, out_ref, planes):
-    fields, rows = got_ref.shape[:2]
+    fields, rows = got_ref.shape[1:3]
     groups = fields // SUBLANES
     last = own_ref.shape[1] - LANES
-    first = lax.axis_index("sec") == 0
-    planes[...] = got_ref[...].astype(jnp.float32)
+    section = lax.axis_index("sec")
+    first = section == 0
+    planes[...] = got_ref[section].astype(jnp.float32)
     bands = [planes[:, row, :] for row in range(rows)]
     air = groups * rows * LANES
     out_ref[:, air:last] = own_ref[:, air:last]
@@ -388,7 +383,7 @@
 LATE_LOAD = -1
 HELD = 9
 VMEM_GRANT = 24 * 1024 * 1024
-PADS = {"sea_in": 2, "sea_hid": 2, "air_in": 2, "hid1": 2, "hid2": 4}
+PADS = {"sea_in": 2, "sea_hid": 2, "air_in": 2, "hid1": 2, "hid2": 6}
 
 
 def forecast_kernel(sizes, stage, *refs):
@@ -546,7 +541,7 @@
         add(base + 2, *reach(7), sea_exit, ("sea_hid", "sea_now", "air_now"), ("sea_now", "air_in"), 1)
         add(base + 3, *reach(6), air_entry, ("air_in",), ("hid1",), 1)
         add(base + 4, *reach(4), air_middle, ("hid1",), ("hid2",), 2)
-        low, high = (rows, 2 * rows) if last else (rows - 10, 2 * rows + 10)
+        low, high = (rows, 2 * rows) if last else (rows - 9, 2 * rows + 9)
         writes = ("planes",) if last else ("air_now", "sea_in")
         body = functools.partial(air_exit, last=last)
         add(base + 5, low, high, body, ("hid2", "air_now", "sea_now"), writes, 4)
@@ -606,15 +601,7 @@
     swap = [(0, 1), (1, 0)]
     bf16, f32 = jnp.bfloat16, jnp.float32
 
-    sent = pl.pallas_call(
-        pick_kernel,
-        out_shape=pltpu.VMEM(atmosphere.shape[1:], bf16),
-        in_specs=[pl.BlockSpec(memory_space=pl.ANY)],
-        out_specs=vmem_specs(1)[0],
-        scratch_shapes=[pltpu.SemaphoreType.DMA(())],
-        name="pick",
-    )(atmosphere)
-    got = lax.ppermute(sent, "sec", swap)
+    got = lax.ppermute(atmosphere, "sec", swap)
     packed_shape = pltpu.VMEM((SUBLANES, (kept // SUBLANES * rows + 2) * LANES), bf16)
     small = pl.CostEstimate(flops=1000000, bytes_accessed=1000000, transcendentals=0)
     own = pl.pallas_call(
@@ -676,7 +663,7 @@
         and ocean_state.shape[3] == band
         and rows == SUBLANES
         and atmosphere.shape[1] <= LANES
-        and 2 * rows + 10 <= blocks * rows
+        and 2 * rows + 9 <= blocks * rows
         and blocks * rows <= 64
         and all(c % SUBLANES == 0 for c in (fields, surface, flux_count, sea_entry.shape[3]))
         and (surface + flux_count) % PACKED == 0

time: 28.9 us -> 28.7 us (level)
  waiting for transfers between devices: 5.2 us -> 6.14 us
  Pallas kernels: 12.9 us -> 12.1 us
    ppermute x1, waiting for transfers between devices: 0.87 us -> 1.79 us  [belt_shards(): got = lax.ppermute(atmosphere, 'sec', swap)]
    pallas_call x1 -> x0, Pallas kernels: 0.82 us -> none  [belt_shards(): pl.pallas_call(pick_kernel, out_shape=pltpu.VMEM(atmosphere.shape[1:], bf...]
  transfers between devices with their start and end apart: 5 -> 5, of which waited for: 4 -> 5; matrix products, arithmetic and copies ran while one was open for 0% -> 0% of each run, Pallas kernels for 18% -> 18%
where the time goes in v8:
time: 28.7 us; the launch traced here: 28.5 us
  Pallas kernels  12.1 us (42%)
  starting transfers between devices  9.65 us (34%)
  waiting for transfers between devices  6.14 us (21%)
  between operations  0.66 us (2%)
    pallas_call x1, Pallas kernels, forecast(): pl.pallas_call(functools.partial(forecast_kernel, sizes, 1), out_shape=(p...  6.04 us
    ppermute x3, starting transfers between devices, belt_shards(): frame[index] = lax.ppermute(packed, 'sp', pairs)  5.01 us
    ppermute x1, starting transfers between devices, belt_shards(): got = lax.ppermute(atmosphere, 'sec', swap)  3.03 us
    ppermute x1, waiting for transfers between devices, belt_shards(): other = lax.ppermute(made, 'sec', swap)  2.72 us
    pallas_call x1, Pallas kernels, prepare_weights(): pl.pallas_call(weights_kernel, out_shape=(pltpu.VMEM((hidden, 9 * sea_ent...  2.01 us
    pallas_call x1, Pallas kernels, forecast(): pl.pallas_call(functools.partial(forecast_kernel, sizes, 0), out_shape=tu...  1.94 us
    ppermute x1, waiting for transfers between devices, belt_shards(): got = lax.ppermute(atmosphere, 'sec', swap)  1.79 us
    ppermute x3, waiting for transfers between devices, belt_shards(): frame[index] = lax.ppermute(packed, 'sp', pairs)  1.63 us
  transfers between devices with their start and end apart: 5, of which 5 were waited for; matrix products, arithmetic and copies ran while one was open for 0% of the time, Pallas kernels for 18%

profile of v8, /device:TPU:0, one launch (start us, length us, event | category | flops | bytes accessed | tf_op | source)
XLA Modules:
  0.0 28.5 jit_solution(14261541964450341036)
XLA Ops:
  0.6 3.0 %collective-permute-start = (bf16[2,24,8,128]{3,2,1,0:T(8,128)(2,1)}, bf16[2,24,8,128]{3,2,1,0:T(8,128)(2,1)S(1)}, u32[]{:S(2)}, u32[]{:S(2)}) collective-permute-start(bf16[2,24,8,128]{3,2,1,0:T(8,128)(2,1)} %air_ref.3), channel_id=1, source_target_pairs={{0,2},{2,0},{1,3},{3,1},{4,6},{6,4},{5,7},{7,5},{8,10},{10,8},{9,1... | collective-permute-start | bytes 294920 | tf_op jit(solution)/shard_map/ppermute | solution.py:604
  3.7 1.2 %pack_own.1.own_ref = bf16[8,5376]{1,0:T(8,128)(2,1)S(1)} custom-call(bf16[2,24,8,128]{3,2,1,0:T(8,128)(2,1)} %air_ref.3, bf16[2,8,8,128]{3,2,1,0:T(8,128)(2,1)} %sea_ref.1, bf16[2,8,8,128]{3,2,1,0:T(8,128)(2,1)} %flux_ref.1, s32[8,128]{1,0:T(8,128)} %mask_ref.1), custom_call_target="tpu_custom_call" | custom-call | flops 1000000 | bytes 1000000 | tf_op jit(solution)/shard_map/pack_own/pallas_call | solution.py:607
  4.9 1.8 %collective-permute-done.got_ref = bf16[2,24,8,128]{3,2,1,0:T(8,128)(2,1)S(1)} collective-permute-done((bf16[2,24,8,128]{3,2,1,0:T(8,128)(2,1)}, bf16[2,24,8,128]{3,2,1,0:T(8,128)(2,1)S(1)}, u32[]{:S(2)}, u32[]{:S(2)}) %collective-permute-start) | collective-permute-done | bytes 98336 | tf_op jit(solution)/shard_map/ppermute | solution.py:604
  6.7 0.2 pack_got.1.refs_0_
  6.8 3.0 %collective-permute-start.3 = (bf16[8,5376]{1,0:T(8,128)(2,1)S(1)}, bf16[8,5376]{1,0:T(8,128)(2,1)S(1)}, u32[]{:S(2)}, u32[]{:S(2)}) collective-permute-start(bf16[8,5376]{1,0:T(8,128)(2,1)S(1)} %pack_got.1.refs_0_), channel_id=1, source_target_pairs={{0,8},{4,12},{8,0},{12,4},{1,9},{5,13},{9,1},{13,5},{2,10},{6,14},... | collective-permute-start | bytes 258056 | tf_op jit(solution)/shard_map/ppermute | solution.py:635
  9.8 1.3 %collective-permute-start.2 = (bf16[8,5376]{1,0:T(8,128)(2,1)S(1)}, bf16[8,5376]{1,0:T(8,128)(2,1)S(1)}, u32[]{:S(2)}, u32[]{:S(2)}) collective-permute-start(bf16[8,5376]{1,0:T(8,128)(2,1)S(1)} %pack_got.1.refs_0_), channel_id=1, source_target_pairs={{0,12},{4,0},{8,4},{12,8},{1,13},{5,1},{9,5},{13,9},{2,14},{6,2},{... | collective-permute-start | bytes 258056 | tf_op jit(solution)/shard_map/ppermute | solution.py:635
  11.2 0.7 %collective-permute-start.1 = (bf16[8,5376]{1,0:T(8,128)(2,1)S(1)}, bf16[8,5376]{1,0:T(8,128)(2,1)S(1)}, u32[]{:S(2)}, u32[]{:S(2)}) collective-permute-start(bf16[8,5376]{1,0:T(8,128)(2,1)S(1)} %pack_got.1.refs_0_), channel_id=1, source_target_pairs={{0,4},{4,8},{8,12},{12,0},{1,5},{5,9},{9,13},{13,1},{2,6},{6,10},{... | collective-permute-start | bytes 258056 | tf_op jit(solution)/shard_map/ppermute | solution.py:635
  11.9 2.0 %weights.1 = (bf16[136,144]{1,0:T(8,128)(2,1)S(1)}, bf16[24,432]{1,0:T(8,128)(2,1)S(1)}, bf16[136,288]{1,0:T(8,128)(2,1)S(1)}, bf16[408,432]{1,0:T(8,128)(2,1)S(1)}, bf16[96,432]{1,0:T(8,128)(2,1)S(1)}) custom-call(bf16[3,3,16,136]{3,2,1,0:T(8,128)(2,1)} %se_ref.1, bf16[3,3,8,136]{3,2,1,0:T(8,128)(2,1)} %bitcast.3, bf16[3,3,32,136]{3,2,1,0:T(8,128)(2,1)} %ae_ref.1, ...), custom_call_target="tpu_custom_call" | custom-call | flops 1000000 | bytes 4000000 | tf_op jit(solution)/shard_map/weights/pallas_call | solution.py:327
  13.9 0.3 %collective-permute-done.3.refs_2_ = bf16[8,5376]{1,0:T(8,128)(2,1)S(1)} collective-permute-done((bf16[8,5376]{1,0:T(8,128)(2,1)S(1)}, bf16[8,5376]{1,0:T(8,128)(2,1)S(1)}, u32[]{:S(2)}, u32[]{:S(2)}) %collective-permute-start.3) | collective-permute-done | bytes 86048 | tf_op jit(solution)/shard_map/ppermute | solution.py:635
  14.2 0.9 %collective-permute-done.2.refs_1_ = bf16[8,5376]{1,0:T(8,128)(2,1)S(1)} collective-permute-done((bf16[8,5376]{1,0:T(8,128)(2,1)S(1)}, bf16[8,5376]{1,0:T(8,128)(2,1)S(1)}, u32[]{:S(2)}, u32[]{:S(2)}) %collective-permute-start.2) | collective-permute-done | bytes 86048 | tf_op jit(solution)/shard_map/ppermute | solution.py:635
  15.1 1.9 %forecast_early.1 = (bf16[48,4608]{1,0:T(8,128)(2,1)S(1)}, bf16[144,4608]{1,0:T(8,128)(2,1)S(1)}, bf16[96,4608]{1,0:T(8,128)(2,1)S(1)}, bf16[144,4608]{1,0:T(8,1...) custom-call(bf16[8,5376]{1,0:T(8,128)(2,1)S(1)} %pack_got.1.refs_0_,, ...), custom_call_target="tpu_custom_call" | custom-call | flops 1000 | bytes 1000 | tf_op jit(solution)/shard_map/forecast_early/pallas_call | solution.py:571
  17.1 0.4 %collective-permute-done.1.refs_0_ = bf16[8,5376]{1,0:T(8,128)(2,1)S(1)} collective-permute-done((bf16[8,5376]{1,0:T(8,128)(2,1)S(1)}, bf16[8,5376]{1,0:T(8,128)(2,1)S(1)}, u32[]{:S(2)}, u32[]{:S(2)}) %collective-permute-start.1) | collective-permute-done | bytes 86048 | tf_op jit(solution)/shard_map/ppermute | solution.py:635
  17.5 0.0 copy-start
  17.5 6.0 %forecast_late.1 = (bf16[32,8,128]{2,1,0:T(8,128)(2,1)S(1)}, bf16[48,4608]{1,0:T(8,128)(2,1)S(1)}, bf16[144,4608]{1,0:T(8,128)(2,1)S(1)}, bf16[96,4608]{1,0:T(8,...) custom-call(bf16[8,5376]{1,0:T(8,128)(2,1)S(1)} %collective-permute-, ...), custom_call_target="tpu_custom_call", output_to_operand_aliasing={{1}: (6, {}), {2}: (7, {}), {3}: (8, {}), {4}: (9, {}), {5}... | custom-call | flops 2000000000 | bytes 3000000 | tf_op jit(solution)/shard_map/forecast_late/pallas_call | solution.py:580
  23.5 1.6 %collective-permute-start.4 = (bf16[32,8,128]{2,1,0:T(8,128)(2,1)S(1)}, bf16[32,8,128]{2,1,0:T(8,128)(2,1)S(1)}, u32[]{:S(2)}, u32[]{:S(2)}) collective-permute-start(bf16[32,8,128]{2,1,0:T(8,128)(2,1)S(1)} %get-tuple-element.31.made_ref), channel_id=1, source_target_pairs={{0,2},{2,0},{1,3},{3,1},{4,6},{6,4},{5,7},{7,5},{8,10},{10,8},{9,1... | collective-permute-start | bytes 196616 | tf_op jit(solution)/shard_map/ppermute | solution.py:639
  25.1 2.7 %collective-permute-done.4.other_ref = bf16[32,8,128]{2,1,0:T(8,128)(2,1)S(1)} collective-permute-done((bf16[32,8,128]{2,1,0:T(8,128)(2,1)S(1)}, bf16[32,8,128]{2,1,0:T(8,128)(2,1)S(1)}, u32[]{:S(2)}, u32[]{:S(2)}) %collective-permute-start.4) | collective-permute-done | bytes 65568 | tf_op jit(solution)/shard_map/ppermute | solution.py:639
  27.8 0.0 copy-done
  27.8 0.7 %merge.1 = (bf16[2,24,8,128]{3,2,1,0:T(8,128)(2,1)}, bf16[2,8,8,128]{3,2,1,0:T(8,128)(2,1)}) custom-call(bf16[32,8,128]{2,1,0:T(8,128)(2,1)S(1)} %get-tuple-element.31.made_ref, bf16[32,8,128]{2,1,0:T(8,128)(2,1)S(1)} %collective-permute-done.4.other_ref, bf16[2,24,8,128]{3,2,1,0:T(8,128)(2,1)S(1)} %copy-done), custom_call_target="tpu_custom_call" | custom-call | flops 1000000 | bytes 1000000 | tf_op jit(solution)/shard_map/merge/pallas_call | solution.py:640
Async XLA Ops:
  0.6 6.0 %collective-permute-start = (bf16[2,24,8,128]{3,2,1,0:T(8,128)(2,1)}, bf16[2,24,8,128]{3,2,1,0:T(8,128)(2,1)S(1)}, u32[]{:S(2)}, u32[]{:S(2)}) collective-permute-start(bf16[2,24,8,128]{3,2,1,0:T(8,128)(2,1)} %air_ref.3), channel_id=1, source_target_pairs={{0,2},{2,0},{1,3},{3,1},{4,6},{6,4},{5,7},{7,5},{8,10},{10,8},{9,1... | collective-permute-start | bytes 294920 | tf_op jit(solution)/shard_map/ppermute | solution.py:604
  6.8 7.3 %collective-permute-start.3 = (bf16[8,5376]{1,0:T(8,128)(2,1)S(1)}, bf16[8,5376]{1,0:T(8,128)(2,1)S(1)}, u32[]{:S(2)}, u32[]{:S(2)}) collective-permute-start(bf16[8,5376]{1,0:T(8,128)(2,1)S(1)} %pack_got.1.refs_0_), channel_id=1, source_target_pairs={{0,8},{4,12},{8,0},{12,4},{1,9},{5,13},{9,1},{13,5},{2,10},{6,14},... | collective-permute-start | bytes 258056 | tf_op jit(solution)/shard_map/ppermute | solution.py:635
  9.8 5.3 %collective-permute-start.2 = (bf16[8,5376]{1,0:T(8,128)(2,1)S(1)}, bf16[8,5376]{1,0:T(8,128)(2,1)S(1)}, u32[]{:S(2)}, u32[]{:S(2)}) collective-permute-start(bf16[8,5376]{1,0:T(8,128)(2,1)S(1)} %pack_got.1.refs_0_), channel_id=1, source_target_pairs={{0,12},{4,0},{8,4},{12,8},{1,13},{5,1},{9,5},{13,9},{2,14},{6,2},{... | collective-permute-start | bytes 258056 | tf_op jit(solution)/shard_map/ppermute | solution.py:635
  11.2 6.3 %collective-permute-start.1 = (bf16[8,5376]{1,0:T(8,128)(2,1)S(1)}, bf16[8,5376]{1,0:T(8,128)(2,1)S(1)}, u32[]{:S(2)}, u32[]{:S(2)}) collective-permute-start(bf16[8,5376]{1,0:T(8,128)(2,1)S(1)} %pack_got.1.refs_0_), channel_id=1, source_target_pairs={{0,4},{4,8},{8,12},{12,0},{1,5},{5,9},{9,13},{13,1},{2,6},{6,10},{... | collective-permute-start | bytes 258056 | tf_op jit(solution)/shard_map/ppermute | solution.py:635
  17.5 10.4 %copy-start = (bf16[2,24,8,128]{3,2,1,0:T(8,128)(2,1)S(1)}, bf16[2,24,8,128]{3,2,1,0:T(8,128)(2,1)}, u32[]{:S(2)}) copy-start(bf16[2,24,8,128]{3,2,1,0:T(8,128)(2,1)} %air_ref.3) | copy-start | bytes 294916
  23.5 4.3 %collective-permute-start.4 = (bf16[32,8,128]{2,1,0:T(8,128)(2,1)S(1)}, bf16[32,8,128]{2,1,0:T(8,128)(2,1)S(1)}, u32[]{:S(2)}, u32[]{:S(2)}) collective-permute-start(bf16[32,8,128]{2,1,0:T(8,128)(2,1)S(1)} %get-tuple-element.31.made_ref), channel_id=1, source_target_pairs={{0,2},{2,0},{1,3},{3,1},{4,6},{6,4},{5,7},{7,5},{8,10},{10,8},{9,1... | collective-permute-start | bytes 196616 | tf_op jit(solution)/shard_map/ppermute | solution.py:639

commit v9 on v8

--- a/solution.py
+++ b/solution.py
@@ -308,7 +308,15 @@
             source[a, b].astype(jnp.float32).T for a in range(3) for b in range(3)
         ]
         target[...] = jnp.concatenate(taps, axis=1).astype(jnp.bfloat16)
-    for source, target, turned in ((sx_ref, sx_out, True), (am_ref, am_out, False), (ax_ref, ax_out, True)):
+    surface, depth = sx_ref.shape[2:]
+    blank = jnp.zeros((surface, sx_out.shape[1] - depth), jnp.float32)
+    rows = []
+    for a in range(3):
+        for b in range(3):
+            tap = 0.5 * sx_ref[a, b].astype(jnp.float32)
+            rows.append(jnp.concatenate([tap, blank], axis=1) if blank.shape[1] else tap)
+    sx_out[...] = jnp.concatenate(rows, axis=0).astype(jnp.bfloat16)
+    for source, target, turned in ((am_ref, am_out, False), (ax_ref, ax_out, True)):
         width, depth = source.shape[2:] if turned else source.shape[:1:-1]
         blank = jnp.zeros((width, pad_to(depth, PACKED) - depth), jnp.float32)
         groups = []
@@ -328,7 +336,7 @@
         weights_kernel,
         out_shape=(
             pltpu.VMEM((hidden, 9 * sea_entry.shape[2]), jnp.bfloat16),
-            pltpu.VMEM((3 * surface, 3 * hidden_rows), jnp.bfloat16),
+            pltpu.VMEM((9 * surface, hidden_rows), jnp.bfloat16),
             pltpu.VMEM((hidden, 9 * air_entry.shape[2]), jnp.bfloat16),
             pltpu.VMEM((3 * hidden, 3 * hidden_rows), jnp.bfloat16),
             pltpu.VMEM((3 * produced, 3 * hidden_rows), jnp.bfloat16),
@@ -378,12 +386,12 @@
 
 
 CHUNK = 2
-LAG = 20
+LAG = 28
 LOAD = 0
 LATE_LOAD = -1
-HELD = 9
+HELD = 10
 VMEM_GRANT = 24 * 1024 * 1024
-PADS = {"sea_in": 2, "sea_hid": 2, "air_in": 2, "hid1": 2, "hid2": 6}
+PADS = {"sea_in": 2, "sea_hid": 2, "air_in": 2, "hid1": 2, "hid2": 6, "sea_taps": 2}
 
 
 def forecast_kernel(sizes, stage, *refs):
@@ -395,8 +403,8 @@
     if stage:
         out_ref, planes = rest[HELD], rest[-1]
         rest = rest[HELD + 1 : -1]
-    held = dict(zip(("sea_in", "sea_hid", "air_in", "hid1", "hid2"), rest, strict=False))
-    air_now, sea_now, edge_in, mask_in = rest[5:]
+    held = dict(zip(("sea_in", "sea_hid", "air_in", "hid1", "hid2", "sea_taps"), rest, strict=False))
+    air_now, sea_now, edge_in, mask_in = rest[6:]
     ring = blocks * rows
     kept = fields + surface + flux_count
     hidden_pad = held["sea_hid"].shape[0] - hidden
@@ -453,11 +461,22 @@
     def sea_entry(row, count):
         put_hidden("sea_hid", row, count, product(se_ref, gather_rows("sea_in", row, count, 1)))
 
+    def sea_taps(row, count):
+        hidden_rows = held["sea_hid"][:, span(row % ring + PADS["sea_hid"], count)]
+        put("sea_taps", row, count, product(sx_ref, hidden_rows))
+
     def sea_exit(row, count):
-        made = product(sx_ref, gather_rows("sea_hid", row, count, 1))
         for i in range(count):
             at = (row + i) % ring
-            change = side_sum(made, surface, 1, i)
+            sides = []
+            for b in range(3):
+                parts = []
+                for a in range(3):
+                    low = (3 * a + b) * surface
+                    place = span(at + a - 1 + PADS["sea_taps"], 1)
+                    parts.append(held["sea_taps"][low : low + surface, place])
+                sides.append(parts[0] + parts[1] + parts[2])
+            change = sides[1] + from_left(sides[0], 1) + from_right(sides[2], 1)
             old = sea_now[:, span(at, 1)]
             new = (old + mask_in[at : at + 1, :] * change).astype(jnp.bfloat16).astype(jnp.float32)
             sea_now[:, span(at, 1)] = new
@@ -538,7 +557,8 @@
             return (rows - halo, 2 * rows + halo) if last else (0, ring)
 
         add(base + 1, *reach(8), sea_entry, ("sea_in",), ("sea_hid",), 1)
-        add(base + 2, *reach(7), sea_exit, ("sea_hid", "sea_now", "air_now"), ("sea_now", "air_in"), 1)
+        add(base + 1, *reach(8), sea_taps, ("sea_hid",), ("sea_taps",), 0)
+        add(base + 2, *reach(7), sea_exit, ("sea_taps", "sea_now", "air_now"), ("sea_now", "air_in"), 1)
         add(base + 3, *reach(6), air_entry, ("air_in",), ("hid1",), 1)
         add(base + 4, *reach(4), air_middle, ("hid1",), ("hid2",), 2)
         low, high = (rows, 2 * rows) if last else (rows - 9, 2 * rows + 9)
@@ -564,6 +584,8 @@
         ("hid2", hidden_rows),
     ):
         held.append(pltpu.VMEM((depth, (ring + 2 * PADS[name]) * LANES), jnp.bfloat16))
+    wide = (ring + 2 * PADS["sea_taps"]) * LANES
+    held.append(pltpu.VMEM((9 * surface, wide), jnp.float32))
     for depth in (fields, surface, fields):
         held.append(pltpu.VMEM((depth, ring * LANES), jnp.float32))
     held.append(pltpu.VMEM((ring, LANES), jnp.float32))

time: 28.7 us -> 28.7 us (level)
  no operation moved by 1% of the time
where the time goes in v9:
time: 28.7 us; the launch traced here: 28.5 us
  Pallas kernels  12.1 us (42%)
  starting transfers between devices  9.71 us (34%)
  waiting for transfers between devices  6.03 us (21%)
  between operations  0.66 us (2%)
    pallas_call x1, Pallas kernels, forecast(): pl.pallas_call(functools.partial(forecast_kernel, sizes, 1), out_shape=(p...  6.01 us
    ppermute x3, starting transfers between devices, belt_shards(): frame[index] = lax.ppermute(packed, 'sp', pairs)  5.01 us
    ppermute x1, starting transfers between devices, belt_shards(): got = lax.ppermute(atmosphere, 'sec', swap)  3.03 us
    ppermute x1, waiting for transfers between devices, belt_shards(): other = lax.ppermute(made, 'sec', swap)  2.67 us
    pallas_call x1, Pallas kernels, prepare_weights(): pl.pallas_call(weights_kernel, out_shape=(pltpu.VMEM((hidden, 9 * sea_ent...  2 us
    pallas_call x1, Pallas kernels, forecast(): pl.pallas_call(functools.partial(forecast_kernel, sizes, 0), out_shape=tu...  2 us
    ppermute x1, waiting for transfers between devices, belt_shards(): got = lax.ppermute(atmosphere, 'sec', swap)  1.79 us
    ppermute x1, starting transfers between devices, belt_shards(): other = lax.ppermute(made, 'sec', swap)  1.66 us
  transfers between devices with their start and end apart: 5, of which 5 were waited for; matrix products, arithmetic and copies ran while one was open for 0% of the time, Pallas kernels for 18%

profile of v9, /device:TPU:0, one launch (start us, length us, event | category | flops | bytes accessed | tf_op | source)
XLA Modules:
  0.0 28.5 jit_solution(151548653806742862)
XLA Ops:
  0.6 3.0 %collective-permute-start = (bf16[2,24,8,128]{3,2,1,0:T(8,128)(2,1)}, bf16[2,24,8,128]{3,2,1,0:T(8,128)(2,1)S(1)}, u32[]{:S(2)}, u32[]{:S(2)}) collective-permute-start(bf16[2,24,8,128]{3,2,1,0:T(8,128)(2,1)} %air_ref.3), channel_id=1, source_target_pairs={{0,2},{2,0},{1,3},{3,1},{4,6},{6,4},{5,7},{7,5},{8,10},{10,8},{9,1... | collective-permute-start | bytes 294920 | tf_op jit(solution)/shard_map/ppermute | solution.py:626
  3.7 1.2 %pack_own.1.own_ref = bf16[8,5376]{1,0:T(8,128)(2,1)S(1)} custom-call(bf16[2,24,8,128]{3,2,1,0:T(8,128)(2,1)} %air_ref.3, bf16[2,8,8,128]{3,2,1,0:T(8,128)(2,1)} %sea_ref.1, bf16[2,8,8,128]{3,2,1,0:T(8,128)(2,1)} %flux_ref.1, s32[8,128]{1,0:T(8,128)} %mask_ref.1), custom_call_target="tpu_custom_call" | custom-call | flops 1000000 | bytes 1000000 | tf_op jit(solution)/shard_map/pack_own/pallas_call | solution.py:629
  4.9 1.8 %collective-permute-done.got_ref = bf16[2,24,8,128]{3,2,1,0:T(8,128)(2,1)S(1)} collective-permute-done((bf16[2,24,8,128]{3,2,1,0:T(8,128)(2,1)}, bf16[2,24,8,128]{3,2,1,0:T(8,128)(2,1)S(1)}, u32[]{:S(2)}, u32[]{:S(2)}) %collective-permute-start) | collective-permute-done | bytes 98336 | tf_op jit(solution)/shard_map/ppermute | solution.py:626
  6.7 0.2 pack_got.1.refs_0_
  6.8 3.0 %collective-permute-start.3 = (bf16[8,5376]{1,0:T(8,128)(2,1)S(1)}, bf16[8,5376]{1,0:T(8,128)(2,1)S(1)}, u32[]{:S(2)}, u32[]{:S(2)}) collective-permute-start(bf16[8,5376]{1,0:T(8,128)(2,1)S(1)} %pack_got.1.refs_0_), channel_id=1, source_target_pairs={{0,8},{4,12},{8,0},{12,4},{1,9},{5,13},{9,1},{13,5},{2,10},{6,14},... | collective-permute-start | bytes 258056 | tf_op jit(solution)/shard_map/ppermute | solution.py:657
  9.8 1.3 %collective-permute-start.2 = (bf16[8,5376]{1,0:T(8,128)(2,1)S(1)}, bf16[8,5376]{1,0:T(8,128)(2,1)S(1)}, u32[]{:S(2)}, u32[]{:S(2)}) collective-permute-start(bf16[8,5376]{1,0:T(8,128)(2,1)S(1)} %pack_got.1.refs_0_), channel_id=1, source_target_pairs={{0,12},{4,0},{8,4},{12,8},{1,13},{5,1},{9,5},{13,9},{2,14},{6,2},{... | collective-permute-start | bytes 258056 | tf_op jit(solution)/shard_map/ppermute | solution.py:657
  11.2 0.7 %collective-permute-start.1 = (bf16[8,5376]{1,0:T(8,128)(2,1)S(1)}, bf16[8,5376]{1,0:T(8,128)(2,1)S(1)}, u32[]{:S(2)}, u32[]{:S(2)}) collective-permute-start(bf16[8,5376]{1,0:T(8,128)(2,1)S(1)} %pack_got.1.refs_0_), channel_id=1, source_target_pairs={{0,4},{4,8},{8,12},{12,0},{1,5},{5,9},{9,13},{13,1},{2,6},{6,10},{... | collective-permute-start | bytes 258056 | tf_op jit(solution)/shard_map/ppermute | solution.py:657
  11.9 2.0 %weights.1 = (bf16[136,144]{1,0:T(8,128)(2,1)S(1)}, bf16[72,144]{1,0:T(8,128)(2,1)S(1)}, bf16[136,288]{1,0:T(8,128)(2,1)S(1)}, bf16[408,432]{1,0:T(8,128)(2,1)S(1)}, bf16[96,432]{1,0:T(8,128)(2,1)S(1)}) custom-call(bf16[3,3,16,136]{3,2,1,0:T(8,128)(2,1)} %se_ref.1, bf16[3,3,8,136]{3,2,1,0:T(8,128)(2,1)} %bitcast.3, bf16[3,3,32,136]{3,2,1,0:T(8,128)(2,1)} %ae_ref.1, ...), custom_call_target="tpu_custom_call" | custom-call | flops 1000000 | bytes 4000000 | tf_op jit(solution)/shard_map/weights/pallas_call | solution.py:335
  13.9 0.3 %collective-permute-done.3.refs_2_ = bf16[8,5376]{1,0:T(8,128)(2,1)S(1)} collective-permute-done((bf16[8,5376]{1,0:T(8,128)(2,1)S(1)}, bf16[8,5376]{1,0:T(8,128)(2,1)S(1)}, u32[]{:S(2)}, u32[]{:S(2)}) %collective-permute-start.3) | collective-permute-done | bytes 86048 | tf_op jit(solution)/shard_map/ppermute | solution.py:657
  14.2 0.9 %collective-permute-done.2.refs_1_ = bf16[8,5376]{1,0:T(8,128)(2,1)S(1)} collective-permute-done((bf16[8,5376]{1,0:T(8,128)(2,1)S(1)}, bf16[8,5376]{1,0:T(8,128)(2,1)S(1)}, u32[]{:S(2)}, u32[]{:S(2)}) %collective-permute-start.2) | collective-permute-done | bytes 86048 | tf_op jit(solution)/shard_map/ppermute | solution.py:657
  15.1 2.0 %forecast_early.1 = (bf16[48,4608]{1,0:T(8,128)(2,1)S(1)}, bf16[144,4608]{1,0:T(8,128)(2,1)S(1)}, bf16[96,4608]{1,0:T(8,128)(2,1)S(1)}, bf16[144,4608]{1,0:T(8,1...) custom-call(bf16[8,5376]{1,0:T(8,128)(2,1)S(1)} %pack_got.1.refs_0_,, ...), custom_call_target="tpu_custom_call" | custom-call | flops 1000 | bytes 1000 | tf_op jit(solution)/shard_map/forecast_early/pallas_call | solution.py:593
  17.1 0.3 %collective-permute-done.1.refs_0_ = bf16[8,5376]{1,0:T(8,128)(2,1)S(1)} collective-permute-done((bf16[8,5376]{1,0:T(8,128)(2,1)S(1)}, bf16[8,5376]{1,0:T(8,128)(2,1)S(1)}, u32[]{:S(2)}, u32[]{:S(2)}) %collective-permute-start.1) | collective-permute-done | bytes 86048 | tf_op jit(solution)/shard_map/ppermute | solution.py:657
  17.5 0.0 copy-start
  17.5 6.0 %forecast_late.1 = (bf16[32,8,128]{2,1,0:T(8,128)(2,1)S(1)}, bf16[48,4608]{1,0:T(8,128)(2,1)S(1)}, bf16[144,4608]{1,0:T(8,128)(2,1)S(1)}, bf16[96,4608]{1,0:T(8,...) custom-call(bf16[8,5376]{1,0:T(8,128)(2,1)S(1)} %collective-permute-, ...), custom_call_target="tpu_custom_call", output_to_operand_aliasing={{1}: (6, {}), {2}: (7, {}), {3}: (8, {}), {4}: (9, {}), {5}... | custom-call | flops 2000000000 | bytes 3000000 | tf_op jit(solution)/shard_map/forecast_late/pallas_call | solution.py:602
  23.5 1.7 %collective-permute-start.4 = (bf16[32,8,128]{2,1,0:T(8,128)(2,1)S(1)}, bf16[32,8,128]{2,1,0:T(8,128)(2,1)S(1)}, u32[]{:S(2)}, u32[]{:S(2)}) collective-permute-start(bf16[32,8,128]{2,1,0:T(8,128)(2,1)S(1)} %get-tuple-element.33.made_ref), channel_id=1, source_target_pairs={{0,2},{2,0},{1,3},{3,1},{4,6},{6,4},{5,7},{7,5},{8,10},{10,8},{9,1... | collective-permute-start | bytes 196616 | tf_op jit(solution)/shard_map/ppermute | solution.py:661
  25.2 2.7 %collective-permute-done.4.other_ref = bf16[32,8,128]{2,1,0:T(8,128)(2,1)S(1)} collective-permute-done((bf16[32,8,128]{2,1,0:T(8,128)(2,1)S(1)}, bf16[32,8,128]{2,1,0:T(8,128)(2,1)S(1)}, u32[]{:S(2)}, u32[]{:S(2)}) %collective-permute-start.4) | collective-permute-done | bytes 65568 | tf_op jit(solution)/shard_map/ppermute | solution.py:661
  27.8 0.0 copy-done
  27.8 0.7 %merge.1 = (bf16[2,24,8,128]{3,2,1,0:T(8,128)(2,1)}, bf16[2,8,8,128]{3,2,1,0:T(8,128)(2,1)}) custom-call(bf16[32,8,128]{2,1,0:T(8,128)(2,1)S(1)} %get-tuple-element.33.made_ref, bf16[32,8,128]{2,1,0:T(8,128)(2,1)S(1)} %collective-permute-done.4.other_ref, bf16[2,24,8,128]{3,2,1,0:T(8,128)(2,1)S(1)} %copy-done), custom_call_target="tpu_custom_call" | custom-call | flops 1000000 | bytes 1000000 | tf_op jit(solution)/shard_map/merge/pallas_call | solution.py:662
Async XLA Ops:
  0.6 6.0 %collective-permute-start = (bf16[2,24,8,128]{3,2,1,0:T(8,128)(2,1)}, bf16[2,24,8,128]{3,2,1,0:T(8,128)(2,1)S(1)}, u32[]{:S(2)}, u32[]{:S(2)}) collective-permute-start(bf16[2,24,8,128]{3,2,1,0:T(8,128)(2,1)} %air_ref.3), channel_id=1, source_target_pairs={{0,2},{2,0},{1,3},{3,1},{4,6},{6,4},{5,7},{7,5},{8,10},{10,8},{9,1... | collective-permute-start | bytes 294920 | tf_op jit(solution)/shard_map/ppermute | solution.py:626
  6.8 7.3 %collective-permute-start.3 = (bf16[8,5376]{1,0:T(8,128)(2,1)S(1)}, bf16[8,5376]{1,0:T(8,128)(2,1)S(1)}, u32[]{:S(2)}, u32[]{:S(2)}) collective-permute-start(bf16[8,5376]{1,0:T(8,128)(2,1)S(1)} %pack_got.1.refs_0_), channel_id=1, source_target_pairs={{0,8},{4,12},{8,0},{12,4},{1,9},{5,13},{9,1},{13,5},{2,10},{6,14},... | collective-permute-start | bytes 258056 | tf_op jit(solution)/shard_map/ppermute | solution.py:657
  9.8 5.3 %collective-permute-start.2 = (bf16[8,5376]{1,0:T(8,128)(2,1)S(1)}, bf16[8,5376]{1,0:T(8,128)(2,1)S(1)}, u32[]{:S(2)}, u32[]{:S(2)}) collective-permute-start(bf16[8,5376]{1,0:T(8,128)(2,1)S(1)} %pack_got.1.refs_0_), channel_id=1, source_target_pairs={{0,12},{4,0},{8,4},{12,8},{1,13},{5,1},{9,5},{13,9},{2,14},{6,2},{... | collective-permute-start | bytes 258056 | tf_op jit(solution)/shard_map/ppermute | solution.py:657
  11.2 6.3 %collective-permute-start.1 = (bf16[8,5376]{1,0:T(8,128)(2,1)S(1)}, bf16[8,5376]{1,0:T(8,128)(2,1)S(1)}, u32[]{:S(2)}, u32[]{:S(2)}) collective-permute-start(bf16[8,5376]{1,0:T(8,128)(2,1)S(1)} %pack_got.1.refs_0_), channel_id=1, source_target_pairs={{0,4},{4,8},{8,12},{12,0},{1,5},{5,9},{9,13},{13,1},{2,6},{6,10},{... | collective-permute-start | bytes 258056 | tf_op jit(solution)/shard_map/ppermute | solution.py:657
  17.5 10.4 %copy-start = (bf16[2,24,8,128]{3,2,1,0:T(8,128)(2,1)S(1)}, bf16[2,24,8,128]{3,2,1,0:T(8,128)(2,1)}, u32[]{:S(2)}) copy-start(bf16[2,24,8,128]{3,2,1,0:T(8,128)(2,1)} %air_ref.3) | copy-start | bytes 294916
  23.5 4.3 %collective-permute-start.4 = (bf16[32,8,128]{2,1,0:T(8,128)(2,1)S(1)}, bf16[32,8,128]{2,1,0:T(8,128)(2,1)S(1)}, u32[]{:S(2)}, u32[]{:S(2)}) collective-permute-start(bf16[32,8,128]{2,1,0:T(8,128)(2,1)S(1)} %get-tuple-element.33.made_ref), channel_id=1, source_target_pairs={{0,2},{2,0},{1,3},{3,1},{4,6},{6,4},{5,7},{7,5},{8,10},{10,8},{9,1... | collective-permute-start | bytes 196616 | tf_op jit(solution)/shard_map/ppermute | solution.py:661

commit v10 on v8

--- a/solution.py
+++ b/solution.py
@@ -378,7 +378,7 @@
 
 
 CHUNK = 2
-LAG = 20
+LAG = 14
 LOAD = 0
 LATE_LOAD = -1
 HELD = 9

time: 28.7 us -> 28.7 us (level)
  no operation moved by 1% of the time
where the time goes in v10:
time: 28.7 us; the launch traced here: 28.5 us
  Pallas kernels  12.1 us (42%)
  starting transfers between devices  9.65 us (34%)
  waiting for transfers between devices  6.14 us (21%)
  between operations  0.66 us (2%)
    pallas_call x1, Pallas kernels, forecast(): pl.pallas_call(functools.partial(forecast_kernel, sizes, 1), out_shape=(p...  6.04 us
    ppermute x3, starting transfers between devices, belt_shards(): frame[index] = lax.ppermute(packed, 'sp', pairs)  5.01 us
    ppermute x1, starting transfers between devices, belt_shards(): got = lax.ppermute(atmosphere, 'sec', swap)  3.03 us
    ppermute x1, waiting for transfers between devices, belt_shards(): other = lax.ppermute(made, 'sec', swap)  2.72 us
    pallas_call x1, Pallas kernels, prepare_weights(): pl.pallas_call(weights_kernel, out_shape=(pltpu.VMEM((hidden, 9 * sea_ent...  2.01 us
    pallas_call x1, Pallas kernels, forecast(): pl.pallas_call(functools.partial(forecast_kernel, sizes, 0), out_shape=tu...  1.94 us
    ppermute x1, waiting for transfers between devices, belt_shards(): got = lax.ppermute(atmosphere, 'sec', swap)  1.79 us
    ppermute x3, waiting for transfers between devices, belt_shards(): frame[index] = lax.ppermute(packed, 'sp', pairs)  1.63 us
  transfers between devices with their start and end apart: 5, of which 5 were waited for; matrix products, arithmetic and copies ran while one was open for 0% of the time, Pallas kernels for 18%

profile of v10, /device:TPU:0, one launch (start us, length us, event | category | flops | bytes accessed | tf_op | source)
XLA Modules:
  0.0 28.5 jit_solution(14261541964450341036)
XLA Ops:
  0.6 3.0 %collective-permute-start = (bf16[2,24,8,128]{3,2,1,0:T(8,128)(2,1)}, bf16[2,24,8,128]{3,2,1,0:T(8,128)(2,1)S(1)}, u32[]{:S(2)}, u32[]{:S(2)}) collective-permute-start(bf16[2,24,8,128]{3,2,1,0:T(8,128)(2,1)} %air_ref.3), channel_id=1, source_target_pairs={{0,2},{2,0},{1,3},{3,1},{4,6},{6,4},{5,7},{7,5},{8,10},{10,8},{9,1... | collective-permute-start | bytes 294920 | tf_op jit(solution)/shard_map/ppermute | solution.py:604
  3.7 1.2 %pack_own.1.own_ref = bf16[8,5376]{1,0:T(8,128)(2,1)S(1)} custom-call(bf16[2,24,8,128]{3,2,1,0:T(8,128)(2,1)} %air_ref.3, bf16[2,8,8,128]{3,2,1,0:T(8,128)(2,1)} %sea_ref.1, bf16[2,8,8,128]{3,2,1,0:T(8,128)(2,1)} %flux_ref.1, s32[8,128]{1,0:T(8,128)} %mask_ref.1), custom_call_target="tpu_custom_call" | custom-call | flops 1000000 | bytes 1000000 | tf_op jit(solution)/shard_map/pack_own/pallas_call | solution.py:607
  4.9 1.8 %collective-permute-done.got_ref = bf16[2,24,8,128]{3,2,1,0:T(8,128)(2,1)S(1)} collective-permute-done((bf16[2,24,8,128]{3,2,1,0:T(8,128)(2,1)}, bf16[2,24,8,128]{3,2,1,0:T(8,128)(2,1)S(1)}, u32[]{:S(2)}, u32[]{:S(2)}) %collective-permute-start) | collective-permute-done | bytes 98336 | tf_op jit(solution)/shard_map/ppermute | solution.py:604
  6.7 0.2 pack_got.1.refs_0_
  6.8 3.0 %collective-permute-start.3 = (bf16[8,5376]{1,0:T(8,128)(2,1)S(1)}, bf16[8,5376]{1,0:T(8,128)(2,1)S(1)}, u32[]{:S(2)}, u32[]{:S(2)}) collective-permute-start(bf16[8,5376]{1,0:T(8,128)(2,1)S(1)} %pack_got.1.refs_0_), channel_id=1, source_target_pairs={{0,8},{4,12},{8,0},{12,4},{1,9},{5,13},{9,1},{13,5},{2,10},{6,14},... | collective-permute-start | bytes 258056 | tf_op jit(solution)/shard_map/ppermute | solution.py:635
  9.8 1.3 %collective-permute-start.2 = (bf16[8,5376]{1,0:T(8,128)(2,1)S(1)}, bf16[8,5376]{1,0:T(8,128)(2,1)S(1)}, u32[]{:S(2)}, u32[]{:S(2)}) collective-permute-start(bf16[8,5376]{1,0:T(8,128)(2,1)S(1)} %pack_got.1.refs_0_), channel_id=1, source_target_pairs={{0,12},{4,0},{8,4},{12,8},{1,13},{5,1},{9,5},{13,9},{2,14},{6,2},{... | collective-permute-start | bytes 258056 | tf_op jit(solution)/shard_map/ppermute | solution.py:635
  11.2 0.7 %collective-permute-start.1 = (bf16[8,5376]{1,0:T(8,128)(2,1)S(1)}, bf16[8,5376]{1,0:T(8,128)(2,1)S(1)}, u32[]{:S(2)}, u32[]{:S(2)}) collective-permute-start(bf16[8,5376]{1,0:T(8,128)(2,1)S(1)} %pack_got.1.refs_0_), channel_id=1, source_target_pairs={{0,4},{4,8},{8,12},{12,0},{1,5},{5,9},{9,13},{13,1},{2,6},{6,10},{... | collective-permute-start | bytes 258056 | tf_op jit(solution)/shard_map/ppermute | solution.py:635
  11.9 2.0 %weights.1 = (bf16[136,144]{1,0:T(8,128)(2,1)S(1)}, bf16[24,432]{1,0:T(8,128)(2,1)S(1)}, bf16[136,288]{1,0:T(8,128)(2,1)S(1)}, bf16[408,432]{1,0:T(8,128)(2,1)S(1)}, bf16[96,432]{1,0:T(8,128)(2,1)S(1)}) custom-call(bf16[3,3,16,136]{3,2,1,0:T(8,128)(2,1)} %se_ref.1, bf16[3,3,8,136]{3,2,1,0:T(8,128)(2,1)} %bitcast.3, bf16[3,3,32,136]{3,2,1,0:T(8,128)(2,1)} %ae_ref.1, ...), custom_call_target="tpu_custom_call" | custom-call | flops 1000000 | bytes 4000000 | tf_op jit(solution)/shard_map/weights/pallas_call | solution.py:327
  13.9 0.3 %collective-permute-done.3.refs_2_ = bf16[8,5376]{1,0:T(8,128)(2,1)S(1)} collective-permute-done((bf16[8,5376]{1,0:T(8,128)(2,1)S(1)}, bf16[8,5376]{1,0:T(8,128)(2,1)S(1)}, u32[]{:S(2)}, u32[]{:S(2)}) %collective-permute-start.3) | collective-permute-done | bytes 86048 | tf_op jit(solution)/shard_map/ppermute | solution.py:635
  14.2 0.9 %collective-permute-done.2.refs_1_ = bf16[8,5376]{1,0:T(8,128)(2,1)S(1)} collective-permute-done((bf16[8,5376]{1,0:T(8,128)(2,1)S(1)}, bf16[8,5376]{1,0:T(8,128)(2,1)S(1)}, u32[]{:S(2)}, u32[]{:S(2)}) %collective-permute-start.2) | collective-permute-done | bytes 86048 | tf_op jit(solution)/shard_map/ppermute | solution.py:635
  15.1 1.9 %forecast_early.1 = (bf16[48,4608]{1,0:T(8,128)(2,1)S(1)}, bf16[144,4608]{1,0:T(8,128)(2,1)S(1)}, bf16[96,4608]{1,0:T(8,128)(2,1)S(1)}, bf16[144,4608]{1,0:T(8,1...) custom-call(bf16[8,5376]{1,0:T(8,128)(2,1)S(1)} %pack_got.1.refs_0_,, ...), custom_call_target="tpu_custom_call" | custom-call | flops 1000 | bytes 1000 | tf_op jit(solution)/shard_map/forecast_early/pallas_call | solution.py:571
  17.1 0.4 %collective-permute-done.1.refs_0_ = bf16[8,5376]{1,0:T(8,128)(2,1)S(1)} collective-permute-done((bf16[8,5376]{1,0:T(8,128)(2,1)S(1)}, bf16[8,5376]{1,0:T(8,128)(2,1)S(1)}, u32[]{:S(2)}, u32[]{:S(2)}) %collective-permute-start.1) | collective-permute-done | bytes 86048 | tf_op jit(solution)/shard_map/ppermute | solution.py:635
  17.5 0.0 copy-start
  17.5 6.0 %forecast_late.1 = (bf16[32,8,128]{2,1,0:T(8,128)(2,1)S(1)}, bf16[48,4608]{1,0:T(8,128)(2,1)S(1)}, bf16[144,4608]{1,0:T(8,128)(2,1)S(1)}, bf16[96,4608]{1,0:T(8,...) custom-call(bf16[8,5376]{1,0:T(8,128)(2,1)S(1)} %collective-permute-, ...), custom_call_target="tpu_custom_call", output_to_operand_aliasing={{1}: (6, {}), {2}: (7, {}), {3}: (8, {}), {4}: (9, {}), {5}... | custom-call | flops 2000000000 | bytes 3000000 | tf_op jit(solution)/shard_map/forecast_late/pallas_call | solution.py:580
  23.5 1.6 %collective-permute-start.4 = (bf16[32,8,128]{2,1,0:T(8,128)(2,1)S(1)}, bf16[32,8,128]{2,1,0:T(8,128)(2,1)S(1)}, u32[]{:S(2)}, u32[]{:S(2)}) collective-permute-start(bf16[32,8,128]{2,1,0:T(8,128)(2,1)S(1)} %get-tuple-element.31.made_ref), channel_id=1, source_target_pairs={{0,2},{2,0},{1,3},{3,1},{4,6},{6,4},{5,7},{7,5},{8,10},{10,8},{9,1... | collective-permute-start | bytes 196616 | tf_op jit(solution)/shard_map/ppermute | solution.py:639
  25.1 2.7 %collective-permute-done.4.other_ref = bf16[32,8,128]{2,1,0:T(8,128)(2,1)S(1)} collective-permute-done((bf16[32,8,128]{2,1,0:T(8,128)(2,1)S(1)}, bf16[32,8,128]{2,1,0:T(8,128)(2,1)S(1)}, u32[]{:S(2)}, u32[]{:S(2)}) %collective-permute-start.4) | collective-permute-done | bytes 65568 | tf_op jit(solution)/shard_map/ppermute | solution.py:639
  27.8 0.0 copy-done
  27.8 0.7 %merge.1 = (bf16[2,24,8,128]{3,2,1,0:T(8,128)(2,1)}, bf16[2,8,8,128]{3,2,1,0:T(8,128)(2,1)}) custom-call(bf16[32,8,128]{2,1,0:T(8,128)(2,1)S(1)} %get-tuple-element.31.made_ref, bf16[32,8,128]{2,1,0:T(8,128)(2,1)S(1)} %collective-permute-done.4.other_ref, bf16[2,24,8,128]{3,2,1,0:T(8,128)(2,1)S(1)} %copy-done), custom_call_target="tpu_custom_call" | custom-call | flops 1000000 | bytes 1000000 | tf_op jit(solution)/shard_map/merge/pallas_call | solution.py:640
Async XLA Ops:
  0.6 6.0 %collective-permute-start = (bf16[2,24,8,128]{3,2,1,0:T(8,128)(2,1)}, bf16[2,24,8,128]{3,2,1,0:T(8,128)(2,1)S(1)}, u32[]{:S(2)}, u32[]{:S(2)}) collective-permute-start(bf16[2,24,8,128]{3,2,1,0:T(8,128)(2,1)} %air_ref.3), channel_id=1, source_target_pairs={{0,2},{2,0},{1,3},{3,1},{4,6},{6,4},{5,7},{7,5},{8,10},{10,8},{9,1... | collective-permute-start | bytes 294920 | tf_op jit(solution)/shard_map/ppermute | solution.py:604
  6.8 7.3 %collective-permute-start.3 = (bf16[8,5376]{1,0:T(8,128)(2,1)S(1)}, bf16[8,5376]{1,0:T(8,128)(2,1)S(1)}, u32[]{:S(2)}, u32[]{:S(2)}) collective-permute-start(bf16[8,5376]{1,0:T(8,128)(2,1)S(1)} %pack_got.1.refs_0_), channel_id=1, source_target_pairs={{0,8},{4,12},{8,0},{12,4},{1,9},{5,13},{9,1},{13,5},{2,10},{6,14},... | collective-permute-start | bytes 258056 | tf_op jit(solution)/shard_map/ppermute | solution.py:635
  9.8 5.3 %collective-permute-start.2 = (bf16[8,5376]{1,0:T(8,128)(2,1)S(1)}, bf16[8,5376]{1,0:T(8,128)(2,1)S(1)}, u32[]{:S(2)}, u32[]{:S(2)}) collective-permute-start(bf16[8,5376]{1,0:T(8,128)(2,1)S(1)} %pack_got.1.refs_0_), channel_id=1, source_target_pairs={{0,12},{4,0},{8,4},{12,8},{1,13},{5,1},{9,5},{13,9},{2,14},{6,2},{... | collective-permute-start | bytes 258056 | tf_op jit(solution)/shard_map/ppermute | solution.py:635
  11.2 6.3 %collective-permute-start.1 = (bf16[8,5376]{1,0:T(8,128)(2,1)S(1)}, bf16[8,5376]{1,0:T(8,128)(2,1)S(1)}, u32[]{:S(2)}, u32[]{:S(2)}) collective-permute-start(bf16[8,5376]{1,0:T(8,128)(2,1)S(1)} %pack_got.1.refs_0_), channel_id=1, source_target_pairs={{0,4},{4,8},{8,12},{12,0},{1,5},{5,9},{9,13},{13,1},{2,6},{6,10},{... | collective-permute-start | bytes 258056 | tf_op jit(solution)/shard_map/ppermute | solution.py:635
  17.5 10.4 %copy-start = (bf16[2,24,8,128]{3,2,1,0:T(8,128)(2,1)S(1)}, bf16[2,24,8,128]{3,2,1,0:T(8,128)(2,1)}, u32[]{:S(2)}) copy-start(bf16[2,24,8,128]{3,2,1,0:T(8,128)(2,1)} %air_ref.3) | copy-start | bytes 294916
  23.5 4.3 %collective-permute-start.4 = (bf16[32,8,128]{2,1,0:T(8,128)(2,1)S(1)}, bf16[32,8,128]{2,1,0:T(8,128)(2,1)S(1)}, u32[]{:S(2)}, u32[]{:S(2)}) collective-permute-start(bf16[32,8,128]{2,1,0:T(8,128)(2,1)S(1)} %get-tuple-element.31.made_ref), channel_id=1, source_target_pairs={{0,2},{2,0},{1,3},{3,1},{4,6},{6,4},{5,7},{7,5},{8,10},{10,8},{9,1... | collective-permute-start | bytes 196616 | tf_op jit(solution)/shard_map/ppermute | solution.py:639
